TPU v7x, 512 devices: a whole 4x4x16 slice. The times are simulated.
512 devices in a mesh: expert: 128 (over y, z, core), dp: 4 (over x).
Axes of the slice: x: 4, y: 4, z: 16, core: 2. Of those that a mesh axis runs over, the one named last changes fastest.
Arguments:
- inputs: bfloat16 [16384, 2048], P('expert', 'dp'), may hold values from -6 to 6
- out_grad: bfloat16 [16384, 2048], P('expert', 'dp'), may hold values from -3 to 3
- gate_weights: float32 [16384, 4], P('expert'), may hold values from 0.05 to 0.6
- routes: int32 [16384, 4], P('expert'), may hold values from 0 to 127, all different within a row; in each aligned block of 128 rows (0 to 127, 128 to 255, ...) at most 8 rows name the same one
- up_weight: bfloat16 [128, 768, 2048], P('expert', 'dp'), may hold values from -0.125 to 0.125
- down_weight: bfloat16 [128, 768, 2048], P('expert', 'dp'), may hold values from -0.21875 to 0.21875
Outputs:
- in_grad: bfloat16 [16384, 2048], P('expert', 'dp')
- grad_up: bfloat16 [128, 768, 2048], P('expert', 'dp')
- grad_down: bfloat16 [128, 768, 2048], P('expert', 'dp')
Inputs may be any that keep to these rules, and one draw needn't show every extreme that they name: A token's 4 experts differ. Among the routes of the tokens b * 128 to (b + 1) * 128 - 1, no expert is named more than 8 times, a bound that some expert reaches in some of these blocks.
All inputs are finite; a program needn't handle non-finite values.
Results may differ from a plain program's by a relative error of at most 0.015.
Values may be sent and summed in bfloat16 or wider, within the bound.
No kernel may reach another device: no remote copies, remote signals or barrier semaphores. Data moves between devices by JAX's collectives and lax.ppermute only.
A program may use at most 64 MiB of HBM per device.

v0:
```python
import jax
import jax.numpy as jnp
from jax import lax
from jax.sharding import PartitionSpec as P


def slot_targets(routes, expert_count, capacity):
    flat_routes = routes.reshape(-1)
    onehot = (flat_routes[:, None] == jnp.arange(expert_count, dtype=jnp.int32)[None, :]).astype(
        jnp.int32
    )
    earlier = jnp.cumsum(onehot, axis=0) - onehot
    ranks = jnp.sum(earlier * onehot, axis=1)
    return flat_routes * capacity + ranks


def local(inputs, out_grad, gate_weights, routes, up_weight, down_weight):
    expert_count = lax.axis_size("expert")
    token_count, route_count = routes.shape
    capacity = max(2, token_count * route_count * 2 // expert_count)
    row_total = expert_count * capacity
    targets = slot_targets(routes, expert_count, capacity)
    full_in, full_out = (
        lax.all_gather(inputs, "dp", axis=1, tiled=True),
        lax.all_gather(out_grad, "dp", axis=1, tiled=True),
    )
    width = full_in.shape[1]
    scaled = (gate_weights[:, :, None] * full_out[:, None, :].astype(jnp.float32)).astype(
        jnp.bfloat16
    )
    scaled = scaled.reshape(token_count * route_count, width)
    repeated = jnp.broadcast_to(full_in[:, None, :], (token_count, route_count, width)).reshape(
        token_count * route_count, width
    )
    in_buffer = jnp.zeros((row_total, width), jnp.bfloat16).at[targets].set(repeated)
    grad_buffer = jnp.zeros((row_total, width), jnp.bfloat16).at[targets].set(scaled)
    send_in = in_buffer.reshape(expert_count, capacity, width)
    send_grad = grad_buffer.reshape(expert_count, capacity, width)
    in_rows, grad_rows = (
        lax.all_to_all(send_in, "expert", split_axis=0, concat_axis=0, tiled=True),
        lax.all_to_all(send_grad, "expert", split_axis=0, concat_axis=0, tiled=True),
    )
    in_rows = in_rows.reshape(row_total, -1)
    grad_rows = grad_rows.reshape(row_total, -1)
    up_local = up_weight[0]
    down_local = down_weight[0]
    contract_last = (((1,), (1,)), ((), ()))
    pre = lax.dot_general(in_rows, up_local, contract_last, preferred_element_type=jnp.float32)
    sigma = jax.nn.sigmoid(pre)
    hidden = (pre * sigma).astype(jnp.bfloat16)
    back = lax.dot_general(grad_rows, down_local, contract_last, preferred_element_type=jnp.float32)
    d_pre = (back * sigma * (1.0 + pre * (1.0 - sigma))).astype(jnp.bfloat16)
    grad_up = jnp.dot(d_pre.T, in_rows, preferred_element_type=jnp.float32).astype(jnp.bfloat16)[
        None
    ]
    grad_down = jnp.dot(hidden.T, grad_rows, preferred_element_type=jnp.float32).astype(
        jnp.bfloat16
    )[None]
    partial_rows = jnp.dot(d_pre, up_local, preferred_element_type=jnp.float32).astype(jnp.bfloat16)
    returned = lax.all_to_all(
        partial_rows.reshape(expert_count, capacity, -1),
        "expert",
        split_axis=0,
        concat_axis=0,
        tiled=True,
    )
    picked = returned.reshape(row_total, -1)[targets].astype(jnp.float32)
    token_sums = jnp.sum(picked.reshape(token_count, route_count, -1), axis=1)
    in_grad = lax.psum_scatter(
        token_sums.astype(jnp.bfloat16), "dp", scatter_dimension=1, tiled=True
    )
    return (in_grad, grad_up, grad_down)


def solution(mesh):
    return jax.shard_map(
        local,
        mesh=mesh,
        in_specs=(
            P("expert", "dp"),
            P("expert", "dp"),
            P("expert", None),
            P("expert", None),
            P("expert", "dp", None),
            P("expert", "dp", None),
        ),
        out_specs=(P("expert", "dp"), P("expert", "dp", None), P("expert", "dp", None)),
        check_vma=False,
    )
```

profile of v0, /device:TPU:1, one launch (start us, length us, event | category | flops | bytes accessed | tf_op | source)
XLA Modules:
  0.0 688.8 jit_solution(3234940106353235567)
XLA Ops:
  7.2 0.0 copy-start
  7.2 0.8 broadcast_multiply_fusion
  7.9 0.8 copy.10
  8.7 0.1 eq.29
  8.8 0.1 eq.25
  8.9 0.1 copy.9
  9.1 0.1 mul.51
  9.2 0.1 copy.12
  9.3 0.2 fusion.40
  9.6 11.3 %all_gather.7 = bf16[128,2048]{1,0:T(8,128)(2,1)S(1)} all-gather(bf16[128,512]{1,0:T(8,128)(2,1)} %param.6), channel_id=1, replica_groups=mesh['expert'=128,'dp'=4] {'dp'}, dimensions={1}, use_global_device_ids=true | all-gather | bytes 655360 | tf_op jit(solution)/shard_map/all_gather | solution.py:24
  20.9 1.0 broadcast_in_dim.6
  21.9 2.1 reshape.111
  24.0 0.2 fusion.39
  24.3 7.3 %scatter_custom_fusion.1 = bf16[1024,2048]{1,0:T(8,128)(2,1)} fusion(s32[512]{0:T(512)S(1)} %bitcast.66, bf16[512,2048]{1,0:T(8,128)(2,1)} %reshape.111, bf16[]{:T(256)} %constant.5.clone.1), kind=kCustom, calls=%fused_computation.19 | custom fusion | bytes 4194816 | tf_op jit(solution)/shard_map/scatter | solution.py:35
  31.5 0.0 copy-start.2
  31.5 0.0 copy-start.1
  31.5 23.2 %all-to-all-start.1 = ((bf16[128,8,2048]{2,1,0:T(8,128)(2,1)}), bf16[128,8,2048]{2,1,0:T(8,128)(2,1)}, u32[]{:S(2)}, u32[]{:S(2)}) async-start(bf16[128,8,2048]{2,1,0:T(8,128)(2,1)} %bitcast.61), calls=%async_computation.1 | async-start | bytes 8388608 | tf_op jit(solution)/shard_map/all_to_all | solution.py:40
  54.7 0.0 copy-done.2
  54.8 0.1 copy.14
  54.9 0.1 mul.53
  55.0 0.0 copy-done.1
  55.0 12.1 %all_gather.6 = bf16[128,2048]{1,0:T(8,128)(2,1)S(1)} all-gather(bf16[128,512]{1,0:T(8,128)(2,1)S(1)} %copy-done.1), channel_id=1, replica_groups=mesh['expert'=128,'dp'=4] {'dp'}, dimensions={1}, use_global_device_ids=true | all-gather | bytes 655360 | tf_op jit(solution)/shard_map/all_gather | solution.py:25
  67.1 3.0 mul.55
  70.1 5.3 mul.56
  75.4 7.9 %scatter_custom_fusion = bf16[1024,2048]{1,0:T(8,128)(2,1)} fusion(s32[512]{0:T(512)S(1)} %bitcast.67, f32[512,2048]{1,0:T(8,128)} %mul.56, f32[512]{0:T(512)S(1)} %mul.53, bf16[]{:T(256)} %constant.5.clone.1), kind=kCustom, calls=%fused_computation.17 | custom fusion | flops 2097152 | bytes 8390658 | tf_op jit(solution)/shard_map/scatter | solution.py:36
  83.3 156.7 %all-to-all-done.1 = bf16[128,8,2048]{2,1,0:T(8,128)(2,1)} async-done(((bf16[128,8,2048]{2,1,0:T(8,128)(2,1)}), bf16[128,8,2048]{2,1,0:T(8,128)(2,1)}, u32[]{:S(2)}, u32[]{:S(2)}) %all-to-all-start.1) | async-done | bytes 4194336 | tf_op jit(solution)/shard_map/all_to_all | solution.py:40
  240.0 12.6 %all-to-all-start = ((bf16[128,8,2048]{2,1,0:T(8,128)(2,1)}), bf16[128,8,2048]{2,1,0:T(8,128)(2,1)}, u32[]{:S(2)}, u32[]{:S(2)}) async-start(bf16[128,8,2048]{2,1,0:T(8,128)(2,1)} %bitcast.60), calls=%async_computation | async-start | bytes 8388608 | tf_op jit(solution)/shard_map/all_to_all | solution.py:41
  252.6 0.0 copy-done
  252.6 0.0 copy-start.3
  252.6 3.8 fusion.2
  256.4 0.0 copy-start.4
  256.4 181.4 %all-to-all-done = bf16[128,8,2048]{2,1,0:T(8,128)(2,1)} async-done(((bf16[128,8,2048]{2,1,0:T(8,128)(2,1)}), bf16[128,8,2048]{2,1,0:T(8,128)(2,1)}, u32[]{:S(2)}, u32[]{:S(2)}) %all-to-all-start) | async-done | bytes 4194336 | tf_op jit(solution)/shard_map/all_to_all | solution.py:41
  437.9 0.0 copy-done.3
  437.9 3.8 fusion.31
  441.7 0.0 copy-done.4
  441.7 3.3 convert_bitcast_fusion
  445.0 12.8 %all-to-all-start.2 = ((bf16[128,8,2048]{2,1,0:T(8,128)(2,1)}), bf16[128,8,2048]{2,1,0:T(8,128)(2,1)}, u32[]{:S(2)}, u32[]{:S(2)}) async-start(bf16[128,8,2048]{2,1,0:T(8,128)(2,1)} %convert_bitcast_fusion), calls=%async_computation.2 | async-start | bytes 8388608 | tf_op jit(solution)/shard_map/all_to_all | solution.py:60
  457.8 0.0 reduce-scatter.2.cloned.1.call-start
  457.8 185.2 %all-to-all-done.2 = bf16[128,8,2048]{2,1,0:T(8,128)(2,1)} async-done(((bf16[128,8,2048]{2,1,0:T(8,128)(2,1)}), bf16[128,8,2048]{2,1,0:T(8,128)(2,1)}, u32[]{:S(2)}, u32[]{:S(2)}) %all-to-all-start.2) | async-done | bytes 4194336 | tf_op jit(solution)/shard_map/all_to_all | solution.py:60
  643.0 7.1 %gather_fusion = bf16[512,2048]{1,0:T(8,128)(2,1)S(1)} fusion(bf16[1024,2048]{1,0:T(8,128)(2,1)} %bitcast.12, s32[1024]{0:T(1024)S(1)} %pad_clamp_fusion), kind=kCustom, calls=%fused_computation | custom fusion | bytes 4196352 | tf_op jit(solution)/shard_map/gather | solution.py:67
  650.2 2.3 gather.6
  652.5 0.0 copy-start.5
  652.5 5.1 reduce_sum.25
  657.5 0.0 reduce-scatter.2.cloned.1.call-update
  657.5 4.1 fusion.14
  661.6 0.0 copy-done.5
  661.6 4.1 fusion.17
  665.7 16.3 %reduce-scatter.2.cloned.1.call-done = bf16[128,512]{1,0:T(8,128)(2,1)} async-done(((bf16[128,2048]{1,0:T(8,128)(2,1)}), bf16[128,512]{1,0:T(8,128)(2,1)}) %reduce-scatter.2.cloned.1.call-update) | async-done | bytes 131088 | tf_op jit(solution)/shard_map/reduce_scatter | solution.py:69
  (8 shorter events, 0.1 us)
Async XLA Ops:
  7.2 245.4 %copy-start = (bf16[1,192,2048]{2,1,0:T(8,128)(2,1)S(1)}, bf16[1,192,2048]{2,1,0:T(8,128)(2,1)}, u32[]{:S(2)}) copy-start(bf16[1,192,2048]{2,1,0:T(8,128)(2,1)} %param.10) | copy-start | bytes 2359300
  31.5 23.2 %copy-start.2 = (f32[128,4]{0,1:T(4,128)S(1)}, f32[128,4]{0,1:T(4,128)}, u32[]{:S(2)}) copy-start(f32[128,4]{0,1:T(4,128)} %param.8) | copy-start | bytes 6148
  31.5 23.5 %copy-start.1 = (bf16[128,512]{1,0:T(8,128)(2,1)S(1)}, bf16[128,512]{1,0:T(8,128)(2,1)}, u32[]{:S(2)}) copy-start(bf16[128,512]{1,0:T(8,128)(2,1)} %param.7) | copy-start | bytes 393220
  31.5 208.5 %all-to-all-start.1 = ((bf16[128,8,2048]{2,1,0:T(8,128)(2,1)}), bf16[128,8,2048]{2,1,0:T(8,128)(2,1)}, u32[]{:S(2)}, u32[]{:S(2)}) async-start(bf16[128,8,2048]{2,1,0:T(8,128)(2,1)} %bitcast.61), calls=%async_computation.1 | async-start | bytes 8388608 | tf_op jit(solution)/shard_map/all_to_all | solution.py:40
  240.0 197.9 %all-to-all-start = ((bf16[128,8,2048]{2,1,0:T(8,128)(2,1)}), bf16[128,8,2048]{2,1,0:T(8,128)(2,1)}, u32[]{:S(2)}, u32[]{:S(2)}) async-start(bf16[128,8,2048]{2,1,0:T(8,128)(2,1)} %bitcast.60), calls=%async_computation | async-start | bytes 8388608 | tf_op jit(solution)/shard_map/all_to_all | solution.py:41
  252.6 185.3 %copy-start.3 = (bf16[1,192,2048]{2,1,0:T(8,128)(2,1)S(1)}, bf16[1,192,2048]{2,1,0:T(8,128)(2,1)}, u32[]{:S(2)}) copy-start(bf16[1,192,2048]{2,1,0:T(8,128)(2,1)} %param.11) | copy-start | bytes 2359300
  256.4 185.3 %copy-start.4 = (f32[1024,192]{0,1:T(8,128)}, f32[1024,192]{0,1:T(8,128)S(1)}, u32[]{:S(2)}) copy-start(f32[1024,192]{0,1:T(8,128)S(1)} %fusion.2) | copy-start | bytes 2359300
  445.0 198.1 %all-to-all-start.2 = ((bf16[128,8,2048]{2,1,0:T(8,128)(2,1)}), bf16[128,8,2048]{2,1,0:T(8,128)(2,1)}, u32[]{:S(2)}, u32[]{:S(2)}) async-start(bf16[128,8,2048]{2,1,0:T(8,128)(2,1)} %convert_bitcast_fusion), calls=%async_computation.2 | async-start | bytes 8388608 | tf_op jit(solution)/shard_map/all_to_all | solution.py:60
  457.8 224.2 %reduce-scatter.2.cloned.1.call-start = ((), (), s32[]{:S(2)}) async-start(), calls=%async_computation.4 | async-start | bytes 655360 | tf_op jit(solution)/shard_map/reduce_scatter | solution.py:69
  652.5 9.2 %copy-start.5 = (f32[1024,192]{0,1:T(8,128)S(1)}, f32[1024,192]{0,1:T(8,128)}, u32[]{:S(2)}) copy-start(f32[1024,192]{0,1:T(8,128)} %copy-done.4) | copy-start | bytes 2359300
Sparse Core Ops, SparseCore 0:
  657.7 24.2 reduce-scatter.1
where the time goes:
time: 690 us; the launch traced here: 689 us
  waiting for transfers between devices  540 us (78%)
  starting transfers between devices  48.6 us (7%)
  local copies, waits for them, and re-layouts  29.7 us (4%)
  blocking collectives  23.4 us (3%)
  matrix products  19 us (3%)
  other arithmetic  14.2 us (2%)
  between operations  14.2 us (2%)
    all_to_all x1, waiting for transfers between devices, local(): lax.all_to_all(partial_rows.reshape(expert_count, capacity, -1), 'expert'...  185 us
    all_to_all x1, waiting for transfers between devices, local(): lax.all_to_all(send_grad, 'expert', split_axis=0, concat_axis=0, tiled=True)  181 us
    all_to_all x1, waiting for transfers between devices, local(): lax.all_to_all(send_in, 'expert', split_axis=0, concat_axis=0, tiled=True)  157 us
    all_to_all x1, starting transfers between devices, local(): lax.all_to_all(send_in, 'expert', split_axis=0, concat_axis=0, tiled=True)  23.2 us
    reduce_scatter x1, waiting for transfers between devices, local(): lax.psum_scatter(token_sums.astype(jnp.bfloat16), 'dp', scatter_dimension...  16.3 us
  transfers between devices with their start and end apart: 4, of which 4 were waited for; matrix products, arithmetic and copies ran while one was open for 4% of the time, Pallas kernels for 0%

commit v1 on v0

v1 whole, which is shorter than its diff:
```python
import jax
import jax.numpy as jnp
from jax import lax
from jax.sharding import PartitionSpec as P

F32 = jnp.float32
BF16 = jnp.bfloat16
CONTRACT_LAST = (((1,), (1,)), ((), ()))
CONTRACT_FIRST = (((0,), (0,)), ((), ()))


def route_masks(routes, gate_weights, expert_count, capacity):
    token_count = routes.shape[0]
    experts = lax.broadcasted_iota(jnp.int32, (expert_count, token_count), 0)
    match = jnp.zeros((expert_count, token_count), jnp.bool_)
    gates = jnp.zeros((expert_count, token_count), F32)
    for k in range(routes.shape[1]):
        hit = routes[:, k][None, :] == experts
        match = match | hit
        gates = gates + jnp.where(hit, gate_weights[:, k][None, :], 0.0)
    before = lax.broadcasted_iota(jnp.int32, (token_count, token_count), 0)
    after = lax.broadcasted_iota(jnp.int32, (token_count, token_count), 1)
    ranks = jnp.dot(
        match.astype(BF16), (before < after).astype(BF16), preferred_element_type=F32
    ).astype(jnp.int32)
    slots = jnp.arange(capacity, dtype=jnp.int32)
    chosen = match[:, None, :] & (ranks[:, None, :] == slots[None, :, None])
    slot_gates = jnp.sum(jnp.where(chosen, gates[:, None, :], 0.0), axis=2)
    chosen = chosen.reshape(expert_count * capacity, token_count).astype(BF16)
    return chosen, slot_gates.reshape(expert_count * capacity, 1)


def local(inputs, out_grad, gate_weights, routes, up_weight, down_weight):
    expert_count = lax.axis_size("expert")
    dp_count = lax.axis_size("dp")
    token_count, route_count = routes.shape
    capacity = max(2, token_count * route_count * 2 // expert_count)
    per_dev = capacity // dp_count
    rows = expert_count * per_dev
    part = inputs.shape[1]
    width = part * dp_count
    peers = expert_count * dp_count

    up_full = lax.all_gather(up_weight[0], "dp", axis=0, tiled=True)
    down_full = lax.all_gather(down_weight[0], "dp", axis=0, tiled=True)

    chosen, slot_gates = route_masks(routes, gate_weights, expert_count, capacity)

    def swap(values):
        return lax.all_to_all(values, ("expert", "dp"), split_axis=0, concat_axis=0, tiled=True)

    send_in = jnp.dot(chosen, inputs, preferred_element_type=F32).astype(BF16)
    scaled = slot_gates * jnp.dot(chosen, out_grad, preferred_element_type=F32)
    send_grad = scaled.astype(BF16)
    both = jnp.concatenate(
        [send_in.reshape(peers, per_dev, part), send_grad.reshape(peers, per_dev, part)], axis=1
    )
    both = swap(both).reshape(expert_count, dp_count, 2, per_dev, part)
    both = both.transpose(2, 0, 3, 1, 4).reshape(2, rows, width)
    in_rows, grad_rows = both[0], both[1]

    pre = lax.dot_general(in_rows, up_full, CONTRACT_LAST, preferred_element_type=F32)
    sigma = jax.nn.sigmoid(pre)
    hidden = (pre * sigma).astype(BF16)
    back = lax.dot_general(grad_rows, down_full, CONTRACT_LAST, preferred_element_type=F32)
    d_pre = (back * sigma * (1.0 + pre * (1.0 - sigma))).astype(BF16)

    back_rows = jnp.dot(d_pre, up_full, preferred_element_type=F32).astype(BF16)
    back_rows = back_rows.reshape(expert_count, per_dev, dp_count, part).transpose(0, 2, 1, 3)
    returned = swap(back_rows.reshape(peers, per_dev, part))
    returned = returned.reshape(peers * per_dev, part)

    def weight_grad(left, right):
        total = lax.dot_general(left, right, CONTRACT_FIRST, preferred_element_type=F32)
        return total.astype(BF16).reshape(dp_count, 1, -1, width)

    grads = jnp.concatenate([weight_grad(d_pre, in_rows), weight_grad(hidden, grad_rows)], axis=1)
    grads = lax.psum_scatter(grads, "dp", scatter_dimension=0, tiled=False)

    in_grad = lax.dot_general(chosen, returned, CONTRACT_FIRST, preferred_element_type=F32)
    return (in_grad.astype(BF16), grads[0][None], grads[1][None])


def solution(mesh):
    return jax.shard_map(
        local,
        mesh=mesh,
        in_specs=(
            P("expert", "dp"),
            P("expert", "dp"),
            P("expert", None),
            P("expert", None),
            P("expert", "dp", None),
            P("expert", "dp", None),
        ),
        out_specs=(P("expert", "dp"), P("expert", "dp", None), P("expert", "dp", None)),
        check_vma=False,
    )
```

time: 690 us -> 245 us (0.36)
  waiting for transfers between devices: 540 us -> 104 us
  blocking collectives: 23.4 us -> 66.5 us
  starting transfers between devices: 48.6 us -> 24.6 us
  local copies, waits for them, and re-layouts: 29.7 us -> 14.9 us
  other arithmetic: 14.2 us -> 6.67 us
    all_to_all x3 -> x1, waiting for transfers between devices: 523 us -> 102 us  [swap(): lax.all_to_all(values, ('expert', 'dp'), split_axis=0, concat_axis=0, til...]
    all_to_all x0 -> x1, blocking collectives: none -> 66.5 us  [swap(): lax.all_to_all(values, ('expert', 'dp'), split_axis=0, concat_axis=0, til...]
    all_to_all x3 -> x1, starting transfers between devices: 48.6 us -> 24.3 us  [swap(): lax.all_to_all(values, ('expert', 'dp'), split_axis=0, concat_axis=0, til...]
    all_gather x2 -> x0, blocking collectives: 23.4 us -> none  [the longest x1 12.1 us: local(): lax.all_gather(out_grad, 'dp', axis=1, tiled=True)]
    reduce_scatter x1, waiting for transfers between devices: 16.3 us -> 0.01 us  [local(): grads = lax.psum_scatter(grads, 'dp', scatter_dimension=0, tiled=False)]
    gather x2 -> x0, local copies, waits for them, and re-layouts: 9.4 us -> none  [local(): picked = returned.reshape(row_total, -1)[targets].astype(jnp.float32)]
    mul x5 -> x1, local copies, waits for them, and re-layouts: 8.67 us -> 0.09 us  [local(): scaled = slot_gates * jnp.dot(chosen, out_grad, preferred_element_type=F32)]
    scatter x1 -> x0, other arithmetic: 7.92 us -> none  [local(): jnp.zeros((row_total, width), jnp.bfloat16).at[targets].set(scaled)]
  transfers between devices with their start and end apart: 4 -> 4, of which waited for: 4 -> 1; matrix products, arithmetic and copies ran while one was open for 4% -> 10% of each run, Pallas kernels for 0% -> 0%
where the time goes in v1:
time: 245 us
  waiting for transfers between devices  104 us (42%)
  blocking collectives  66.5 us (27%)
  starting transfers between devices  24.6 us (10%)
  local copies, waits for them, and re-layouts  14.9 us (6%)
  matrix products  14.6 us (6%)
  between operations  14 us (6%)
  other arithmetic  6.67 us (3%)
    all_to_all x1, waiting for transfers between devices, swap(): lax.all_to_all(values, ('expert', 'dp'), split_axis=0, concat_axis=0, til...  102 us
    all_to_all x1, blocking collectives, swap(): lax.all_to_all(values, ('expert', 'dp'), split_axis=0, concat_axis=0, til...  66.5 us
    all_to_all x1, starting transfers between devices, swap(): lax.all_to_all(values, ('expert', 'dp'), split_axis=0, concat_axis=0, til...  24.3 us
  transfers between devices with their start and end apart: 4, of which 1 were waited for; matrix products, arithmetic and copies ran while one was open for 10% of the time, Pallas kernels for 0%

profile of v1, /device:TPU:1, one launch (start us, length us, event | category | flops | bytes accessed | tf_op | source)
XLA Modules:
  0.0 245.0 jit_solution(12638796201508769802)
XLA Ops:
  7.2 0.0 copy-start
  7.2 0.0 copy-start.2
  7.2 0.0 all-gather.7.cloned.1.call-start
  7.2 0.7 all-gather.7.cloned.1.call-update
  7.9 0.8 slice_bitcast_fusion.9
  8.8 0.2 convolution_convert_fusion.4
  9.0 0.8 slice_bitcast_fusion.5
  9.8 0.2 select_reduce_fusion
  10.0 0.1 mul.22
  10.2 0.1 eq.116
  10.2 0.0 copy-done
  10.3 0.5 multiply_convert_fusion
  10.8 0.4 reshape.264
  11.2 0.0 copy-done.2
  11.2 0.5 convolution_convert_fusion.2
  11.7 0.4 reshape.263
  12.2 3.2 %pad_maximum_fusion.1 = bf16[512,4,512]{2,1,0:T(4,128)(2,1)} fusion(bf16[512,2,512]{2,1,0:T(2,128)(2,1)S(1)} %reshape.264, bf16[512,2,512]{2,1,0:T(2,128)(2,1)S(1)} %reshape.263), kind=kLoop, calls=%fused_computation.10 | loop fusion | flops 4194304 | bytes 4194304 | tf_op jit(solution)/shard_map/concatenate | solution.py:55
  15.3 24.3 %all-to-all-start = ((bf16[512,4,512]{2,1,0:T(4,128)(2,1)}), bf16[512,4,512]{2,1,0:T(4,128)(2,1)S(1)}, u32[]{:S(2)}, u32[]{:S(2)}) async-start(bf16[512,4,512]{2,1,0:T(4,128)(2,1)} %pad_maximum_fusion.1), calls=%async_computation | async-start | bytes 4194304 | tf_op jit(solution)/shard_map/all_to_all | solution.py:50
  39.6 0.0 all-gather.5.cloned.1.call-start
  39.7 0.7 all-gather.5.cloned.1.call-update
  40.4 0.2 reduce-scatter.2.cloned.1.call-start
  40.6 102.3 %all-to-all-done = bf16[512,4,512]{2,1,0:T(4,128)(2,1)S(1)} async-done(((bf16[512,4,512]{2,1,0:T(4,128)(2,1)}), bf16[512,4,512]{2,1,0:T(4,128)(2,1)S(1)}, u32[]{:S(2)}, u32[]{:S(2)}) %all-to-all-start) | async-done | bytes 2097184 | tf_op jit(solution)/shard_map/all_to_all | solution.py:50
  142.9 2.2 reshape.273
  145.1 2.4 copy.37
  147.5 0.7 fusion.38
  148.3 0.4 copy.29
  148.6 0.3 copy.35
  148.9 0.4 copy.28
  149.3 0.3 copy.34
  149.5 0.0 all-gather.7.cloned.1.call-done
  149.6 2.9 %fusion.2 = f32[256,768]{1,0:T(8,128)S(1)} fusion(bf16[256,2048]{1,0:T(8,128)(2,1)S(1)} %bitcast.81, bf16[1,768,2048]{2,1,0:T(8,128)(2,1)} %all-gather.7.cloned.1.call-done), kind=kOutput, calls=%fused_computation.5 | convolution fusion | flops 805306368 | bytes 4980736 | tf_op jit(solution)/shard_map/dot_general | solution.py:62
  152.5 2.7 %convolution_convert_fusion = bf16[768,2048]{1,0:T(8,128)(2,1)} fusion(bf16[256,2048]{1,0:T(8,128)(2,1)S(1)} %bitcast.84, f32[256,768]{1,0:T(8,128)S(1)} %fusion.2), kind=kOutput, calls=%fused_computation.1 | convolution fusion | flops 807862272 | bytes 4980736 | tf_op jit(solution)/shard_map/dot_general | solution.py:74
  155.2 0.0 all-gather.5.cloned.1.call-done
  155.2 3.0 %fusion.15 = bf16[256,768]{1,0:T(8,128)(2,1)S(1)} fusion(bf16[256,2048]{1,0:T(8,128)(2,1)S(1)} %bitcast.85, bf16[1,768,2048]{2,1,0:T(8,128)(2,1)} %all-gather.5.cloned.1.call-done, f32[256,768]{1,0:T(8,128)S(1)} %fusion.2), kind=kOutput, calls=%fused_computation.16 | convolution fusion | flops 807075840 | bytes 5373952 | tf_op jit(solution)/shard_map/dot_general | solution.py:65
  158.2 0.0 copy-start.1
  158.2 1.0 convolution_convert_fusion.1
  159.2 0.9 copy-done.1
  160.1 3.2 %pad_maximum_fusion = bf16[4,2,192,2048]{3,2,1,0:T(8,128)(2,1)} fusion(bf16[4,1,192,2048]{3,2,1,0:T(8,128)(2,1)S(1)} %bitcast.83, bf16[4,1,192,2048]{3,2,1,0:T(8,128)(2,1)S(1)} %bitcast.76), kind=kLoop, calls=%fused_computation | loop fusion | flops 3145728 | bytes 12582912 | tf_op jit(solution)/shard_map/concatenate | solution.py:77
  163.3 0.0 reduce-scatter.2.cloned.1.call-update
  163.3 2.9 %fusion.6 = bf16[256,2048]{1,0:T(8,128)(2,1)S(1)} fusion(bf16[256,768]{1,0:T(8,128)(2,1)S(1)} %fusion.15, bf16[1,768,2048]{2,1,0:T(8,128)(2,1)} %all-gather.7.cloned.1.call-done), kind=kOutput, calls=%fused_computation.9 | convolution fusion | flops 805830656 | bytes 4587520 | tf_op jit(solution)/shard_map/dot_general | solution.py:68
  166.2 0.8 reshape.266
  167.0 0.8 copy.30
  167.9 66.5 %all_to_all.10 = bf16[512,2,512]{2,1,0:T(2,128)(2,1)S(1)} all-to-all(bf16[512,2,512]{2,1,0:T(2,128)(2,1)S(1)} %bitcast.80), channel_id=1, replica_groups=mesh['expert'=128,'dp'=4] {'expert','dp'}, dimensions={0} | all-to-all | bytes 2097152 | tf_op jit(solution)/shard_map/all_to_all | solution.py:50
  234.4 0.4 reshape.268
  234.8 1.0 convolution_convert_fusion.3
  235.8 0.0 reduce-scatter.2.cloned.1.call-done
  235.8 2.7 %slice_bitcast_fusion = (bf16[1,192,2048]{2,1,0:T(8,128)(2,1)}, bf16[1,192,2048]{2,1,0:T(8,128)(2,1)}) fusion(bf16[1,2,192,2048]{3,2,1,0:T(8,128)(2,1)} %reduce-scatter.2.cloned.1.call-done), kind=kLoop, calls=%fused_computation.19 | loop fusion | bytes 3145728 | tf_op jit(solution)/shard_map/slice | solution.py:81
  (3 shorter events, 0.1 us)
Async XLA Ops:
  7.2 3.1 %copy-start = (bf16[128,512]{1,0:T(8,128)(2,1)S(1)}, bf16[128,512]{1,0:T(8,128)(2,1)}, u32[]{:S(2)}) copy-start(bf16[128,512]{1,0:T(8,128)(2,1)} %param.7) | copy-start | bytes 393220
  7.2 4.0 %copy-start.2 = (bf16[128,512]{1,0:T(8,128)(2,1)S(1)}, bf16[128,512]{1,0:T(8,128)(2,1)}, u32[]{:S(2)}) copy-start(bf16[128,512]{1,0:T(8,128)(2,1)} %param.6) | copy-start | bytes 393220
  7.2 142.4 %all-gather.7.cloned.1.call-start = ((), (), s32[]{:S(2)}) async-start(), calls=%async_computation.5 | async-start | bytes 3932160 | tf_op jit(solution)/shard_map/all_gather | solution.py:44
  15.3 127.6 %all-to-all-start = ((bf16[512,4,512]{2,1,0:T(4,128)(2,1)}), bf16[512,4,512]{2,1,0:T(4,128)(2,1)S(1)}, u32[]{:S(2)}, u32[]{:S(2)}) async-start(bf16[512,4,512]{2,1,0:T(4,128)(2,1)} %pad_maximum_fusion.1), calls=%async_computation | async-start | bytes 4194304 | tf_op jit(solution)/shard_map/all_to_all | solution.py:50
  39.6 115.6 %all-gather.5.cloned.1.call-start = ((), (), s32[]{:S(2)}) async-start(), calls=%async_computation.4 | async-start | bytes 3932160 | tf_op jit(solution)/shard_map/all_gather | solution.py:45
  40.4 195.4 %reduce-scatter.2.cloned.1.call-start = ((), (), s32[]{:S(2)}) async-start(), calls=%async_computation.3 | async-start | bytes 7864320 | tf_op jit(solution)/shard_map/reduce_scatter | solution.py:78
  158.2 1.9 copy-start.1
Sparse Core Ops, SparseCore 0:
  10.1 59.5 all-gather.6
  71.8 56.7 all-gather.4
  163.5 70.9 reduce-scatter.1

commit v2 on v1

v2 whole, which is shorter than its diff:
```python
import jax
import jax.numpy as jnp
from jax import lax
from jax.experimental import pallas as pl
from jax.experimental.pallas import tpu as pltpu
from jax.sharding import PartitionSpec as P

F32 = jnp.float32
BF16 = jnp.bfloat16
I32 = jnp.int32
CONTRACT_LAST = (((1,), (1,)), ((), ()))
CONTRACT_FIRST = (((0,), (0,)), ((), ()))
BLOCK = 256
VMEM_LIMIT = 56 * 1024 * 1024


def bits(values, low, count):
    return (values >> low) & ((1 << count) - 1)


def row_permutation(source_of):
    row = lax.broadcasted_iota(I32, (BLOCK, BLOCK), 0)
    col = lax.broadcasted_iota(I32, (BLOCK, BLOCK), 1)
    return (col == source_of(row)).astype(F32).astype(BF16)


def pick(matrix, values):
    return jnp.dot(matrix, values, preferred_element_type=F32).astype(BF16)


def send_source(i):
    e, q, h, a, r = bits(i, 5, 3), bits(i, 3, 2), bits(i, 2, 1), bits(i, 1, 1), bits(i, 0, 1)
    return a * 128 + h * 64 + e * 8 + q * 2 + r


def lanes_source(i):
    g, e, r = bits(i, 4, 4), bits(i, 1, 3), bits(i, 0, 1)
    return e * 32 + g * 2 + r


def rows_source(i):
    e, g, r = bits(i, 5, 3), bits(i, 1, 4), bits(i, 0, 1)
    return g * 16 + e * 2 + r


def final_source(i):
    f, e, q, r = bits(i, 6, 2), bits(i, 3, 3), bits(i, 1, 2), bits(i, 0, 1)
    return e * 32 + q * 8 + f * 2 + r


def dispatch_kernel(routes_ref, gates_ref, in_ref, out_ref, send_ref, chosen_ref, nat_in, nat_grad):
    route_count, tokens = routes_ref.shape
    slot_rows = chosen_ref.shape[0]
    capacity = 8
    experts = slot_rows // capacity
    expert_id = lax.broadcasted_iota(I32, (experts, tokens), 0)
    match = jnp.zeros((experts, tokens), F32)
    gates = jnp.zeros((experts, tokens), F32)
    for k in range(route_count):
        hit = routes_ref[k : k + 1, :] == expert_id
        match = jnp.where(hit, 1.0, match)
        gates = jnp.where(hit, gates_ref[k : k + 1, :], gates)
    before = lax.broadcasted_iota(I32, (tokens, tokens), 0)
    after = lax.broadcasted_iota(I32, (tokens, tokens), 1)
    earlier = jnp.where(before < after, 1.0, 0.0).astype(BF16)
    ranks = jnp.dot(match.astype(BF16), earlier, preferred_element_type=F32)
    ranks = jnp.where(match > 0.0, ranks, -1.0)
    slot = lax.broadcasted_iota(I32, (experts, capacity, tokens), 1).astype(F32)
    chosen = jnp.where(ranks[:, None, :] == slot, 1.0, 0.0)
    slot_gates = jnp.sum((chosen * gates[:, None, :]).reshape(slot_rows, tokens), axis=1, keepdims=True)
    chosen = chosen.reshape(slot_rows, tokens).astype(BF16)
    chosen_ref[...] = chosen
    nat_in[...] = jnp.dot(chosen, in_ref[...], preferred_element_type=F32).astype(BF16)
    scaled = slot_gates * jnp.dot(chosen, out_ref[...], preferred_element_type=F32)
    nat_grad[...] = scaled.astype(BF16)
    order = row_permutation(send_source)
    for blk in range(send_ref.shape[0] // BLOCK):
        at = slice(blk * 64, blk * 64 + 64)
        parts = [nat[at, h * BLOCK : h * BLOCK + BLOCK] for nat in (nat_in, nat_grad) for h in (0, 1)]
        send_ref[blk * BLOCK : blk * BLOCK + BLOCK, :] = pick(order, jnp.concatenate(parts, axis=0))


def expert_kernel(
    recv_ref, u0, u1, u2, u3, d0, d1, d2, d3,
    ret_ref, own_out, first_p, first_m, plain_p, plain_m, held_p, held_m,
    up, down, in_rows, grad_rows, own_s, fp_s, fm_s, pp_s, pm_s, hp_s, hm_s, sems, out_sems,
):
    part = u0.shape[0]
    half = part // 2
    copies = []
    for i, (ref, full) in enumerate(
        [(r, up) for r in (u0, u1, u2, u3)] + [(r, down) for r in (d0, d1, d2, d3)]
    ):
        at = (i % 4) * part
        copies.append(pltpu.make_async_copy(ref, full.at[pl.ds(at, part), :], sems.at[i]))
        copies[-1].start()
    to_lanes = row_permutation(lanes_source)
    for blk in range(recv_ref.shape[0] // BLOCK):
        moved = pick(to_lanes, recv_ref[blk * BLOCK : blk * BLOCK + BLOCK, :])
        for g in range(8):
            for a, rows in ((0, in_rows), (1, grad_rows)):
                rows[blk * 16 : blk * 16 + 16, g * BLOCK : g * BLOCK + BLOCK] = moved[
                    (2 * g + a) * 16 : (2 * g + a) * 16 + 16, :
                ]
    for copy in copies[:4]:
        copy.wait()
    pre = lax.dot_general(up[...], in_rows[...], CONTRACT_LAST, preferred_element_type=F32)
    for copy in copies[4:]:
        copy.wait()
    back = lax.dot_general(down[...], grad_rows[...], CONTRACT_LAST, preferred_element_type=F32)
    sigma = jax.nn.sigmoid(pre)
    hidden = (pre * sigma).astype(BF16)
    d_pre = (back * sigma * (1.0 + pre * (1.0 - sigma))).astype(BF16)

    width = in_rows.shape[1]
    step = 512
    for w, (left, rows) in enumerate(((d_pre, in_rows), (hidden, grad_rows))):
        for n in range(width // step):
            lanes = slice(n * step, n * step + step)
            total = jnp.dot(left, rows[:, lanes], preferred_element_type=F32).astype(BF16)
            one, two = slice(w * half, w * half + half), slice(w * part, w * part + part)
            own_s[two, lanes] = total[:part]
            hp_s[one, lanes] = total[part : part + half]
            pp_s[one, lanes] = total[part + half : 2 * part]
            pm_s[one, lanes] = total[2 * part : 2 * part + half]
            hm_s[one, lanes] = total[2 * part + half : 3 * part]
            fp_s[one, lanes] = total[3 * part : 3 * part + half]
            fm_s[one, lanes] = total[3 * part + half :]
    outs = []
    for i, (src, dst) in enumerate(
        (
            (fp_s, first_p), (fm_s, first_m), (pp_s, plain_p), (pm_s, plain_m),
            (hp_s, held_p), (hm_s, held_m), (own_s, own_out),
        )
    ):
        outs.append(pltpu.make_async_copy(src, dst, out_sems.at[i]))
        outs[-1].start()

    rows_back = lax.dot_general(d_pre, up[...], CONTRACT_FIRST, preferred_element_type=F32)
    rows_back = rows_back.astype(BF16)
    to_rows = row_permutation(rows_source)
    for blk in range(ret_ref.shape[0] // BLOCK):
        parts = [rows_back[blk * 16 : blk * 16 + 16, g * 128 : g * 128 + 128] for g in range(16)]
        ret_ref[blk * BLOCK : blk * BLOCK + BLOCK, :] = pick(to_rows, jnp.concatenate(parts, axis=0))
    for copy in outs:
        copy.wait()


def combine_kernel(recv_ref, chosen_ref, out_ref, rows):
    order = row_permutation(final_source)
    for blk in range(recv_ref.shape[0] // BLOCK):
        moved = pick(order, recv_ref[blk * BLOCK : blk * BLOCK + BLOCK, :])
        for f in range(4):
            rows[blk * 64 : blk * 64 + 64, f * 128 : f * 128 + 128] = moved[f * 64 : f * 64 + 64, :]
    total = lax.dot_general(
        chosen_ref[...], rows[...], CONTRACT_FIRST, preferred_element_type=F32
    )
    out_ref[...] = total.astype(BF16)


def grads_kernel(own, last_p, last_m, plain_p, plain_m, up_out, down_out):
    half = last_p.shape[0] // 2
    for w, out in enumerate((up_out, down_out)):
        one = slice(w * half, w * half + half)
        low = slice(2 * w * half, 2 * w * half + half)
        high = slice(2 * w * half + half, 2 * w * half + 2 * half)
        out[:half, :] = (
            own[low, :].astype(F32) + last_p[one, :].astype(F32) + plain_m[one, :].astype(F32)
        ).astype(BF16)
        out[half:, :] = (
            own[high, :].astype(F32) + plain_p[one, :].astype(F32) + last_m[one, :].astype(F32)
        ).astype(BF16)


def shape(dims, dtype=BF16):
    return jax.ShapeDtypeStruct(dims, dtype)


PARAMS = pltpu.CompilerParams(vmem_limit_bytes=VMEM_LIMIT)


def local(inputs, out_grad, gate_weights, routes, up_weight, down_weight):
    expert_count = lax.axis_size("expert")
    dp_count = lax.axis_size("dp")
    token_count, route_count = routes.shape
    capacity = 8
    slot_rows = expert_count * capacity
    row_count = slot_rows // dp_count
    part = inputs.shape[1]
    width = part * dp_count
    peers = expert_count * dp_count
    hidden_part = up_weight.shape[1]
    hidden = hidden_part * dp_count
    half = hidden_part // 2

    def shift(value, by):
        pairs = [(i, (i + by) % dp_count) for i in range(dp_count)]
        return lax.ppermute(value, "dp", pairs)

    def swap(values):
        lanes = values.shape[1]
        moved = lax.all_to_all(
            values.reshape(peers, 8, lanes), ("expert", "dp"), split_axis=0, concat_axis=0, tiled=True
        )
        return moved.reshape(peers * 8, lanes)

    send, chosen = pl.pallas_call(
        dispatch_kernel,
        out_shape=(shape((slot_rows * 4, BLOCK)), shape((slot_rows, token_count))),
        scratch_shapes=[pltpu.VMEM((slot_rows, part), BF16), pltpu.VMEM((slot_rows, part), BF16)],
        compiler_params=PARAMS,
        name="dispatch",
    )(routes.T, gate_weights.T, inputs, out_grad)
    recv = swap(send)

    up_own, down_own = up_weight[0], down_weight[0]
    ups = [up_own] + [shift(up_own, by) for by in (-1, 1, 2)]
    downs = [down_own] + [shift(down_own, by) for by in (-1, 1, 2)]

    any_spec = pl.BlockSpec(memory_space=pl.ANY)
    vmem_spec = pl.BlockSpec(memory_space=pltpu.VMEM)
    piece = shape((hidden_part, width))
    whole = shape((2 * hidden_part, width))
    ret, own, first_p, first_m, plain_p, plain_m, held_p, held_m = pl.pallas_call(
        expert_kernel,
        in_specs=[vmem_spec] + [any_spec] * 8,
        out_specs=(vmem_spec,) + (any_spec,) * 7,
        out_shape=(shape((slot_rows * 4, 128)), whole) + (piece,) * 6,
        scratch_shapes=[
            pltpu.VMEM((hidden, width), BF16),
            pltpu.VMEM((hidden, width), BF16),
            pltpu.VMEM((row_count, width), BF16),
            pltpu.VMEM((row_count, width), BF16),
            pltpu.VMEM((2 * hidden_part, width), BF16),
        ]
        + [pltpu.VMEM((hidden_part, width), BF16)] * 6
        + [pltpu.SemaphoreType.DMA((8,)), pltpu.SemaphoreType.DMA((7,))],
        compiler_params=PARAMS,
        name="expert",
    )(recv, *ups, *downs)

    got_p, got_m = shift(first_p, 1), shift(first_m, -1)
    returned = swap(ret)
    plain_p, plain_m = shift(plain_p, 1), shift(plain_m, -1)
    last_p = shift((held_p.astype(F32) + got_p.astype(F32)).astype(BF16), 1)
    last_m = shift((held_m.astype(F32) + got_m.astype(F32)).astype(BF16), -1)
    grad_up, grad_down = pl.pallas_call(
        grads_kernel,
        out_shape=(piece, piece),
        compiler_params=PARAMS,
        name="grads",
    )(own, last_p, last_m, plain_p, plain_m)

    in_grad = pl.pallas_call(
        combine_kernel,
        out_shape=shape((token_count, part)),
        scratch_shapes=[pltpu.VMEM((slot_rows, part), BF16)],
        compiler_params=PARAMS,
        name="combine",
    )(returned, chosen)
    return (in_grad, grad_up[None], grad_down[None])


def solution(mesh):
    return jax.shard_map(
        local,
        mesh=mesh,
        in_specs=(
            P("expert", "dp"),
            P("expert", "dp"),
            P("expert", None),
            P("expert", None),
            P("expert", "dp", None),
            P("expert", "dp", None),
        ),
        out_specs=(P("expert", "dp"), P("expert", "dp", None), P("expert", "dp", None)),
        check_vma=False,
    )
```

time: 245 us -> 234 us (0.955); the launches traced: 245 us -> 231 us
  blocking collectives: 66.5 us -> 0 us
  starting transfers between devices: 24.6 us -> 82.2 us
  Pallas kernels: 0 us -> 22.8 us
  waiting for transfers between devices: 104 us -> 121 us
  matrix products: 14.6 us -> 0 us
  between operations: 14 us -> 0.86 us
  local copies, waits for them, and re-layouts: 14.9 us -> 4.17 us
  other arithmetic: 6.67 us -> 0.53 us
    ppermute x0 -> x12, waiting for transfers between devices: none -> 112 us  [shift(): return lax.ppermute(value, 'dp', pairs)]
    all_to_all x1 -> x2, waiting for transfers between devices: 102 us -> 8.8 us  [swap(): lax.all_to_all(values.reshape(peers, 8, lanes), ('expert', 'dp'), split_a...]
    all_to_all x1 -> x0, blocking collectives: 66.5 us -> none  [swap(): lax.all_to_all(values, ('expert', 'dp'), split_axis=0, concat_axis=0, til...]
    ppermute x0 -> x12, starting transfers between devices: none -> 46 us  [shift(): return lax.ppermute(value, 'dp', pairs)]
    pallas_call x0 -> x4, Pallas kernels: none -> 22.8 us  [the longest x1 12.4 us: local(): pl.pallas_call(expert_kernel, in_specs=[vmem_spec] + [any_spec] * 8, out_...]
    dot_general x9 -> x0, matrix products: 14.6 us -> none  [the longest x2 3.73 us: weight_grad(): lax.dot_general(left, right, CONTRACT_FIRST, preferred_element_type=F32)]
    all_to_all x1 -> x2, starting transfers between devices: 24.3 us -> 36.1 us  [swap(): lax.all_to_all(values.reshape(peers, 8, lanes), ('expert', 'dp'), split_a...]
    reshape x7 -> x0, local copies, waits for them, and re-layouts: 7.54 us -> none  [the longest x2 4.61 us: local(): both = swap(both).reshape(expert_count, dp_count, 2, per_dev, part)]
  transfers between devices with their start and end apart: 4 -> 14, of which waited for: 1 -> 10; matrix products, arithmetic and copies ran while one was open for 10% -> 0% of each run, Pallas kernels for 0% -> 2%
where the time goes in v2:
time: 234 us; the launch traced here: 231 us
  waiting for transfers between devices  121 us (52%)
  starting transfers between devices  82.2 us (35%)
  Pallas kernels  22.8 us (10%)
  local copies, waits for them, and re-layouts  4.17 us (2%)
    ppermute x12, waiting for transfers between devices, shift(): return lax.ppermute(value, 'dp', pairs)  112 us
    ppermute x12, starting transfers between devices, shift(): return lax.ppermute(value, 'dp', pairs)  46 us
    all_to_all x2, starting transfers between devices, swap(): lax.all_to_all(values.reshape(peers, 8, lanes), ('expert', 'dp'), split_a...  36.1 us
    pallas_call x1, Pallas kernels, local(): pl.pallas_call(expert_kernel, in_specs=[vmem_spec] + [any_spec] * 8, out_...  12.4 us
    all_to_all x2, waiting for transfers between devices, swap(): lax.all_to_all(values.reshape(peers, 8, lanes), ('expert', 'dp'), split_a...  8.8 us
  transfers between devices with their start and end apart: 14, of which 10 were waited for; matrix products, arithmetic and copies ran while one was open for 0% of the time, Pallas kernels for 2%

profile of v2, /device:TPU:1, one launch (start us, length us, event | category | flops | bytes accessed | tf_op | source)
XLA Modules:
  0.0 231.4 jit_solution(15036576551060355607)
XLA Ops:
  0.6 3.8 %dispatch.1 = (bf16[4096,256]{1,0:T(8,128)(2,1)}, bf16[1024,128]{1,0:T(8,128)(2,1)}) custom-call(s32[4,128]{1,0:T(4,128)} %bitcast.22, f32[4,128]{1,0:T(4,128)} %bitcast.23, bf16[128,512]{1,0:T(8,128)(2,1)} %in_ref.1, bf16[128,512]{1,0:T(8,128)(2,1)} %out_ref.1), custom_call_target="tpu_custom_call" | custom-call | tf_op jit(solution)/shard_map/dispatch/pallas_call | solution.py:207
  4.5 0.0 copy-start.2
  4.5 24.3 %all-to-all-start = ((bf16[512,8,256]{2,1,0:T(8,128)(2,1)}), bf16[512,8,256]{2,1,0:T(8,128)(2,1)S(1)}, u32[]{:S(2)}, u32[]{:S(2)}) async-start(bf16[512,8,256]{2,1,0:T(8,128)(2,1)} %bitcast.12), calls=%async_computation | async-start | bytes 4194304 | tf_op jit(solution)/shard_map/all_to_all | solution.py:202
  28.8 0.0 copy-done.2
  28.8 4.8 %collective-permute-start.2 = (bf16[192,2048]{1,0:T(8,128)(2,1)S(1)}, bf16[192,2048]{1,0:T(8,128)(2,1)S(1)}, u32[]{:S(2)}, u32[]{:S(2)}) collective-permute-start(bf16[192,2048]{1,0:T(8,128)(2,1)S(1)} %bitcast.15), channel_id=1, source_target_pairs={{0,2},{1,3},{2,0},{3,1},{4,6},{5,7},{6,4},{7,5},{8,10},{9,11},{10,... | collective-permute-start | bytes 2359304 | tf_op jit(solution)/shard_map/ppermute | solution.py:198
  33.6 2.2 collective-permute-start.1
  35.8 4.3 %collective-permute-start = (bf16[192,2048]{1,0:T(8,128)(2,1)S(1)}, bf16[192,2048]{1,0:T(8,128)(2,1)S(1)}, u32[]{:S(2)}, u32[]{:S(2)}) collective-permute-start(bf16[192,2048]{1,0:T(8,128)(2,1)S(1)} %bitcast.17), channel_id=1, source_target_pairs={{0,3},{1,0},{2,1},{3,2},{4,7},{5,4},{6,5},{7,6},{8,11},{9,8},{10,9... | collective-permute-start | bytes 2359304 | tf_op jit(solution)/shard_map/ppermute | solution.py:198
  40.1 1.9 collective-permute-start.5
  42.0 2.5 %collective-permute-start.4 = (bf16[192,2048]{1,0:T(8,128)(2,1)}, bf16[192,2048]{1,0:T(8,128)(2,1)S(1)}, u32[]{:S(2)}, u32[]{:S(2)}) collective-permute-start(bf16[192,2048]{1,0:T(8,128)(2,1)} %bitcast.19), channel_id=1, source_target_pairs={{0,1},{1,2},{2,3},{3,0},{4,5},{5,6},{6,7},{7,4},{8,9},{9,10},{10,1... | collective-permute-start | bytes 2359304 | tf_op jit(solution)/shard_map/ppermute | solution.py:198
  44.5 9.7 %collective-permute-done.2.u3 = bf16[192,2048]{1,0:T(8,128)(2,1)S(1)} collective-permute-done((bf16[192,2048]{1,0:T(8,128)(2,1)S(1)}, bf16[192,2048]{1,0:T(8,128)(2,1)S(1)}, u32[]{:S(2)}, u32[]{:S(2)}) %collective-permute-start.2) | collective-permute-done | bytes 786464 | tf_op jit(solution)/shard_map/ppermute | solution.py:198
  54.2 0.0 copy-start.3
  54.2 7.6 %collective-permute-start.3 = (bf16[192,2048]{1,0:T(8,128)(2,1)}, bf16[192,2048]{1,0:T(8,128)(2,1)}, u32[]{:S(2)}, u32[]{:S(2)}) collective-permute-start(bf16[192,2048]{1,0:T(8,128)(2,1)} %bitcast.20), channel_id=1, source_target_pairs={{0,3},{1,0},{2,1},{3,2},{4,7},{5,4},{6,5},{7,6},{8,11},{9,8},{10,9... | collective-permute-start | bytes 2359304 | tf_op jit(solution)/shard_map/ppermute | solution.py:198
  61.9 21.6 %collective-permute-done.1.u2 = bf16[192,2048]{1,0:T(8,128)(2,1)S(1)} collective-permute-done((bf16[192,2048]{1,0:T(8,128)(2,1)S(1)}, bf16[192,2048]{1,0:T(8,128)(2,1)S(1)}, u32[]{:S(2)}, u32[]{:S(2)}) %collective-permute-start.1) | collective-permute-done | bytes 786464 | tf_op jit(solution)/shard_map/ppermute | solution.py:198
  83.5 0.0 copy-start.4
  83.5 0.0 collective-permute-done.u1
  83.5 0.0 copy-start.5
  83.5 15.2 %collective-permute-done.5.d3 = bf16[192,2048]{1,0:T(8,128)(2,1)S(1)} collective-permute-done((bf16[192,2048]{1,0:T(8,128)(2,1)}, bf16[192,2048]{1,0:T(8,128)(2,1)S(1)}, u32[]{:S(2)}, u32[]{:S(2)}) %collective-permute-start.5) | collective-permute-done | bytes 786464 | tf_op jit(solution)/shard_map/ppermute | solution.py:198
  98.8 0.0 copy-start.7
  98.8 23.6 %collective-permute-done.4.d2 = bf16[192,2048]{1,0:T(8,128)(2,1)S(1)} collective-permute-done((bf16[192,2048]{1,0:T(8,128)(2,1)}, bf16[192,2048]{1,0:T(8,128)(2,1)S(1)}, u32[]{:S(2)}, u32[]{:S(2)}) %collective-permute-start.4) | collective-permute-done | bytes 786464 | tf_op jit(solution)/shard_map/ppermute | solution.py:198
  122.3 0.0 copy-done.3
  122.3 0.0 copy-done.4
  122.4 0.0 copy-done.5
  122.4 0.0 copy-done.7
  122.4 0.0 copy-start.9
  122.4 0.9 copy-done.9
  123.3 0.0 collective-permute-done.3.d1
  123.3 8.8 %all-to-all-done = bf16[512,8,256]{2,1,0:T(8,128)(2,1)S(1)} async-done(((bf16[512,8,256]{2,1,0:T(8,128)(2,1)}), bf16[512,8,256]{2,1,0:T(8,128)(2,1)S(1)}, u32[]{:S(2)}, u32[]{:S(2)}) %all-to-all-start) | async-done | bytes 2097184 | tf_op jit(solution)/shard_map/all_to_all | solution.py:202
  132.1 0.0 copy-start
  132.1 1.4 copy-done
  133.4 12.4 %expert.1 = (bf16[4096,128]{1,0:T(8,128)(2,1)}, bf16[384,2048]{1,0:T(8,128)(2,1)}, bf16[192,2048]{1,0:T(8,128)(2,1)}, bf16[192,2048]{1,0:T(8,128)(2,1)}, bf16[19...) custom-call(bf16[4096,256]{1,0:T(8,128)(2,1)} %bitcast.10, ...), custom_call_target="tpu_custom_call" | custom-call | tf_op jit(solution)/shard_map/expert/pallas_call | solution.py:224
  145.8 0.0 copy-start.14
  145.8 0.0 copy-start.13
  145.8 11.8 %all-to-all-start.1 = ((bf16[512,8,128]{2,1,0:T(8,128)(2,1)}), bf16[512,8,128]{2,1,0:T(8,128)(2,1)S(1)}, u32[]{:S(2)}, u32[]{:S(2)}) async-start(bf16[512,8,128]{2,1,0:T(8,128)(2,1)} %bitcast.13), calls=%async_computation.1 | async-start | bytes 2097152 | tf_op jit(solution)/shard_map/all_to_all | solution.py:202
  157.6 0.0 copy-start.12
  157.7 3.4 %collective-permute-start.6 = (bf16[192,2048]{1,0:T(8,128)(2,1)}, bf16[192,2048]{1,0:T(8,128)(2,1)S(1)}, u32[]{:S(2)}, u32[]{:S(2)}) collective-permute-start(bf16[192,2048]{1,0:T(8,128)(2,1)} %get-tuple-element.20), channel_id=1, source_target_pairs={{0,1},{1,2},{2,3},{3,0},{4,5},{5,6},{6,7},{7,4},{8,9},{9,10},{10,1... | collective-permute-start | bytes 2359304 | tf_op jit(solution)/shard_map/ppermute | solution.py:198
  161.1 3.2 %collective-permute-start.8 = (bf16[192,2048]{1,0:T(8,128)(2,1)}, bf16[192,2048]{1,0:T(8,128)(2,1)S(1)}, u32[]{:S(2)}, u32[]{:S(2)}) collective-permute-start(bf16[192,2048]{1,0:T(8,128)(2,1)} %get-tuple-element.22), channel_id=1, source_target_pairs={{0,3},{1,0},{2,1},{3,2},{4,7},{5,4},{6,5},{7,6},{8,11},{9,8},{10,9... | collective-permute-start | bytes 2359304 | tf_op jit(solution)/shard_map/ppermute | solution.py:198
  164.3 2.1 collective-permute-start.10
  166.4 0.0 copy-done.14
  166.4 4.4 %collective-permute-start.11 = (bf16[192,2048]{1,0:T(8,128)(2,1)S(1)}, bf16[192,2048]{1,0:T(8,128)(2,1)S(1)}, u32[]{:S(2)}, u32[]{:S(2)}) collective-permute-start(bf16[192,2048]{1,0:T(8,128)(2,1)S(1)} %copy-done.14), channel_id=1, source_target_pairs={{0,3},{1,0},{2,1},{3,2},{4,7},{5,4},{6,5},{7,6},{8,11},{9,8},{10,9... | collective-permute-start | bytes 2359304 | tf_op jit(solution)/shard_map/ppermute | solution.py:198
  170.8 10.0 %collective-permute-done.6 = bf16[192,2048]{1,0:T(8,128)(2,1)S(1)} collective-permute-done((bf16[192,2048]{1,0:T(8,128)(2,1)}, bf16[192,2048]{1,0:T(8,128)(2,1)S(1)}, u32[]{:S(2)}, u32[]{:S(2)}) %collective-permute-start.6) | collective-permute-done | bytes 786464 | tf_op jit(solution)/shard_map/ppermute | solution.py:198
  180.8 0.0 copy-done.13
  180.8 0.3 add_convert_fusion.1
  181.1 5.5 %collective-permute-start.7 = (bf16[192,2048]{1,0:T(8,128)(2,1)S(1)}, bf16[192,2048]{1,0:T(8,128)(2,1)S(1)}, u32[]{:S(2)}, u32[]{:S(2)}) collective-permute-start(bf16[192,2048]{1,0:T(8,128)(2,1)S(1)} %add_convert_fusion.1), channel_id=1, source_target_pairs={{0,1},{1,2},{2,3},{3,0},{4,5},{5,6},{6,7},{7,4},{8,9},{9,10},{10,1... | collective-permute-start | bytes 2359304 | tf_op jit(solution)/shard_map/ppermute | solution.py:198
  186.6 0.0 collective-permute-done.8
  186.6 0.0 copy-done.12
  186.6 0.3 add_convert_fusion
  186.9 4.1 %collective-permute-start.9 = (bf16[192,2048]{1,0:T(8,128)(2,1)S(1)}, bf16[192,2048]{1,0:T(8,128)(2,1)S(1)}, u32[]{:S(2)}, u32[]{:S(2)}) collective-permute-start(bf16[192,2048]{1,0:T(8,128)(2,1)S(1)} %add_convert_fusion), channel_id=1, source_target_pairs={{0,3},{1,0},{2,1},{3,2},{4,7},{5,4},{6,5},{7,6},{8,11},{9,8},{10,9... | collective-permute-start | bytes 2359304 | tf_op jit(solution)/shard_map/ppermute | solution.py:198
  191.0 11.8 %collective-permute-done.10.plain_p = bf16[192,2048]{1,0:T(8,128)(2,1)S(1)} collective-permute-done((bf16[192,2048]{1,0:T(8,128)(2,1)}, bf16[192,2048]{1,0:T(8,128)(2,1)S(1)}, u32[]{:S(2)}, u32[]{:S(2)}) %collective-permute-start.10) | collective-permute-done | bytes 786464 | tf_op jit(solution)/shard_map/ppermute | solution.py:198
  202.8 0.0 copy-start.6
  202.8 2.9 %collective-permute-done.11.plain_m = bf16[192,2048]{1,0:T(8,128)(2,1)S(1)} collective-permute-done((bf16[192,2048]{1,0:T(8,128)(2,1)S(1)}, bf16[192,2048]{1,0:T(8,128)(2,1)S(1)}, u32[]{:S(2)}, u32[]{:S(2)}) %collective-permute-start.11) | collective-permute-done | bytes 786464 | tf_op jit(solution)/shard_map/ppermute | solution.py:198
  205.6 0.0 copy-start.8
  205.6 15.2 %collective-permute-done.7.last_p = bf16[192,2048]{1,0:T(8,128)(2,1)S(1)} collective-permute-done((bf16[192,2048]{1,0:T(8,128)(2,1)S(1)}, bf16[192,2048]{1,0:T(8,128)(2,1)S(1)}, u32[]{:S(2)}, u32[]{:S(2)}) %collective-permute-start.7) | collective-permute-done | bytes 786464 | tf_op jit(solution)/shard_map/ppermute | solution.py:198
  220.8 0.0 copy-start.10
  220.8 2.1 collective-permute-done.9.last_m
  223.0 0.0 copy-start.11
  223.0 0.0 copy-done.6
  223.0 0.0 copy-done.8
  223.0 0.0 copy-done.10
  223.0 0.9 copy-done.11
  223.9 3.8 %grads.1 = (bf16[192,2048]{1,0:T(8,128)(2,1)}, bf16[192,2048]{1,0:T(8,128)(2,1)}) custom-call(bf16[384,2048]{1,0:T(8,128)(2,1)} %get-tuple-element.18.own, bf16[192,2048]{1,0:T(8,128)(2,1)} %copy-done.10, bf16[192,2048]{1,0:T(8,128)(2,1)} %copy-done.11, bf16[192,2048]{1,0:T(8,128)(2,1)} %copy-done.6, bf16[192,2048]{1,0:T(8,128)(2,1)} %copy-done.8), custom_call_target="tpu_custom_call" | custom-call | tf_op jit(solution)/shard_map/grads/pallas_call | solution.py:247
  227.6 0.0 all-to-all-done.1
  227.6 0.0 copy-start.1
  227.6 1.0 copy-done.1
  228.6 2.8 %combine.1 = bf16[128,512]{1,0:T(8,128)(2,1)} custom-call(bf16[4096,128]{1,0:T(8,128)(2,1)} %bitcast.11, bf16[1024,128]{1,0:T(8,128)(2,1)} %get-tuple-element.17.chosen_ref), custom_call_target="tpu_custom_call" | custom-call | tf_op jit(solution)/shard_map/combine/pallas_call | solution.py:254
Async XLA Ops:
  4.5 24.3 %copy-start.2 = (bf16[1,192,2048]{2,1,0:T(8,128)(2,1)S(1)}, bf16[1,192,2048]{2,1,0:T(8,128)(2,1)}, u32[]{:S(2)}) copy-start(bf16[1,192,2048]{2,1,0:T(8,128)(2,1)} %param.10) | copy-start | bytes 2359300
  4.5 127.6 %all-to-all-start = ((bf16[512,8,256]{2,1,0:T(8,128)(2,1)}), bf16[512,8,256]{2,1,0:T(8,128)(2,1)S(1)}, u32[]{:S(2)}, u32[]{:S(2)}) async-start(bf16[512,8,256]{2,1,0:T(8,128)(2,1)} %bitcast.12), calls=%async_computation | async-start | bytes 4194304 | tf_op jit(solution)/shard_map/all_to_all | solution.py:202
  28.8 25.5 %collective-permute-start.2 = (bf16[192,2048]{1,0:T(8,128)(2,1)S(1)}, bf16[192,2048]{1,0:T(8,128)(2,1)S(1)}, u32[]{:S(2)}, u32[]{:S(2)}) collective-permute-start(bf16[192,2048]{1,0:T(8,128)(2,1)S(1)} %bitcast.15), channel_id=1, source_target_pairs={{0,2},{1,3},{2,0},{3,1},{4,6},{5,7},{6,4},{7,5},{8,10},{9,11},{10,... | collective-permute-start | bytes 2359304 | tf_op jit(solution)/shard_map/ppermute | solution.py:198
  33.6 49.9 %collective-permute-start.1 = (bf16[192,2048]{1,0:T(8,128)(2,1)S(1)}, bf16[192,2048]{1,0:T(8,128)(2,1)S(1)}, u32[]{:S(2)}, u32[]{:S(2)}) collective-permute-start(bf16[192,2048]{1,0:T(8,128)(2,1)S(1)} %bitcast.16), channel_id=1, source_target_pairs={{0,1},{1,2},{2,3},{3,0},{4,5},{5,6},{6,7},{7,4},{8,9},{9,10},{10,1... | collective-permute-start | bytes 2359304 | tf_op jit(solution)/shard_map/ppermute | solution.py:198
  35.8 47.7 %collective-permute-start = (bf16[192,2048]{1,0:T(8,128)(2,1)S(1)}, bf16[192,2048]{1,0:T(8,128)(2,1)S(1)}, u32[]{:S(2)}, u32[]{:S(2)}) collective-permute-start(bf16[192,2048]{1,0:T(8,128)(2,1)S(1)} %bitcast.17), channel_id=1, source_target_pairs={{0,3},{1,0},{2,1},{3,2},{4,7},{5,4},{6,5},{7,6},{8,11},{9,8},{10,9... | collective-permute-start | bytes 2359304 | tf_op jit(solution)/shard_map/ppermute | solution.py:198
  40.1 58.6 %collective-permute-start.5 = (bf16[192,2048]{1,0:T(8,128)(2,1)}, bf16[192,2048]{1,0:T(8,128)(2,1)S(1)}, u32[]{:S(2)}, u32[]{:S(2)}) collective-permute-start(bf16[192,2048]{1,0:T(8,128)(2,1)} %bitcast.18), channel_id=1, source_target_pairs={{0,2},{1,3},{2,0},{3,1},{4,6},{5,7},{6,4},{7,5},{8,10},{9,11},{10,... | collective-permute-start | bytes 2359304 | tf_op jit(solution)/shard_map/ppermute | solution.py:198
  42.0 80.3 %collective-permute-start.4 = (bf16[192,2048]{1,0:T(8,128)(2,1)}, bf16[192,2048]{1,0:T(8,128)(2,1)S(1)}, u32[]{:S(2)}, u32[]{:S(2)}) collective-permute-start(bf16[192,2048]{1,0:T(8,128)(2,1)} %bitcast.19), channel_id=1, source_target_pairs={{0,1},{1,2},{2,3},{3,0},{4,5},{5,6},{6,7},{7,4},{8,9},{9,10},{10,1... | collective-permute-start | bytes 2359304 | tf_op jit(solution)/shard_map/ppermute | solution.py:198
  54.2 68.1 %copy-start.3 = (bf16[192,2048]{1,0:T(8,128)(2,1)}, bf16[192,2048]{1,0:T(8,128)(2,1)S(1)}, u32[]{:S(2)}) copy-start(bf16[192,2048]{1,0:T(8,128)(2,1)S(1)} %collective-permute-done.2.u3) | copy-start | bytes 2359300
  54.2 69.0 %collective-permute-start.3 = (bf16[192,2048]{1,0:T(8,128)(2,1)}, bf16[192,2048]{1,0:T(8,128)(2,1)}, u32[]{:S(2)}, u32[]{:S(2)}) collective-permute-start(bf16[192,2048]{1,0:T(8,128)(2,1)} %bitcast.20), channel_id=1, source_target_pairs={{0,3},{1,0},{2,1},{3,2},{4,7},{5,4},{6,5},{7,6},{8,11},{9,8},{10,9... | collective-permute-start | bytes 2359304 | tf_op jit(solution)/shard_map/ppermute | solution.py:198
  83.5 38.8 %copy-start.4 = (bf16[192,2048]{1,0:T(8,128)(2,1)}, bf16[192,2048]{1,0:T(8,128)(2,1)S(1)}, u32[]{:S(2)}) copy-start(bf16[192,2048]{1,0:T(8,128)(2,1)S(1)} %collective-permute-done.1.u2) | copy-start | bytes 2359300
  83.5 38.8 %copy-start.5 = (bf16[192,2048]{1,0:T(8,128)(2,1)}, bf16[192,2048]{1,0:T(8,128)(2,1)S(1)}, u32[]{:S(2)}) copy-start(bf16[192,2048]{1,0:T(8,128)(2,1)S(1)} %collective-permute-done.u1) | copy-start | bytes 2359300
  98.8 23.6 %copy-start.7 = (bf16[192,2048]{1,0:T(8,128)(2,1)}, bf16[192,2048]{1,0:T(8,128)(2,1)S(1)}, u32[]{:S(2)}) copy-start(bf16[192,2048]{1,0:T(8,128)(2,1)S(1)} %collective-permute-done.5.d3) | copy-start | bytes 2359300
  122.4 0.9 copy-start.9
  132.1 1.4 copy-start
  145.8 20.6 %copy-start.14 = (bf16[192,2048]{1,0:T(8,128)(2,1)S(1)}, bf16[192,2048]{1,0:T(8,128)(2,1)}, u32[]{:S(2)}) copy-start(bf16[192,2048]{1,0:T(8,128)(2,1)} %get-tuple-element.24) | copy-start | bytes 2359300
  145.8 35.0 %copy-start.13 = (bf16[192,2048]{1,0:T(8,128)(2,1)S(1)}, bf16[192,2048]{1,0:T(8,128)(2,1)}, u32[]{:S(2)}) copy-start(bf16[192,2048]{1,0:T(8,128)(2,1)} %get-tuple-element.19) | copy-start | bytes 2359300
  145.8 81.8 %all-to-all-start.1 = ((bf16[512,8,128]{2,1,0:T(8,128)(2,1)}), bf16[512,8,128]{2,1,0:T(8,128)(2,1)S(1)}, u32[]{:S(2)}, u32[]{:S(2)}) async-start(bf16[512,8,128]{2,1,0:T(8,128)(2,1)} %bitcast.13), calls=%async_computation.1 | async-start | bytes 2097152 | tf_op jit(solution)/shard_map/all_to_all | solution.py:202
  157.6 29.0 %copy-start.12 = (bf16[192,2048]{1,0:T(8,128)(2,1)S(1)}, bf16[192,2048]{1,0:T(8,128)(2,1)}, u32[]{:S(2)}) copy-start(bf16[192,2048]{1,0:T(8,128)(2,1)} %get-tuple-element.21) | copy-start | bytes 2359300
  157.7 23.2 %collective-permute-start.6 = (bf16[192,2048]{1,0:T(8,128)(2,1)}, bf16[192,2048]{1,0:T(8,128)(2,1)S(1)}, u32[]{:S(2)}, u32[]{:S(2)}) collective-permute-start(bf16[192,2048]{1,0:T(8,128)(2,1)} %get-tuple-element.20), channel_id=1, source_target_pairs={{0,1},{1,2},{2,3},{3,0},{4,5},{5,6},{6,7},{7,4},{8,9},{9,10},{10,1... | collective-permute-start | bytes 2359304 | tf_op jit(solution)/shard_map/ppermute | solution.py:198
  161.1 25.5 %collective-permute-start.8 = (bf16[192,2048]{1,0:T(8,128)(2,1)}, bf16[192,2048]{1,0:T(8,128)(2,1)S(1)}, u32[]{:S(2)}, u32[]{:S(2)}) collective-permute-start(bf16[192,2048]{1,0:T(8,128)(2,1)} %get-tuple-element.22), channel_id=1, source_target_pairs={{0,3},{1,0},{2,1},{3,2},{4,7},{5,4},{6,5},{7,6},{8,11},{9,8},{10,9... | collective-permute-start | bytes 2359304 | tf_op jit(solution)/shard_map/ppermute | solution.py:198
  164.3 38.5 %collective-permute-start.10 = (bf16[192,2048]{1,0:T(8,128)(2,1)}, bf16[192,2048]{1,0:T(8,128)(2,1)S(1)}, u32[]{:S(2)}, u32[]{:S(2)}) collective-permute-start(bf16[192,2048]{1,0:T(8,128)(2,1)} %get-tuple-element.23), channel_id=1, source_target_pairs={{0,1},{1,2},{2,3},{3,0},{4,5},{5,6},{6,7},{7,4},{8,9},{9,10},{10,1... | collective-permute-start | bytes 2359304 | tf_op jit(solution)/shard_map/ppermute | solution.py:198
  166.4 39.2 %collective-permute-start.11 = (bf16[192,2048]{1,0:T(8,128)(2,1)S(1)}, bf16[192,2048]{1,0:T(8,128)(2,1)S(1)}, u32[]{:S(2)}, u32[]{:S(2)}) collective-permute-start(bf16[192,2048]{1,0:T(8,128)(2,1)S(1)} %copy-done.14), channel_id=1, source_target_pairs={{0,3},{1,0},{2,1},{3,2},{4,7},{5,4},{6,5},{7,6},{8,11},{9,8},{10,9... | collective-permute-start | bytes 2359304 | tf_op jit(solution)/shard_map/ppermute | solution.py:198
  181.1 39.7 %collective-permute-start.7 = (bf16[192,2048]{1,0:T(8,128)(2,1)S(1)}, bf16[192,2048]{1,0:T(8,128)(2,1)S(1)}, u32[]{:S(2)}, u32[]{:S(2)}) collective-permute-start(bf16[192,2048]{1,0:T(8,128)(2,1)S(1)} %add_convert_fusion.1), channel_id=1, source_target_pairs={{0,1},{1,2},{2,3},{3,0},{4,5},{5,6},{6,7},{7,4},{8,9},{9,10},{10,1... | collective-permute-start | bytes 2359304 | tf_op jit(solution)/shard_map/ppermute | solution.py:198
  186.9 36.1 %collective-permute-start.9 = (bf16[192,2048]{1,0:T(8,128)(2,1)S(1)}, bf16[192,2048]{1,0:T(8,128)(2,1)S(1)}, u32[]{:S(2)}, u32[]{:S(2)}) collective-permute-start(bf16[192,2048]{1,0:T(8,128)(2,1)S(1)} %add_convert_fusion), channel_id=1, source_target_pairs={{0,3},{1,0},{2,1},{3,2},{4,7},{5,4},{6,5},{7,6},{8,11},{9,8},{10,9... | collective-permute-start | bytes 2359304 | tf_op jit(solution)/shard_map/ppermute | solution.py:198
  202.8 20.2 %copy-start.6 = (bf16[192,2048]{1,0:T(8,128)(2,1)}, bf16[192,2048]{1,0:T(8,128)(2,1)S(1)}, u32[]{:S(2)}) copy-start(bf16[192,2048]{1,0:T(8,128)(2,1)S(1)} %collective-permute-done.10.plain_p) | copy-start | bytes 2359300
  205.6 17.3 %copy-start.8 = (bf16[192,2048]{1,0:T(8,128)(2,1)}, bf16[192,2048]{1,0:T(8,128)(2,1)S(1)}, u32[]{:S(2)}) copy-start(bf16[192,2048]{1,0:T(8,128)(2,1)S(1)} %collective-permute-done.11.plain_m) | copy-start | bytes 2359300
  220.8 2.1 copy-start.10
  223.0 0.9 copy-start.11
  227.6 1.0 copy-start.1

commit v3 on v2

--- a/solution.py
+++ b/solution.py
@@ -11,7 +11,7 @@
 CONTRACT_LAST = (((1,), (1,)), ((), ()))
 CONTRACT_FIRST = (((0,), (0,)), ((), ()))
 BLOCK = 256
-VMEM_LIMIT = 56 * 1024 * 1024
+VMEM_LIMIT = 32 * 1024 * 1024
 
 
 def bits(values, low, count):
@@ -48,7 +48,29 @@
     return e * 32 + q * 8 + f * 2 + r
 
 
-def dispatch_kernel(routes_ref, gates_ref, in_ref, out_ref, send_ref, chosen_ref, nat_in, nat_grad):
+CHUNKS = 4
+
+
+def chunk_copy(src, dst, sems, i):
+    rows = src.shape[0] // CHUNKS
+    at = pl.ds(i * rows, rows)
+    return pltpu.make_async_copy(src.at[at, :], dst.at[at, :], sems.at[i])
+
+
+def drain(src, dst, sems, blk):
+    per_chunk = src.shape[0] // BLOCK // CHUNKS
+    if (blk + 1) % per_chunk == 0:
+        chunk_copy(src, dst, sems, blk // per_chunk).start()
+
+
+def finish(src, dst, sems):
+    for i in range(CHUNKS):
+        chunk_copy(src, dst, sems, i).wait()
+
+
+def dispatch_kernel(
+    routes_ref, gates_ref, in_ref, out_ref, send_hbm, chosen_ref, send_ref, nat_in, nat_grad, sems
+):
     route_count, tokens = routes_ref.shape
     slot_rows = chosen_ref.shape[0]
     capacity = 8
@@ -78,12 +100,14 @@
         at = slice(blk * 64, blk * 64 + 64)
         parts = [nat[at, h * BLOCK : h * BLOCK + BLOCK] for nat in (nat_in, nat_grad) for h in (0, 1)]
         send_ref[blk * BLOCK : blk * BLOCK + BLOCK, :] = pick(order, jnp.concatenate(parts, axis=0))
+        drain(send_ref, send_hbm, sems, blk)
+    finish(send_ref, send_hbm, sems)
 
 
 def expert_kernel(
     recv_ref, u0, u1, u2, u3, d0, d1, d2, d3,
-    ret_ref, own_out, first_p, first_m, plain_p, plain_m, held_p, held_m,
-    up, down, in_rows, grad_rows, own_s, fp_s, fm_s, pp_s, pm_s, hp_s, hm_s, sems, out_sems,
+    d_pre_ref, up, own_out, first_p, first_m, plain_p, plain_m, held_p, held_m,
+    down, in_rows, grad_rows, own_s, fp_s, fm_s, pp_s, pm_s, hp_s, hm_s, sems, out_sems,
 ):
     part = u0.shape[0]
     half = part // 2
@@ -111,39 +135,60 @@
     sigma = jax.nn.sigmoid(pre)
     hidden = (pre * sigma).astype(BF16)
     d_pre = (back * sigma * (1.0 + pre * (1.0 - sigma))).astype(BF16)
+    d_pre_ref[...] = d_pre
+
+    outs = []
+
+    def send(i, src, dst):
+        outs.append(pltpu.make_async_copy(src, dst, out_sems.at[i]))
+        outs[-1].start()
 
     width = in_rows.shape[1]
     step = 512
-    for w, (left, rows) in enumerate(((d_pre, in_rows), (hidden, grad_rows))):
-        for n in range(width // step):
-            lanes = slice(n * step, n * step + step)
-            total = jnp.dot(left, rows[:, lanes], preferred_element_type=F32).astype(BF16)
+    for top in (3 * part, 2 * part, part, 0):
+        for w, (left, rows) in enumerate(((d_pre, in_rows), (hidden, grad_rows))):
             one, two = slice(w * half, w * half + half), slice(w * part, w * part + part)
-            own_s[two, lanes] = total[:part]
-            hp_s[one, lanes] = total[part : part + half]
-            pp_s[one, lanes] = total[part + half : 2 * part]
-            pm_s[one, lanes] = total[2 * part : 2 * part + half]
-            hm_s[one, lanes] = total[2 * part + half : 3 * part]
-            fp_s[one, lanes] = total[3 * part : 3 * part + half]
-            fm_s[one, lanes] = total[3 * part + half :]
-    outs = []
-    for i, (src, dst) in enumerate(
-        (
-            (fp_s, first_p), (fm_s, first_m), (pp_s, plain_p), (pm_s, plain_m),
-            (hp_s, held_p), (hm_s, held_m), (own_s, own_out),
-        )
-    ):
-        outs.append(pltpu.make_async_copy(src, dst, out_sems.at[i]))
-        outs[-1].start()
-
-    rows_back = lax.dot_general(d_pre, up[...], CONTRACT_FIRST, preferred_element_type=F32)
-    rows_back = rows_back.astype(BF16)
+            for n in range(width // step):
+                lanes = slice(n * step, n * step + step)
+                total = jnp.dot(
+                    left[top : top + part], rows[:, lanes], preferred_element_type=F32
+                ).astype(BF16)
+                if top == 0:
+                    own_s[two, lanes] = total
+                elif top == part:
+                    hp_s[one, lanes] = total[:half]
+                    pp_s[one, lanes] = total[half:]
+                elif top == 2 * part:
+                    pm_s[one, lanes] = total[:half]
+                    hm_s[one, lanes] = total[half:]
+                else:
+                    fp_s[one, lanes] = total[:half]
+                    fm_s[one, lanes] = total[half:]
+        if top == 0:
+            send(6, own_s, own_out)
+        elif top == part:
+            send(4, hp_s, held_p)
+            send(2, pp_s, plain_p)
+        elif top == 2 * part:
+            send(3, pm_s, plain_m)
+            send(5, hm_s, held_m)
+        else:
+            send(0, fp_s, first_p)
+            send(1, fm_s, first_m)
+    for copy in outs:
+        copy.wait()
+
+
+def return_kernel(d_pre_ref, up_ref, ret_hbm, ret_ref, sems):
+    rows_back = lax.dot_general(
+        d_pre_ref[...], up_ref[...], CONTRACT_FIRST, preferred_element_type=F32
+    ).astype(BF16)
     to_rows = row_permutation(rows_source)
     for blk in range(ret_ref.shape[0] // BLOCK):
         parts = [rows_back[blk * 16 : blk * 16 + 16, g * 128 : g * 128 + 128] for g in range(16)]
         ret_ref[blk * BLOCK : blk * BLOCK + BLOCK, :] = pick(to_rows, jnp.concatenate(parts, axis=0))
-    for copy in outs:
-        copy.wait()
+        drain(ret_ref, ret_hbm, sems, blk)
+    finish(ret_ref, ret_hbm, sems)
 
 
 def combine_kernel(recv_ref, chosen_ref, out_ref, rows):
@@ -174,6 +219,18 @@
 
 def shape(dims, dtype=BF16):
     return jax.ShapeDtypeStruct(dims, dtype)
+
+
+def on_chip(dims):
+    return pltpu.VMEM(dims, BF16)
+
+
+def in_hbm(dims):
+    return pltpu.HBM(dims, BF16)
+
+
+def keep(value):
+    return pltpu.with_memory_space_constraint(value, pltpu.VMEM)
 
 
 PARAMS = pltpu.CompilerParams(vmem_limit_bytes=VMEM_LIMIT)
@@ -204,10 +261,19 @@
         )
         return moved.reshape(peers * 8, lanes)
 
+    hbm = pl.BlockSpec(memory_space=pltpu.HBM)
+    vmem = pl.BlockSpec(memory_space=pltpu.VMEM)
+    send_rows = slot_rows * 4
     send, chosen = pl.pallas_call(
         dispatch_kernel,
-        out_shape=(shape((slot_rows * 4, BLOCK)), shape((slot_rows, token_count))),
-        scratch_shapes=[pltpu.VMEM((slot_rows, part), BF16), pltpu.VMEM((slot_rows, part), BF16)],
+        out_specs=(hbm, vmem),
+        out_shape=(in_hbm((send_rows, BLOCK)), on_chip((slot_rows, token_count))),
+        scratch_shapes=[
+            pltpu.VMEM((send_rows, BLOCK), BF16),
+            pltpu.VMEM((slot_rows, part), BF16),
+            pltpu.VMEM((slot_rows, part), BF16),
+            pltpu.SemaphoreType.DMA((CHUNKS,)),
+        ],
         compiler_params=PARAMS,
         name="dispatch",
     )(routes.T, gate_weights.T, inputs, out_grad)
@@ -216,40 +282,44 @@
     up_own, down_own = up_weight[0], down_weight[0]
     ups = [up_own] + [shift(up_own, by) for by in (-1, 1, 2)]
     downs = [down_own] + [shift(down_own, by) for by in (-1, 1, 2)]
-
-    any_spec = pl.BlockSpec(memory_space=pl.ANY)
-    vmem_spec = pl.BlockSpec(memory_space=pltpu.VMEM)
-    piece = shape((hidden_part, width))
-    whole = shape((2 * hidden_part, width))
-    ret, own, first_p, first_m, plain_p, plain_m, held_p, held_m = pl.pallas_call(
+    weights = [pltpu.with_memory_space_constraint(value, pltpu.HBM) for value in ups + downs]
+
+    piece = (hidden_part, width)
+    whole = (2 * hidden_part, width)
+    d_pre, up_full, own, first_p, first_m, plain_p, plain_m, held_p, held_m = pl.pallas_call(
         expert_kernel,
-        in_specs=[vmem_spec] + [any_spec] * 8,
-        out_specs=(vmem_spec,) + (any_spec,) * 7,
-        out_shape=(shape((slot_rows * 4, 128)), whole) + (piece,) * 6,
-        scratch_shapes=[
-            pltpu.VMEM((hidden, width), BF16),
-            pltpu.VMEM((hidden, width), BF16),
-            pltpu.VMEM((row_count, width), BF16),
-            pltpu.VMEM((row_count, width), BF16),
-            pltpu.VMEM((2 * hidden_part, width), BF16),
-        ]
-        + [pltpu.VMEM((hidden_part, width), BF16)] * 6
+        in_specs=[vmem] + [hbm] * 8,
+        out_specs=(vmem,) * 2 + (hbm,) * 7,
+        out_shape=(on_chip((hidden, row_count)), on_chip((hidden, width)), in_hbm(whole))
+        + (in_hbm(piece),) * 6,
+        scratch_shapes=[pltpu.VMEM((hidden, width), BF16)]
+        + [pltpu.VMEM((row_count, width), BF16)] * 2
+        + [pltpu.VMEM(whole, BF16)]
+        + [pltpu.VMEM(piece, BF16)] * 6
         + [pltpu.SemaphoreType.DMA((8,)), pltpu.SemaphoreType.DMA((7,))],
         compiler_params=PARAMS,
         name="expert",
-    )(recv, *ups, *downs)
+    )(keep(recv), *weights)
 
     got_p, got_m = shift(first_p, 1), shift(first_m, -1)
+    ret = pl.pallas_call(
+        return_kernel,
+        out_specs=hbm,
+        out_shape=in_hbm((send_rows, 128)),
+        scratch_shapes=[pltpu.VMEM((send_rows, 128), BF16), pltpu.SemaphoreType.DMA((CHUNKS,))],
+        compiler_params=PARAMS,
+        name="rows_back",
+    )(keep(d_pre), keep(up_full))
     returned = swap(ret)
     plain_p, plain_m = shift(plain_p, 1), shift(plain_m, -1)
     last_p = shift((held_p.astype(F32) + got_p.astype(F32)).astype(BF16), 1)
     last_m = shift((held_m.astype(F32) + got_m.astype(F32)).astype(BF16), -1)
     grad_up, grad_down = pl.pallas_call(
         grads_kernel,
-        out_shape=(piece, piece),
+        out_shape=(shape(piece), shape(piece)),
         compiler_params=PARAMS,
         name="grads",
-    )(own, last_p, last_m, plain_p, plain_m)
+    )(keep(own), keep(last_p), keep(last_m), keep(plain_p), keep(plain_m))
 
     in_grad = pl.pallas_call(
         combine_kernel,
@@ -257,7 +327,7 @@
         scratch_shapes=[pltpu.VMEM((slot_rows, part), BF16)],
         compiler_params=PARAMS,
         name="combine",
-    )(returned, chosen)
+    )(keep(returned), keep(chosen))
     return (in_grad, grad_up[None], grad_down[None])
 
 

time: 234 us -> 228 us (0.974)
  Pallas kernels: 22.8 us -> 16.9 us
    pallas_call x3 -> x4, Pallas kernels: 20 us -> 15.3 us  [the longest x1 8.87 us: local(): pl.pallas_call(expert_kernel, in_specs=[vmem] + [hbm] * 8, out_specs=(vme...]
  transfers between devices with their start and end apart: 14 -> 14, of which waited for: 10 -> 10; matrix products, arithmetic and copies ran while one was open for 0% -> 0% of each run, Pallas kernels for 2% -> 1%
where the time goes in v3:
time: 228 us; the launch traced here: 225 us
  waiting for transfers between devices  121 us (53%)
  starting transfers between devices  82.3 us (36%)
  Pallas kernels  16.9 us (7%)
  local copies, waits for them, and re-layouts  4.09 us (2%)
    ppermute x12, waiting for transfers between devices, shift(): return lax.ppermute(value, 'dp', pairs)  112 us
    ppermute x12, starting transfers between devices, shift(): return lax.ppermute(value, 'dp', pairs)  46.2 us
    all_to_all x2, starting transfers between devices, swap(): lax.all_to_all(values.reshape(peers, 8, lanes), ('expert', 'dp'), split_a...  36.1 us
    pallas_call x1, Pallas kernels, local(): pl.pallas_call(expert_kernel, in_specs=[vmem] + [hbm] * 8, out_specs=(vme...  8.87 us
    all_to_all x2, waiting for transfers between devices, swap(): lax.all_to_all(values.reshape(peers, 8, lanes), ('expert', 'dp'), split_a...  8.79 us
  transfers between devices with their start and end apart: 14, of which 10 were waited for; matrix products, arithmetic and copies ran while one was open for 0% of the time, Pallas kernels for 1%

profile of v3, /device:TPU:1, one launch (start us, length us, event | category | flops | bytes accessed | tf_op | source)
XLA Modules:
  0.0 225.5 jit_solution(12127066330734877265)
XLA Ops:
  0.6 0.0 copy-start.1
  0.6 0.9 copy-done.1
  1.5 0.0 copy-start.2
  1.5 0.9 copy-done.2
  2.4 0.0 copy-start.3
  2.4 0.7 copy-done.3
  3.1 0.0 copy-start.4
  3.1 0.7 copy-done.4
  3.8 2.4 %dispatch.1 = (bf16[4096,256]{1,0:T(8,128)(2,1)}, bf16[1024,128]{1,0:T(8,128)(2,1)S(1)}) custom-call(s32[4,128]{1,0:T(4,128)S(1)} %bitcast.12, f32[4,128]{1,0:T(4,128)S(1)} %bitcast.13, bf16[128,512]{1,0:T(8,128)(2,1)S(1)} %copy-done.1, bf16[128,512]{1,0:T(8,128)(2,1)S(1)} %copy-done.2), custom_call_target="tpu_custom_call" | custom-call | tf_op jit(solution)/shard_map/dispatch/pallas_call | solution.py:267
  6.3 0.0 copy-start.5
  6.3 24.3 %all-to-all-start = ((bf16[512,8,256]{2,1,0:T(8,128)(2,1)}), bf16[512,8,256]{2,1,0:T(8,128)(2,1)S(1)}, u32[]{:S(2)}, u32[]{:S(2)}) async-start(bf16[512,8,256]{2,1,0:T(8,128)(2,1)} %bitcast.15), calls=%async_computation | async-start | bytes 4194304 | tf_op jit(solution)/shard_map/all_to_all | solution.py:259
  30.6 0.0 copy-done.5
  30.6 4.8 %collective-permute-start.2 = (bf16[192,2048]{1,0:T(8,128)(2,1)S(1)}, bf16[192,2048]{1,0:T(8,128)(2,1)S(1)}, u32[]{:S(2)}, u32[]{:S(2)}) collective-permute-start(bf16[192,2048]{1,0:T(8,128)(2,1)S(1)} %bitcast.17), channel_id=1, source_target_pairs={{0,2},{1,3},{2,0},{3,1},{4,6},{5,7},{6,4},{7,5},{8,10},{9,11},{10,... | collective-permute-start | bytes 2359304 | tf_op jit(solution)/shard_map/ppermute | solution.py:255
  35.4 2.2 collective-permute-start.1
  37.6 4.3 %collective-permute-start = (bf16[192,2048]{1,0:T(8,128)(2,1)S(1)}, bf16[192,2048]{1,0:T(8,128)(2,1)S(1)}, u32[]{:S(2)}, u32[]{:S(2)}) collective-permute-start(bf16[192,2048]{1,0:T(8,128)(2,1)S(1)} %bitcast.19), channel_id=1, source_target_pairs={{0,3},{1,0},{2,1},{3,2},{4,7},{5,4},{6,5},{7,6},{8,11},{9,8},{10,9... | collective-permute-start | bytes 2359304 | tf_op jit(solution)/shard_map/ppermute | solution.py:255
  41.9 1.9 collective-permute-start.5
  43.8 2.5 %collective-permute-start.4 = (bf16[192,2048]{1,0:T(8,128)(2,1)}, bf16[192,2048]{1,0:T(8,128)(2,1)S(1)}, u32[]{:S(2)}, u32[]{:S(2)}) collective-permute-start(bf16[192,2048]{1,0:T(8,128)(2,1)} %bitcast.21), channel_id=1, source_target_pairs={{0,1},{1,2},{2,3},{3,0},{4,5},{5,6},{6,7},{7,4},{8,9},{9,10},{10,1... | collective-permute-start | bytes 2359304 | tf_op jit(solution)/shard_map/ppermute | solution.py:255
  46.3 9.7 %collective-permute-done.2.u3 = bf16[192,2048]{1,0:T(8,128)(2,1)S(1)} collective-permute-done((bf16[192,2048]{1,0:T(8,128)(2,1)S(1)}, bf16[192,2048]{1,0:T(8,128)(2,1)S(1)}, u32[]{:S(2)}, u32[]{:S(2)}) %collective-permute-start.2) | collective-permute-done | bytes 786464 | tf_op jit(solution)/shard_map/ppermute | solution.py:255
  56.0 0.0 copy-start.6
  56.1 7.6 %collective-permute-start.3 = (bf16[192,2048]{1,0:T(8,128)(2,1)}, bf16[192,2048]{1,0:T(8,128)(2,1)}, u32[]{:S(2)}, u32[]{:S(2)}) collective-permute-start(bf16[192,2048]{1,0:T(8,128)(2,1)} %bitcast.22), channel_id=1, source_target_pairs={{0,3},{1,0},{2,1},{3,2},{4,7},{5,4},{6,5},{7,6},{8,11},{9,8},{10,9... | collective-permute-start | bytes 2359304 | tf_op jit(solution)/shard_map/ppermute | solution.py:255
  63.7 21.6 %collective-permute-done.1.u2 = bf16[192,2048]{1,0:T(8,128)(2,1)S(1)} collective-permute-done((bf16[192,2048]{1,0:T(8,128)(2,1)S(1)}, bf16[192,2048]{1,0:T(8,128)(2,1)S(1)}, u32[]{:S(2)}, u32[]{:S(2)}) %collective-permute-start.1) | collective-permute-done | bytes 786464 | tf_op jit(solution)/shard_map/ppermute | solution.py:255
  85.3 0.0 copy-start.7
  85.3 0.0 collective-permute-done.u1
  85.3 0.0 copy-start.8
  85.3 15.2 %collective-permute-done.5.d3 = bf16[192,2048]{1,0:T(8,128)(2,1)S(1)} collective-permute-done((bf16[192,2048]{1,0:T(8,128)(2,1)}, bf16[192,2048]{1,0:T(8,128)(2,1)S(1)}, u32[]{:S(2)}, u32[]{:S(2)}) %collective-permute-start.5) | collective-permute-done | bytes 786464 | tf_op jit(solution)/shard_map/ppermute | solution.py:255
  100.6 0.0 copy-start.9
  100.6 23.6 %collective-permute-done.4.d2 = bf16[192,2048]{1,0:T(8,128)(2,1)S(1)} collective-permute-done((bf16[192,2048]{1,0:T(8,128)(2,1)}, bf16[192,2048]{1,0:T(8,128)(2,1)S(1)}, u32[]{:S(2)}, u32[]{:S(2)}) %collective-permute-start.4) | collective-permute-done | bytes 786464 | tf_op jit(solution)/shard_map/ppermute | solution.py:255
  124.2 0.0 copy-done.6
  124.2 0.0 copy-done.7
  124.2 0.0 copy-done.8
  124.2 0.0 copy-done.9
  124.2 0.0 copy-start.10
  124.2 0.9 copy-done.10
  125.1 0.0 collective-permute-done.3.d1
  125.1 8.8 %all-to-all-done = bf16[512,8,256]{2,1,0:T(8,128)(2,1)S(1)} async-done(((bf16[512,8,256]{2,1,0:T(8,128)(2,1)}), bf16[512,8,256]{2,1,0:T(8,128)(2,1)S(1)}, u32[]{:S(2)}, u32[]{:S(2)}) %all-to-all-start) | async-done | bytes 2097184 | tf_op jit(solution)/shard_map/all_to_all | solution.py:259
  133.9 8.9 %expert.1 = (bf16[768,256]{1,0:T(8,128)(2,1)S(1)}, bf16[768,2048]{1,0:T(8,128)(2,1)S(1)}, bf16[384,2048]{1,0:T(8,128)(2,1)}, bf16[192,2048]{1,0:T(8,128)(2,1)}, ...) custom-call(bf16[4096,256]{1,0:T(8,128)(2,1)S(1)} %bitcast.10, ...), custom_call_target="tpu_custom_call" | custom-call | tf_op jit(solution)/shard_map/expert/pallas_call | solution.py:289
  142.7 2.4 %rows_back.1 = bf16[4096,128]{1,0:T(8,128)(2,1)} custom-call(bf16[768,256]{1,0:T(8,128)(2,1)S(1)} %get-tuple-element.17.d_pre_ref, bf16[768,2048]{1,0:T(8,128)(2,1)S(1)} %get-tuple-element.18.up_ref), custom_call_target="tpu_custom_call" | custom-call | tf_op jit(solution)/shard_map/rows_back/pallas_call | solution.py:305
  145.2 0.0 copy-start.13
  145.2 0.0 copy-start.12
  145.2 11.8 %all-to-all-start.1 = ((bf16[512,8,128]{2,1,0:T(8,128)(2,1)}), bf16[512,8,128]{2,1,0:T(8,128)(2,1)S(1)}, u32[]{:S(2)}, u32[]{:S(2)}) async-start(bf16[512,8,128]{2,1,0:T(8,128)(2,1)} %bitcast.14), calls=%async_computation.1 | async-start | bytes 2097152 | tf_op jit(solution)/shard_map/all_to_all | solution.py:259
  157.0 0.0 copy-start.11
  157.0 3.4 %collective-permute-start.6 = (bf16[192,2048]{1,0:T(8,128)(2,1)}, bf16[192,2048]{1,0:T(8,128)(2,1)S(1)}, u32[]{:S(2)}, u32[]{:S(2)}) collective-permute-start(bf16[192,2048]{1,0:T(8,128)(2,1)} %get-tuple-element.22), channel_id=1, source_target_pairs={{0,1},{1,2},{2,3},{3,0},{4,5},{5,6},{6,7},{7,4},{8,9},{9,10},{10,1... | collective-permute-start | bytes 2359304 | tf_op jit(solution)/shard_map/ppermute | solution.py:255
  160.4 3.2 %collective-permute-start.8 = (bf16[192,2048]{1,0:T(8,128)(2,1)}, bf16[192,2048]{1,0:T(8,128)(2,1)S(1)}, u32[]{:S(2)}, u32[]{:S(2)}) collective-permute-start(bf16[192,2048]{1,0:T(8,128)(2,1)} %get-tuple-element.24), channel_id=1, source_target_pairs={{0,3},{1,0},{2,1},{3,2},{4,7},{5,4},{6,5},{7,6},{8,11},{9,8},{10,9... | collective-permute-start | bytes 2359304 | tf_op jit(solution)/shard_map/ppermute | solution.py:255
  163.7 2.1 collective-permute-start.10
  165.7 0.0 copy-done.13
  165.8 4.4 %collective-permute-start.11 = (bf16[192,2048]{1,0:T(8,128)(2,1)S(1)}, bf16[192,2048]{1,0:T(8,128)(2,1)S(1)}, u32[]{:S(2)}, u32[]{:S(2)}) collective-permute-start(bf16[192,2048]{1,0:T(8,128)(2,1)S(1)} %copy-done.13), channel_id=1, source_target_pairs={{0,3},{1,0},{2,1},{3,2},{4,7},{5,4},{6,5},{7,6},{8,11},{9,8},{10,9... | collective-permute-start | bytes 2359304 | tf_op jit(solution)/shard_map/ppermute | solution.py:255
  170.2 10.0 %collective-permute-done.6 = bf16[192,2048]{1,0:T(8,128)(2,1)S(1)} collective-permute-done((bf16[192,2048]{1,0:T(8,128)(2,1)}, bf16[192,2048]{1,0:T(8,128)(2,1)S(1)}, u32[]{:S(2)}, u32[]{:S(2)}) %collective-permute-start.6) | collective-permute-done | bytes 786464 | tf_op jit(solution)/shard_map/ppermute | solution.py:255
  180.2 0.0 copy-done.12
  180.2 0.3 add_convert_fusion.1
  180.4 0.0 copy-start
  180.5 5.6 %collective-permute-start.7 = (bf16[192,2048]{1,0:T(8,128)(2,1)S(1)}, bf16[192,2048]{1,0:T(8,128)(2,1)S(1)}, u32[]{:S(2)}, u32[]{:S(2)}) collective-permute-start(bf16[192,2048]{1,0:T(8,128)(2,1)S(1)} %add_convert_fusion.1), channel_id=1, source_target_pairs={{0,1},{1,2},{2,3},{3,0},{4,5},{5,6},{6,7},{7,4},{8,9},{9,10},{10,1... | collective-permute-start | bytes 2359304 | tf_op jit(solution)/shard_map/ppermute | solution.py:255
  186.1 0.0 collective-permute-done.8
  186.1 0.0 copy-done.11
  186.1 0.3 add_convert_fusion
  186.4 4.1 %collective-permute-start.9 = (bf16[192,2048]{1,0:T(8,128)(2,1)S(1)}, bf16[192,2048]{1,0:T(8,128)(2,1)S(1)}, u32[]{:S(2)}, u32[]{:S(2)}) collective-permute-start(bf16[192,2048]{1,0:T(8,128)(2,1)S(1)} %add_convert_fusion), channel_id=1, source_target_pairs={{0,3},{1,0},{2,1},{3,2},{4,7},{5,4},{6,5},{7,6},{8,11},{9,8},{10,9... | collective-permute-start | bytes 2359304 | tf_op jit(solution)/shard_map/ppermute | solution.py:255
  190.5 11.7 %collective-permute-done.10.plain_p = bf16[192,2048]{1,0:T(8,128)(2,1)S(1)} collective-permute-done((bf16[192,2048]{1,0:T(8,128)(2,1)}, bf16[192,2048]{1,0:T(8,128)(2,1)S(1)}, u32[]{:S(2)}, u32[]{:S(2)}) %collective-permute-start.10) | collective-permute-done | bytes 786464 | tf_op jit(solution)/shard_map/ppermute | solution.py:255
  202.1 2.9 %collective-permute-done.11.plain_m = bf16[192,2048]{1,0:T(8,128)(2,1)S(1)} collective-permute-done((bf16[192,2048]{1,0:T(8,128)(2,1)S(1)}, bf16[192,2048]{1,0:T(8,128)(2,1)S(1)}, u32[]{:S(2)}, u32[]{:S(2)}) %collective-permute-start.11) | collective-permute-done | bytes 786464 | tf_op jit(solution)/shard_map/ppermute | solution.py:255
  205.0 15.2 %collective-permute-done.7.last_p = bf16[192,2048]{1,0:T(8,128)(2,1)S(1)} collective-permute-done((bf16[192,2048]{1,0:T(8,128)(2,1)S(1)}, bf16[192,2048]{1,0:T(8,128)(2,1)S(1)}, u32[]{:S(2)}, u32[]{:S(2)}) %collective-permute-start.7) | collective-permute-done | bytes 786464 | tf_op jit(solution)/shard_map/ppermute | solution.py:255
  220.2 2.1 collective-permute-done.9.last_m
  222.3 0.0 copy-done
  222.3 1.6 grads.1
  223.9 0.0 all-to-all-done.1
  223.9 1.5 combine.1
Async XLA Ops:
  0.6 0.9 copy-start.1
  1.5 0.9 copy-start.2
  2.4 0.7 copy-start.3
  3.1 0.7 copy-start.4
  6.3 24.3 %copy-start.5 = (bf16[1,192,2048]{2,1,0:T(8,128)(2,1)S(1)}, bf16[1,192,2048]{2,1,0:T(8,128)(2,1)}, u32[]{:S(2)}) copy-start(bf16[1,192,2048]{2,1,0:T(8,128)(2,1)} %param.10) | copy-start | bytes 2359300
  6.3 127.6 %all-to-all-start = ((bf16[512,8,256]{2,1,0:T(8,128)(2,1)}), bf16[512,8,256]{2,1,0:T(8,128)(2,1)S(1)}, u32[]{:S(2)}, u32[]{:S(2)}) async-start(bf16[512,8,256]{2,1,0:T(8,128)(2,1)} %bitcast.15), calls=%async_computation | async-start | bytes 4194304 | tf_op jit(solution)/shard_map/all_to_all | solution.py:259
  30.6 25.5 %collective-permute-start.2 = (bf16[192,2048]{1,0:T(8,128)(2,1)S(1)}, bf16[192,2048]{1,0:T(8,128)(2,1)S(1)}, u32[]{:S(2)}, u32[]{:S(2)}) collective-permute-start(bf16[192,2048]{1,0:T(8,128)(2,1)S(1)} %bitcast.17), channel_id=1, source_target_pairs={{0,2},{1,3},{2,0},{3,1},{4,6},{5,7},{6,4},{7,5},{8,10},{9,11},{10,... | collective-permute-start | bytes 2359304 | tf_op jit(solution)/shard_map/ppermute | solution.py:255
  35.4 49.9 %collective-permute-start.1 = (bf16[192,2048]{1,0:T(8,128)(2,1)S(1)}, bf16[192,2048]{1,0:T(8,128)(2,1)S(1)}, u32[]{:S(2)}, u32[]{:S(2)}) collective-permute-start(bf16[192,2048]{1,0:T(8,128)(2,1)S(1)} %bitcast.18), channel_id=1, source_target_pairs={{0,1},{1,2},{2,3},{3,0},{4,5},{5,6},{6,7},{7,4},{8,9},{9,10},{10,1... | collective-permute-start | bytes 2359304 | tf_op jit(solution)/shard_map/ppermute | solution.py:255
  37.6 47.7 %collective-permute-start = (bf16[192,2048]{1,0:T(8,128)(2,1)S(1)}, bf16[192,2048]{1,0:T(8,128)(2,1)S(1)}, u32[]{:S(2)}, u32[]{:S(2)}) collective-permute-start(bf16[192,2048]{1,0:T(8,128)(2,1)S(1)} %bitcast.19), channel_id=1, source_target_pairs={{0,3},{1,0},{2,1},{3,2},{4,7},{5,4},{6,5},{7,6},{8,11},{9,8},{10,9... | collective-permute-start | bytes 2359304 | tf_op jit(solution)/shard_map/ppermute | solution.py:255
  41.9 58.6 %collective-permute-start.5 = (bf16[192,2048]{1,0:T(8,128)(2,1)}, bf16[192,2048]{1,0:T(8,128)(2,1)S(1)}, u32[]{:S(2)}, u32[]{:S(2)}) collective-permute-start(bf16[192,2048]{1,0:T(8,128)(2,1)} %bitcast.20), channel_id=1, source_target_pairs={{0,2},{1,3},{2,0},{3,1},{4,6},{5,7},{6,4},{7,5},{8,10},{9,11},{10,... | collective-permute-start | bytes 2359304 | tf_op jit(solution)/shard_map/ppermute | solution.py:255
  43.8 80.3 %collective-permute-start.4 = (bf16[192,2048]{1,0:T(8,128)(2,1)}, bf16[192,2048]{1,0:T(8,128)(2,1)S(1)}, u32[]{:S(2)}, u32[]{:S(2)}) collective-permute-start(bf16[192,2048]{1,0:T(8,128)(2,1)} %bitcast.21), channel_id=1, source_target_pairs={{0,1},{1,2},{2,3},{3,0},{4,5},{5,6},{6,7},{7,4},{8,9},{9,10},{10,1... | collective-permute-start | bytes 2359304 | tf_op jit(solution)/shard_map/ppermute | solution.py:255
  56.0 68.1 %copy-start.6 = (bf16[192,2048]{1,0:T(8,128)(2,1)}, bf16[192,2048]{1,0:T(8,128)(2,1)S(1)}, u32[]{:S(2)}) copy-start(bf16[192,2048]{1,0:T(8,128)(2,1)S(1)} %collective-permute-done.2.u3) | copy-start | bytes 2359300
  56.1 69.0 %collective-permute-start.3 = (bf16[192,2048]{1,0:T(8,128)(2,1)}, bf16[192,2048]{1,0:T(8,128)(2,1)}, u32[]{:S(2)}, u32[]{:S(2)}) collective-permute-start(bf16[192,2048]{1,0:T(8,128)(2,1)} %bitcast.22), channel_id=1, source_target_pairs={{0,3},{1,0},{2,1},{3,2},{4,7},{5,4},{6,5},{7,6},{8,11},{9,8},{10,9... | collective-permute-start | bytes 2359304 | tf_op jit(solution)/shard_map/ppermute | solution.py:255
  85.3 38.8 %copy-start.7 = (bf16[192,2048]{1,0:T(8,128)(2,1)}, bf16[192,2048]{1,0:T(8,128)(2,1)S(1)}, u32[]{:S(2)}) copy-start(bf16[192,2048]{1,0:T(8,128)(2,1)S(1)} %collective-permute-done.1.u2) | copy-start | bytes 2359300
  85.3 38.8 %copy-start.8 = (bf16[192,2048]{1,0:T(8,128)(2,1)}, bf16[192,2048]{1,0:T(8,128)(2,1)S(1)}, u32[]{:S(2)}) copy-start(bf16[192,2048]{1,0:T(8,128)(2,1)S(1)} %collective-permute-done.u1) | copy-start | bytes 2359300
  100.6 23.6 %copy-start.9 = (bf16[192,2048]{1,0:T(8,128)(2,1)}, bf16[192,2048]{1,0:T(8,128)(2,1)S(1)}, u32[]{:S(2)}) copy-start(bf16[192,2048]{1,0:T(8,128)(2,1)S(1)} %collective-permute-done.5.d3) | copy-start | bytes 2359300
  124.2 0.9 copy-start.10
  145.2 20.6 %copy-start.13 = (bf16[192,2048]{1,0:T(8,128)(2,1)S(1)}, bf16[192,2048]{1,0:T(8,128)(2,1)}, u32[]{:S(2)}) copy-start(bf16[192,2048]{1,0:T(8,128)(2,1)} %get-tuple-element.26) | copy-start | bytes 2359300
  145.2 35.0 %copy-start.12 = (bf16[192,2048]{1,0:T(8,128)(2,1)S(1)}, bf16[192,2048]{1,0:T(8,128)(2,1)}, u32[]{:S(2)}) copy-start(bf16[192,2048]{1,0:T(8,128)(2,1)} %get-tuple-element.21) | copy-start | bytes 2359300
  145.2 78.8 %all-to-all-start.1 = ((bf16[512,8,128]{2,1,0:T(8,128)(2,1)}), bf16[512,8,128]{2,1,0:T(8,128)(2,1)S(1)}, u32[]{:S(2)}, u32[]{:S(2)}) async-start(bf16[512,8,128]{2,1,0:T(8,128)(2,1)} %bitcast.14), calls=%async_computation.1 | async-start | bytes 2097152 | tf_op jit(solution)/shard_map/all_to_all | solution.py:259
  157.0 29.1 %copy-start.11 = (bf16[192,2048]{1,0:T(8,128)(2,1)S(1)}, bf16[192,2048]{1,0:T(8,128)(2,1)}, u32[]{:S(2)}) copy-start(bf16[192,2048]{1,0:T(8,128)(2,1)} %get-tuple-element.23) | copy-start | bytes 2359300
  157.0 23.2 %collective-permute-start.6 = (bf16[192,2048]{1,0:T(8,128)(2,1)}, bf16[192,2048]{1,0:T(8,128)(2,1)S(1)}, u32[]{:S(2)}, u32[]{:S(2)}) collective-permute-start(bf16[192,2048]{1,0:T(8,128)(2,1)} %get-tuple-element.22), channel_id=1, source_target_pairs={{0,1},{1,2},{2,3},{3,0},{4,5},{5,6},{6,7},{7,4},{8,9},{9,10},{10,1... | collective-permute-start | bytes 2359304 | tf_op jit(solution)/shard_map/ppermute | solution.py:255
  160.4 25.7 %collective-permute-start.8 = (bf16[192,2048]{1,0:T(8,128)(2,1)}, bf16[192,2048]{1,0:T(8,128)(2,1)S(1)}, u32[]{:S(2)}, u32[]{:S(2)}) collective-permute-start(bf16[192,2048]{1,0:T(8,128)(2,1)} %get-tuple-element.24), channel_id=1, source_target_pairs={{0,3},{1,0},{2,1},{3,2},{4,7},{5,4},{6,5},{7,6},{8,11},{9,8},{10,9... | collective-permute-start | bytes 2359304 | tf_op jit(solution)/shard_map/ppermute | solution.py:255
  163.7 38.5 %collective-permute-start.10 = (bf16[192,2048]{1,0:T(8,128)(2,1)}, bf16[192,2048]{1,0:T(8,128)(2,1)S(1)}, u32[]{:S(2)}, u32[]{:S(2)}) collective-permute-start(bf16[192,2048]{1,0:T(8,128)(2,1)} %get-tuple-element.25), channel_id=1, source_target_pairs={{0,1},{1,2},{2,3},{3,0},{4,5},{5,6},{6,7},{7,4},{8,9},{9,10},{10,1... | collective-permute-start | bytes 2359304 | tf_op jit(solution)/shard_map/ppermute | solution.py:255
  165.8 39.2 %collective-permute-start.11 = (bf16[192,2048]{1,0:T(8,128)(2,1)S(1)}, bf16[192,2048]{1,0:T(8,128)(2,1)S(1)}, u32[]{:S(2)}, u32[]{:S(2)}) collective-permute-start(bf16[192,2048]{1,0:T(8,128)(2,1)S(1)} %copy-done.13), channel_id=1, source_target_pairs={{0,3},{1,0},{2,1},{3,2},{4,7},{5,4},{6,5},{7,6},{8,11},{9,8},{10,9... | collective-permute-start | bytes 2359304 | tf_op jit(solution)/shard_map/ppermute | solution.py:255
  180.4 41.9 %copy-start = (bf16[384,2048]{1,0:T(8,128)(2,1)S(1)}, bf16[384,2048]{1,0:T(8,128)(2,1)}, u32[]{:S(2)}) copy-start(bf16[384,2048]{1,0:T(8,128)(2,1)} %get-tuple-element.20.own) | copy-start | bytes 4718596
  180.5 39.7 %collective-permute-start.7 = (bf16[192,2048]{1,0:T(8,128)(2,1)S(1)}, bf16[192,2048]{1,0:T(8,128)(2,1)S(1)}, u32[]{:S(2)}, u32[]{:S(2)}) collective-permute-start(bf16[192,2048]{1,0:T(8,128)(2,1)S(1)} %add_convert_fusion.1), channel_id=1, source_target_pairs={{0,1},{1,2},{2,3},{3,0},{4,5},{5,6},{6,7},{7,4},{8,9},{9,10},{10,1... | collective-permute-start | bytes 2359304 | tf_op jit(solution)/shard_map/ppermute | solution.py:255
  186.4 35.9 %collective-permute-start.9 = (bf16[192,2048]{1,0:T(8,128)(2,1)S(1)}, bf16[192,2048]{1,0:T(8,128)(2,1)S(1)}, u32[]{:S(2)}, u32[]{:S(2)}) collective-permute-start(bf16[192,2048]{1,0:T(8,128)(2,1)S(1)} %add_convert_fusion), channel_id=1, source_target_pairs={{0,3},{1,0},{2,1},{3,2},{4,7},{5,4},{6,5},{7,6},{8,11},{9,8},{10,9... | collective-permute-start | bytes 2359304 | tf_op jit(solution)/shard_map/ppermute | solution.py:255

commit v4 on v3

--- a/solution.py
+++ b/solution.py
@@ -69,8 +69,22 @@
 
 
 def dispatch_kernel(
-    routes_ref, gates_ref, in_ref, out_ref, send_hbm, chosen_ref, send_ref, nat_in, nat_grad, sems
+    routes_hbm, gates_hbm, in_hbm_ref, out_hbm_ref, send_hbm, chosen_ref,
+    routes_ref, gates_ref, in_ref, out_ref, send_ref, nat_in, nat_grad, sems, in_sems,
 ):
+    loads = [
+        pltpu.make_async_copy(src, dst, in_sems.at[i])
+        for i, (src, dst) in enumerate(
+            (
+                (routes_hbm, routes_ref), (gates_hbm, gates_ref),
+                (in_hbm_ref, in_ref), (out_hbm_ref, out_ref),
+            )
+        )
+    ]
+    for load in loads:
+        load.start()
+    for load in loads[:2]:
+        load.wait()
     route_count, tokens = routes_ref.shape
     slot_rows = chosen_ref.shape[0]
     capacity = 8
@@ -92,6 +106,8 @@
     slot_gates = jnp.sum((chosen * gates[:, None, :]).reshape(slot_rows, tokens), axis=1, keepdims=True)
     chosen = chosen.reshape(slot_rows, tokens).astype(BF16)
     chosen_ref[...] = chosen
+    for load in loads[2:]:
+        load.wait()
     nat_in[...] = jnp.dot(chosen, in_ref[...], preferred_element_type=F32).astype(BF16)
     scaled = slot_gates * jnp.dot(chosen, out_ref[...], preferred_element_type=F32)
     nat_grad[...] = scaled.astype(BF16)
@@ -233,6 +249,10 @@
     return pltpu.with_memory_space_constraint(value, pltpu.VMEM)
 
 
+def leave(value):
+    return pltpu.with_memory_space_constraint(value, pltpu.HBM)
+
+
 PARAMS = pltpu.CompilerParams(vmem_limit_bytes=VMEM_LIMIT)
 
 
@@ -266,23 +286,29 @@
     send_rows = slot_rows * 4
     send, chosen = pl.pallas_call(
         dispatch_kernel,
+        in_specs=[hbm] * 4,
         out_specs=(hbm, vmem),
         out_shape=(in_hbm((send_rows, BLOCK)), on_chip((slot_rows, token_count))),
         scratch_shapes=[
+            pltpu.VMEM((route_count, token_count), I32),
+            pltpu.VMEM((route_count, token_count), F32),
+            pltpu.VMEM((token_count, part), BF16),
+            pltpu.VMEM((token_count, part), BF16),
             pltpu.VMEM((send_rows, BLOCK), BF16),
             pltpu.VMEM((slot_rows, part), BF16),
             pltpu.VMEM((slot_rows, part), BF16),
             pltpu.SemaphoreType.DMA((CHUNKS,)),
+            pltpu.SemaphoreType.DMA((4,)),
         ],
         compiler_params=PARAMS,
         name="dispatch",
-    )(routes.T, gate_weights.T, inputs, out_grad)
+    )(*[leave(value) for value in (routes.T, gate_weights.T, inputs, out_grad)])
     recv = swap(send)
 
     up_own, down_own = up_weight[0], down_weight[0]
     ups = [up_own] + [shift(up_own, by) for by in (-1, 1, 2)]
     downs = [down_own] + [shift(down_own, by) for by in (-1, 1, 2)]
-    weights = [pltpu.with_memory_space_constraint(value, pltpu.HBM) for value in ups + downs]
+    weights = [leave(value) for value in ups + downs]
 
     piece = (hidden_part, width)
     whole = (2 * hidden_part, width)
@@ -318,6 +344,7 @@
         grads_kernel,
         out_shape=(shape(piece), shape(piece)),
         compiler_params=PARAMS,
+        cost_estimate=pl.CostEstimate(flops=3 * 10**10, transcendentals=0, bytes_accessed=6 * 10**6),
         name="grads",
     )(keep(own), keep(last_p), keep(last_m), keep(plain_p), keep(plain_m))
 

time: 228 us -> 221 us (0.969)
  starting transfers between devices: 82.3 us -> 78.6 us
  local copies, waits for them, and re-layouts: 4.09 us -> 0.97 us
    ppermute x12, waiting for transfers between devices: 112 us -> 103 us  [shift(): return lax.ppermute(value, 'dp', pairs)]
    all_to_all x2, waiting for transfers between devices: 8.79 us -> 17.5 us  [swap(): lax.all_to_all(values.reshape(peers, 8, lanes), ('expert', 'dp'), split_a...]
    unnamed x28 -> x18, local copies, waits for them, and re-layouts: 4.09 us -> 0.97 us
    ppermute x12, starting transfers between devices: 46.2 us -> 43.1 us  [shift(): return lax.ppermute(value, 'dp', pairs)]
  transfers between devices with their start and end apart: 14 -> 14, of which waited for: 10 -> 10; matrix products, arithmetic and copies ran while one was open for 0% -> 1% of each run, Pallas kernels for 1% -> 2%
where the time goes in v4:
time: 221 us; the launch traced here: 220 us
  waiting for transfers between devices  121 us (55%)
  starting transfers between devices  78.6 us (36%)
  Pallas kernels  17.7 us (8%)
    ppermute x12, waiting for transfers between devices, shift(): return lax.ppermute(value, 'dp', pairs)  103 us
    ppermute x12, starting transfers between devices, shift(): return lax.ppermute(value, 'dp', pairs)  43.1 us
    all_to_all x2, starting transfers between devices, swap(): lax.all_to_all(values.reshape(peers, 8, lanes), ('expert', 'dp'), split_a...  35.5 us
    all_to_all x2, waiting for transfers between devices, swap(): lax.all_to_all(values.reshape(peers, 8, lanes), ('expert', 'dp'), split_a...  17.5 us
    pallas_call x1, Pallas kernels, local(): pl.pallas_call(expert_kernel, in_specs=[vmem] + [hbm] * 8, out_specs=(vme...  8.84 us
  transfers between devices with their start and end apart: 14, of which 10 were waited for; matrix products, arithmetic and copies ran while one was open for 1% of the time, Pallas kernels for 2%

profile of v4, /device:TPU:1, one launch (start us, length us, event | category | flops | bytes accessed | tf_op | source)
XLA Modules:
  0.0 220.5 jit_solution(6595469679684377332)
XLA Ops:
  0.6 3.4 %dispatch.1 = (bf16[4096,256]{1,0:T(8,128)(2,1)}, bf16[1024,128]{1,0:T(8,128)(2,1)S(1)}) custom-call(s32[4,128]{1,0:T(4,128)} %bitcast.22, f32[4,128]{1,0:T(4,128)} %bitcast.23, bf16[128,512]{1,0:T(8,128)(2,1)} %in_hbm_ref.1, bf16[128,512]{1,0:T(8,128)(2,1)} %out_hbm_ref.1), custom_call_target="tpu_custom_call" | custom-call | tf_op jit(solution)/shard_map/dispatch/pallas_call | solution.py:287
  4.0 0.0 copy-start.1
  4.0 24.3 %all-to-all-start = ((bf16[512,8,256]{2,1,0:T(8,128)(2,1)}), bf16[512,8,256]{2,1,0:T(8,128)(2,1)S(1)}, u32[]{:S(2)}, u32[]{:S(2)}) async-start(bf16[512,8,256]{2,1,0:T(8,128)(2,1)} %bitcast.13), calls=%async_computation | async-start | bytes 4194304 | tf_op jit(solution)/shard_map/all_to_all | solution.py:279
  28.3 0.0 copy-done.1
  28.3 4.8 %collective-permute-start.2 = (bf16[192,2048]{1,0:T(8,128)(2,1)S(1)}, bf16[192,2048]{1,0:T(8,128)(2,1)S(1)}, u32[]{:S(2)}, u32[]{:S(2)}) collective-permute-start(bf16[192,2048]{1,0:T(8,128)(2,1)S(1)} %bitcast.15), channel_id=1, source_target_pairs={{0,2},{1,3},{2,0},{3,1},{4,6},{5,7},{6,4},{7,5},{8,10},{9,11},{10,... | collective-permute-start | bytes 2359304 | tf_op jit(solution)/shard_map/ppermute | solution.py:275
  33.1 2.2 collective-permute-start.1
  35.3 4.3 %collective-permute-start = (bf16[192,2048]{1,0:T(8,128)(2,1)S(1)}, bf16[192,2048]{1,0:T(8,128)(2,1)S(1)}, u32[]{:S(2)}, u32[]{:S(2)}) collective-permute-start(bf16[192,2048]{1,0:T(8,128)(2,1)S(1)} %bitcast.17), channel_id=1, source_target_pairs={{0,3},{1,0},{2,1},{3,2},{4,7},{5,4},{6,5},{7,6},{8,11},{9,8},{10,9... | collective-permute-start | bytes 2359304 | tf_op jit(solution)/shard_map/ppermute | solution.py:275
  39.6 1.9 collective-permute-start.5
  41.6 2.5 %collective-permute-start.4 = (bf16[192,2048]{1,0:T(8,128)(2,1)}, bf16[192,2048]{1,0:T(8,128)(2,1)S(1)}, u32[]{:S(2)}, u32[]{:S(2)}) collective-permute-start(bf16[192,2048]{1,0:T(8,128)(2,1)} %bitcast.19), channel_id=1, source_target_pairs={{0,1},{1,2},{2,3},{3,0},{4,5},{5,6},{6,7},{7,4},{8,9},{9,10},{10,1... | collective-permute-start | bytes 2359304 | tf_op jit(solution)/shard_map/ppermute | solution.py:275
  44.1 9.7 %collective-permute-done.2.u3 = bf16[192,2048]{1,0:T(8,128)(2,1)S(1)} collective-permute-done((bf16[192,2048]{1,0:T(8,128)(2,1)S(1)}, bf16[192,2048]{1,0:T(8,128)(2,1)S(1)}, u32[]{:S(2)}, u32[]{:S(2)}) %collective-permute-start.2) | collective-permute-done | bytes 786464 | tf_op jit(solution)/shard_map/ppermute | solution.py:275
  53.8 0.0 copy-start.2
  53.8 7.6 %collective-permute-start.3 = (bf16[192,2048]{1,0:T(8,128)(2,1)}, bf16[192,2048]{1,0:T(8,128)(2,1)}, u32[]{:S(2)}, u32[]{:S(2)}) collective-permute-start(bf16[192,2048]{1,0:T(8,128)(2,1)} %bitcast.20), channel_id=1, source_target_pairs={{0,3},{1,0},{2,1},{3,2},{4,7},{5,4},{6,5},{7,6},{8,11},{9,8},{10,9... | collective-permute-start | bytes 2359304 | tf_op jit(solution)/shard_map/ppermute | solution.py:275
  61.4 21.6 %collective-permute-done.1.u2 = bf16[192,2048]{1,0:T(8,128)(2,1)S(1)} collective-permute-done((bf16[192,2048]{1,0:T(8,128)(2,1)S(1)}, bf16[192,2048]{1,0:T(8,128)(2,1)S(1)}, u32[]{:S(2)}, u32[]{:S(2)}) %collective-permute-start.1) | collective-permute-done | bytes 786464 | tf_op jit(solution)/shard_map/ppermute | solution.py:275
  83.1 0.0 copy-start.3
  83.1 0.0 collective-permute-done.u1
  83.1 0.0 copy-start.4
  83.1 15.2 %collective-permute-done.5.d3 = bf16[192,2048]{1,0:T(8,128)(2,1)S(1)} collective-permute-done((bf16[192,2048]{1,0:T(8,128)(2,1)}, bf16[192,2048]{1,0:T(8,128)(2,1)S(1)}, u32[]{:S(2)}, u32[]{:S(2)}) %collective-permute-start.5) | collective-permute-done | bytes 786464 | tf_op jit(solution)/shard_map/ppermute | solution.py:275
  98.3 0.0 copy-start.5
  98.3 23.6 %collective-permute-done.4.d2 = bf16[192,2048]{1,0:T(8,128)(2,1)S(1)} collective-permute-done((bf16[192,2048]{1,0:T(8,128)(2,1)}, bf16[192,2048]{1,0:T(8,128)(2,1)S(1)}, u32[]{:S(2)}, u32[]{:S(2)}) %collective-permute-start.4) | collective-permute-done | bytes 786464 | tf_op jit(solution)/shard_map/ppermute | solution.py:275
  121.9 0.0 copy-done.2
  121.9 0.0 copy-done.3
  121.9 0.0 copy-done.4
  121.9 0.0 copy-done.5
  121.9 0.0 copy-start.6
  121.9 0.9 copy-done.6
  122.9 0.0 collective-permute-done.3.d1
  122.9 8.7 %all-to-all-done = bf16[512,8,256]{2,1,0:T(8,128)(2,1)S(1)} async-done(((bf16[512,8,256]{2,1,0:T(8,128)(2,1)}), bf16[512,8,256]{2,1,0:T(8,128)(2,1)S(1)}, u32[]{:S(2)}, u32[]{:S(2)}) %all-to-all-start) | async-done | bytes 2097184 | tf_op jit(solution)/shard_map/all_to_all | solution.py:279
  131.6 8.8 %expert.1 = (bf16[768,256]{1,0:T(8,128)(2,1)S(1)}, bf16[768,2048]{1,0:T(8,128)(2,1)S(1)}, bf16[384,2048]{1,0:T(8,128)(2,1)}, bf16[192,2048]{1,0:T(8,128)(2,1)}, ...) custom-call(bf16[4096,256]{1,0:T(8,128)(2,1)S(1)} %bitcast.10, ...), custom_call_target="tpu_custom_call" | custom-call | tf_op jit(solution)/shard_map/expert/pallas_call | solution.py:315
  140.4 1.9 collective-permute-start.6
  142.4 4.6 %collective-permute-start.8 = (bf16[192,2048]{1,0:T(8,128)(2,1)}, bf16[192,2048]{1,0:T(8,128)(2,1)S(1)}, u32[]{:S(2)}, u32[]{:S(2)}) collective-permute-start(bf16[192,2048]{1,0:T(8,128)(2,1)} %get-tuple-element.24), channel_id=1, source_target_pairs={{0,3},{1,0},{2,1},{3,2},{4,7},{5,4},{6,5},{7,6},{8,11},{9,8},{10,9... | collective-permute-start | bytes 2359304 | tf_op jit(solution)/shard_map/ppermute | solution.py:275
  147.0 2.4 %rows_back.1 = bf16[4096,128]{1,0:T(8,128)(2,1)} custom-call(bf16[768,256]{1,0:T(8,128)(2,1)S(1)} %get-tuple-element.17.d_pre_ref, bf16[768,2048]{1,0:T(8,128)(2,1)S(1)} %get-tuple-element.18.up_ref), custom_call_target="tpu_custom_call" | custom-call | tf_op jit(solution)/shard_map/rows_back/pallas_call | solution.py:331
  149.3 0.0 copy-start.8
  149.3 11.2 %all-to-all-start.1 = ((bf16[512,8,128]{2,1,0:T(8,128)(2,1)}), bf16[512,8,128]{2,1,0:T(8,128)(2,1)S(1)}, u32[]{:S(2)}, u32[]{:S(2)}) async-start(bf16[512,8,128]{2,1,0:T(8,128)(2,1)} %bitcast.12), calls=%async_computation.1 | async-start | bytes 2097152 | tf_op jit(solution)/shard_map/all_to_all | solution.py:279
  160.6 0.0 copy-start.7
  160.6 3.4 %collective-permute-start.10 = (bf16[192,2048]{1,0:T(8,128)(2,1)}, bf16[192,2048]{1,0:T(8,128)(2,1)S(1)}, u32[]{:S(2)}, u32[]{:S(2)}) collective-permute-start(bf16[192,2048]{1,0:T(8,128)(2,1)} %get-tuple-element.25), channel_id=1, source_target_pairs={{0,1},{1,2},{2,3},{3,0},{4,5},{5,6},{6,7},{7,4},{8,9},{9,10},{10,1... | collective-permute-start | bytes 2359304 | tf_op jit(solution)/shard_map/ppermute | solution.py:275
  164.0 3.2 %collective-permute-start.11 = (bf16[192,2048]{1,0:T(8,128)(2,1)}, bf16[192,2048]{1,0:T(8,128)(2,1)S(1)}, u32[]{:S(2)}, u32[]{:S(2)}) collective-permute-start(bf16[192,2048]{1,0:T(8,128)(2,1)} %get-tuple-element.26), channel_id=1, source_target_pairs={{0,3},{1,0},{2,1},{3,2},{4,7},{5,4},{6,5},{7,6},{8,11},{9,8},{10,9... | collective-permute-start | bytes 2359304 | tf_op jit(solution)/shard_map/ppermute | solution.py:275
  167.2 0.0 collective-permute-done.6
  167.2 0.0 copy-done.8
  167.2 1.4 add_convert_fusion.1
  168.6 0.0 copy-start
  168.6 2.2 %collective-permute-start.7 = (bf16[192,2048]{1,0:T(8,128)(2,1)S(1)}, bf16[192,2048]{1,0:T(8,128)(2,1)S(1)}, u32[]{:S(2)}, u32[]{:S(2)}) collective-permute-start(bf16[192,2048]{1,0:T(8,128)(2,1)S(1)} %add_convert_fusion.1), channel_id=1, source_target_pairs={{0,1},{1,2},{2,3},{3,0},{4,5},{5,6},{6,7},{7,4},{8,9},{9,10},{10,1... | collective-permute-start | bytes 2359304 | tf_op jit(solution)/shard_map/ppermute | solution.py:275
  170.9 0.0 collective-permute-done.8
  170.9 0.0 copy-done.7
  170.9 0.3 add_convert_fusion
  171.2 4.4 %collective-permute-start.9 = (bf16[192,2048]{1,0:T(8,128)(2,1)S(1)}, bf16[192,2048]{1,0:T(8,128)(2,1)S(1)}, u32[]{:S(2)}, u32[]{:S(2)}) collective-permute-start(bf16[192,2048]{1,0:T(8,128)(2,1)S(1)} %add_convert_fusion), channel_id=1, source_target_pairs={{0,3},{1,0},{2,1},{3,2},{4,7},{5,4},{6,5},{7,6},{8,11},{9,8},{10,9... | collective-permute-start | bytes 2359304 | tf_op jit(solution)/shard_map/ppermute | solution.py:275
  175.6 8.1 %collective-permute-done.10.plain_p = bf16[192,2048]{1,0:T(8,128)(2,1)S(1)} collective-permute-done((bf16[192,2048]{1,0:T(8,128)(2,1)}, bf16[192,2048]{1,0:T(8,128)(2,1)S(1)}, u32[]{:S(2)}, u32[]{:S(2)}) %collective-permute-start.10) | collective-permute-done | bytes 786464 | tf_op jit(solution)/shard_map/ppermute | solution.py:275
  183.7 3.3 %collective-permute-done.11.plain_m = bf16[192,2048]{1,0:T(8,128)(2,1)S(1)} collective-permute-done((bf16[192,2048]{1,0:T(8,128)(2,1)}, bf16[192,2048]{1,0:T(8,128)(2,1)S(1)}, u32[]{:S(2)}, u32[]{:S(2)}) %collective-permute-start.11) | collective-permute-done | bytes 786464 | tf_op jit(solution)/shard_map/ppermute | solution.py:275
  187.1 18.5 %collective-permute-done.7.last_p = bf16[192,2048]{1,0:T(8,128)(2,1)S(1)} collective-permute-done((bf16[192,2048]{1,0:T(8,128)(2,1)S(1)}, bf16[192,2048]{1,0:T(8,128)(2,1)S(1)}, u32[]{:S(2)}, u32[]{:S(2)}) %collective-permute-start.7) | collective-permute-done | bytes 786464 | tf_op jit(solution)/shard_map/ppermute | solution.py:275
  205.6 3.0 %collective-permute-done.9.last_m = bf16[192,2048]{1,0:T(8,128)(2,1)S(1)} collective-permute-done((bf16[192,2048]{1,0:T(8,128)(2,1)S(1)}, bf16[192,2048]{1,0:T(8,128)(2,1)S(1)}, u32[]{:S(2)}, u32[]{:S(2)}) %collective-permute-start.9) | collective-permute-done | bytes 786464 | tf_op jit(solution)/shard_map/ppermute | solution.py:275
  208.6 0.0 copy-done
  208.6 1.6 grads.1
  210.2 8.8 %all-to-all-done.1 = bf16[512,8,128]{2,1,0:T(8,128)(2,1)S(1)} async-done(((bf16[512,8,128]{2,1,0:T(8,128)(2,1)}), bf16[512,8,128]{2,1,0:T(8,128)(2,1)S(1)}, u32[]{:S(2)}, u32[]{:S(2)}) %all-to-all-start.1) | async-done | bytes 1048608 | tf_op jit(solution)/shard_map/all_to_all | solution.py:279
  219.0 1.5 combine.1
Async XLA Ops:
  4.0 24.3 %copy-start.1 = (bf16[1,192,2048]{2,1,0:T(8,128)(2,1)S(1)}, bf16[1,192,2048]{2,1,0:T(8,128)(2,1)}, u32[]{:S(2)}) copy-start(bf16[1,192,2048]{2,1,0:T(8,128)(2,1)} %param.10) | copy-start | bytes 2359300
  4.0 127.6 %all-to-all-start = ((bf16[512,8,256]{2,1,0:T(8,128)(2,1)}), bf16[512,8,256]{2,1,0:T(8,128)(2,1)S(1)}, u32[]{:S(2)}, u32[]{:S(2)}) async-start(bf16[512,8,256]{2,1,0:T(8,128)(2,1)} %bitcast.13), calls=%async_computation | async-start | bytes 4194304 | tf_op jit(solution)/shard_map/all_to_all | solution.py:279
  28.3 25.5 %collective-permute-start.2 = (bf16[192,2048]{1,0:T(8,128)(2,1)S(1)}, bf16[192,2048]{1,0:T(8,128)(2,1)S(1)}, u32[]{:S(2)}, u32[]{:S(2)}) collective-permute-start(bf16[192,2048]{1,0:T(8,128)(2,1)S(1)} %bitcast.15), channel_id=1, source_target_pairs={{0,2},{1,3},{2,0},{3,1},{4,6},{5,7},{6,4},{7,5},{8,10},{9,11},{10,... | collective-permute-start | bytes 2359304 | tf_op jit(solution)/shard_map/ppermute | solution.py:275
  33.1 49.9 %collective-permute-start.1 = (bf16[192,2048]{1,0:T(8,128)(2,1)S(1)}, bf16[192,2048]{1,0:T(8,128)(2,1)S(1)}, u32[]{:S(2)}, u32[]{:S(2)}) collective-permute-start(bf16[192,2048]{1,0:T(8,128)(2,1)S(1)} %bitcast.16), channel_id=1, source_target_pairs={{0,1},{1,2},{2,3},{3,0},{4,5},{5,6},{6,7},{7,4},{8,9},{9,10},{10,1... | collective-permute-start | bytes 2359304 | tf_op jit(solution)/shard_map/ppermute | solution.py:275
  35.3 47.7 %collective-permute-start = (bf16[192,2048]{1,0:T(8,128)(2,1)S(1)}, bf16[192,2048]{1,0:T(8,128)(2,1)S(1)}, u32[]{:S(2)}, u32[]{:S(2)}) collective-permute-start(bf16[192,2048]{1,0:T(8,128)(2,1)S(1)} %bitcast.17), channel_id=1, source_target_pairs={{0,3},{1,0},{2,1},{3,2},{4,7},{5,4},{6,5},{7,6},{8,11},{9,8},{10,9... | collective-permute-start | bytes 2359304 | tf_op jit(solution)/shard_map/ppermute | solution.py:275
  39.6 58.6 %collective-permute-start.5 = (bf16[192,2048]{1,0:T(8,128)(2,1)}, bf16[192,2048]{1,0:T(8,128)(2,1)S(1)}, u32[]{:S(2)}, u32[]{:S(2)}) collective-permute-start(bf16[192,2048]{1,0:T(8,128)(2,1)} %bitcast.18), channel_id=1, source_target_pairs={{0,2},{1,3},{2,0},{3,1},{4,6},{5,7},{6,4},{7,5},{8,10},{9,11},{10,... | collective-permute-start | bytes 2359304 | tf_op jit(solution)/shard_map/ppermute | solution.py:275
  41.6 80.3 %collective-permute-start.4 = (bf16[192,2048]{1,0:T(8,128)(2,1)}, bf16[192,2048]{1,0:T(8,128)(2,1)S(1)}, u32[]{:S(2)}, u32[]{:S(2)}) collective-permute-start(bf16[192,2048]{1,0:T(8,128)(2,1)} %bitcast.19), channel_id=1, source_target_pairs={{0,1},{1,2},{2,3},{3,0},{4,5},{5,6},{6,7},{7,4},{8,9},{9,10},{10,1... | collective-permute-start | bytes 2359304 | tf_op jit(solution)/shard_map/ppermute | solution.py:275
  53.8 68.1 %copy-start.2 = (bf16[192,2048]{1,0:T(8,128)(2,1)}, bf16[192,2048]{1,0:T(8,128)(2,1)S(1)}, u32[]{:S(2)}) copy-start(bf16[192,2048]{1,0:T(8,128)(2,1)S(1)} %collective-permute-done.2.u3) | copy-start | bytes 2359300
  53.8 69.1 %collective-permute-start.3 = (bf16[192,2048]{1,0:T(8,128)(2,1)}, bf16[192,2048]{1,0:T(8,128)(2,1)}, u32[]{:S(2)}, u32[]{:S(2)}) collective-permute-start(bf16[192,2048]{1,0:T(8,128)(2,1)} %bitcast.20), channel_id=1, source_target_pairs={{0,3},{1,0},{2,1},{3,2},{4,7},{5,4},{6,5},{7,6},{8,11},{9,8},{10,9... | collective-permute-start | bytes 2359304 | tf_op jit(solution)/shard_map/ppermute | solution.py:275
  83.1 38.8 %copy-start.3 = (bf16[192,2048]{1,0:T(8,128)(2,1)}, bf16[192,2048]{1,0:T(8,128)(2,1)S(1)}, u32[]{:S(2)}) copy-start(bf16[192,2048]{1,0:T(8,128)(2,1)S(1)} %collective-permute-done.1.u2) | copy-start | bytes 2359300
  83.1 38.8 %copy-start.4 = (bf16[192,2048]{1,0:T(8,128)(2,1)}, bf16[192,2048]{1,0:T(8,128)(2,1)S(1)}, u32[]{:S(2)}) copy-start(bf16[192,2048]{1,0:T(8,128)(2,1)S(1)} %collective-permute-done.u1) | copy-start | bytes 2359300
  98.3 23.6 %copy-start.5 = (bf16[192,2048]{1,0:T(8,128)(2,1)}, bf16[192,2048]{1,0:T(8,128)(2,1)S(1)}, u32[]{:S(2)}) copy-start(bf16[192,2048]{1,0:T(8,128)(2,1)S(1)} %collective-permute-done.5.d3) | copy-start | bytes 2359300
  121.9 0.9 copy-start.6
  140.4 26.8 %collective-permute-start.6 = (bf16[192,2048]{1,0:T(8,128)(2,1)}, bf16[192,2048]{1,0:T(8,128)(2,1)}, u32[]{:S(2)}, u32[]{:S(2)}) collective-permute-start(bf16[192,2048]{1,0:T(8,128)(2,1)} %get-tuple-element.22), channel_id=1, source_target_pairs={{0,1},{1,2},{2,3},{3,0},{4,5},{5,6},{6,7},{7,4},{8,9},{9,10},{10,1... | collective-permute-start | bytes 2359304 | tf_op jit(solution)/shard_map/ppermute | solution.py:275
  142.4 28.5 %collective-permute-start.8 = (bf16[192,2048]{1,0:T(8,128)(2,1)}, bf16[192,2048]{1,0:T(8,128)(2,1)S(1)}, u32[]{:S(2)}, u32[]{:S(2)}) collective-permute-start(bf16[192,2048]{1,0:T(8,128)(2,1)} %get-tuple-element.24), channel_id=1, source_target_pairs={{0,3},{1,0},{2,1},{3,2},{4,7},{5,4},{6,5},{7,6},{8,11},{9,8},{10,9... | collective-permute-start | bytes 2359304 | tf_op jit(solution)/shard_map/ppermute | solution.py:275
  149.3 17.9 %copy-start.8 = (bf16[192,2048]{1,0:T(8,128)(2,1)S(1)}, bf16[192,2048]{1,0:T(8,128)(2,1)}, u32[]{:S(2)}) copy-start(bf16[192,2048]{1,0:T(8,128)(2,1)} %get-tuple-element.21) | copy-start | bytes 2359300
  149.3 69.6 %all-to-all-start.1 = ((bf16[512,8,128]{2,1,0:T(8,128)(2,1)}), bf16[512,8,128]{2,1,0:T(8,128)(2,1)S(1)}, u32[]{:S(2)}, u32[]{:S(2)}) async-start(bf16[512,8,128]{2,1,0:T(8,128)(2,1)} %bitcast.12), calls=%async_computation.1 | async-start | bytes 2097152 | tf_op jit(solution)/shard_map/all_to_all | solution.py:279
  160.6 10.3 %copy-start.7 = (bf16[192,2048]{1,0:T(8,128)(2,1)S(1)}, bf16[192,2048]{1,0:T(8,128)(2,1)}, u32[]{:S(2)}) copy-start(bf16[192,2048]{1,0:T(8,128)(2,1)} %get-tuple-element.23) | copy-start | bytes 2359300
  160.6 23.2 %collective-permute-start.10 = (bf16[192,2048]{1,0:T(8,128)(2,1)}, bf16[192,2048]{1,0:T(8,128)(2,1)S(1)}, u32[]{:S(2)}, u32[]{:S(2)}) collective-permute-start(bf16[192,2048]{1,0:T(8,128)(2,1)} %get-tuple-element.25), channel_id=1, source_target_pairs={{0,1},{1,2},{2,3},{3,0},{4,5},{5,6},{6,7},{7,4},{8,9},{9,10},{10,1... | collective-permute-start | bytes 2359304 | tf_op jit(solution)/shard_map/ppermute | solution.py:275
  164.0 23.0 %collective-permute-start.11 = (bf16[192,2048]{1,0:T(8,128)(2,1)}, bf16[192,2048]{1,0:T(8,128)(2,1)S(1)}, u32[]{:S(2)}, u32[]{:S(2)}) collective-permute-start(bf16[192,2048]{1,0:T(8,128)(2,1)} %get-tuple-element.26), channel_id=1, source_target_pairs={{0,3},{1,0},{2,1},{3,2},{4,7},{5,4},{6,5},{7,6},{8,11},{9,8},{10,9... | collective-permute-start | bytes 2359304 | tf_op jit(solution)/shard_map/ppermute | solution.py:275
  168.6 39.9 %copy-start = (bf16[384,2048]{1,0:T(8,128)(2,1)S(1)}, bf16[384,2048]{1,0:T(8,128)(2,1)}, u32[]{:S(2)}) copy-start(bf16[384,2048]{1,0:T(8,128)(2,1)} %get-tuple-element.20.own) | copy-start | bytes 4718596
  168.6 37.0 %collective-permute-start.7 = (bf16[192,2048]{1,0:T(8,128)(2,1)S(1)}, bf16[192,2048]{1,0:T(8,128)(2,1)S(1)}, u32[]{:S(2)}, u32[]{:S(2)}) collective-permute-start(bf16[192,2048]{1,0:T(8,128)(2,1)S(1)} %add_convert_fusion.1), channel_id=1, source_target_pairs={{0,1},{1,2},{2,3},{3,0},{4,5},{5,6},{6,7},{7,4},{8,9},{9,10},{10,1... | collective-permute-start | bytes 2359304 | tf_op jit(solution)/shard_map/ppermute | solution.py:275
  171.2 37.4 %collective-permute-start.9 = (bf16[192,2048]{1,0:T(8,128)(2,1)S(1)}, bf16[192,2048]{1,0:T(8,128)(2,1)S(1)}, u32[]{:S(2)}, u32[]{:S(2)}) collective-permute-start(bf16[192,2048]{1,0:T(8,128)(2,1)S(1)} %add_convert_fusion), channel_id=1, source_target_pairs={{0,3},{1,0},{2,1},{3,2},{4,7},{5,4},{6,5},{7,6},{8,11},{9,8},{10,9... | collective-permute-start | bytes 2359304 | tf_op jit(solution)/shard_map/ppermute | solution.py:275

commit v5 on v4

--- a/solution.py
+++ b/solution.py
@@ -69,8 +69,9 @@
 
 
 def dispatch_kernel(
-    routes_hbm, gates_hbm, in_hbm_ref, out_hbm_ref, send_hbm, chosen_ref,
-    routes_ref, gates_ref, in_ref, out_ref, send_ref, nat_in, nat_grad, sems, in_sems,
+    routes_hbm, gates_hbm, in_hbm_ref, out_hbm_ref, send_hbm, chosen_hbm,
+    routes_ref, gates_ref, in_ref, out_ref, send_ref, chosen_ref, nat_in, nat_grad, sems, in_sems,
+    chosen_sem,
 ):
     loads = [
         pltpu.make_async_copy(src, dst, in_sems.at[i])
@@ -106,6 +107,8 @@
     slot_gates = jnp.sum((chosen * gates[:, None, :]).reshape(slot_rows, tokens), axis=1, keepdims=True)
     chosen = chosen.reshape(slot_rows, tokens).astype(BF16)
     chosen_ref[...] = chosen
+    save = pltpu.make_async_copy(chosen_ref, chosen_hbm, chosen_sem)
+    save.start()
     for load in loads[2:]:
         load.wait()
     nat_in[...] = jnp.dot(chosen, in_ref[...], preferred_element_type=F32).astype(BF16)
@@ -118,12 +121,13 @@
         send_ref[blk * BLOCK : blk * BLOCK + BLOCK, :] = pick(order, jnp.concatenate(parts, axis=0))
         drain(send_ref, send_hbm, sems, blk)
     finish(send_ref, send_hbm, sems)
+    save.wait()
 
 
 def expert_kernel(
     recv_ref, u0, u1, u2, u3, d0, d1, d2, d3,
-    d_pre_ref, up, own_out, first_p, first_m, plain_p, plain_m, held_p, held_m,
-    down, in_rows, grad_rows, own_s, fp_s, fm_s, pp_s, pm_s, hp_s, hm_s, sems, out_sems,
+    d_pre_ref, up, hidden_hbm, d_pre_hbm, in_hbm_ref, grad_hbm_ref, first_p, first_m,
+    down, hidden_ref, in_rows, grad_rows, fp_s, fm_s, sems, out_sems,
 ):
     part = u0.shape[0]
     half = part // 2
@@ -142,6 +146,14 @@
                 rows[blk * 16 : blk * 16 + 16, g * BLOCK : g * BLOCK + BLOCK] = moved[
                     (2 * g + a) * 16 : (2 * g + a) * 16 + 16, :
                 ]
+    outs = []
+
+    def save(src, dst):
+        outs.append(pltpu.make_async_copy(src, dst, out_sems.at[len(outs)]))
+        outs[-1].start()
+
+    save(in_rows, in_hbm_ref)
+    save(grad_rows, grad_hbm_ref)
     for copy in copies[:4]:
         copy.wait()
     pre = lax.dot_general(up[...], in_rows[...], CONTRACT_LAST, preferred_element_type=F32)
@@ -152,45 +164,71 @@
     hidden = (pre * sigma).astype(BF16)
     d_pre = (back * sigma * (1.0 + pre * (1.0 - sigma))).astype(BF16)
     d_pre_ref[...] = d_pre
-
+    hidden_ref[...] = hidden
+    save(d_pre_ref, d_pre_hbm)
+    save(hidden_ref, hidden_hbm)
+    top = 3 * part
+    for w, (left, rows) in enumerate(((d_pre, in_rows), (hidden, grad_rows))):
+        one = slice(w * half, w * half + half)
+        for lanes in lane_steps(rows.shape[1]):
+            total = part_grad(left[top:], rows, lanes)
+            fp_s[one, lanes] = total[:half]
+            fm_s[one, lanes] = total[half:]
+    save(fp_s, first_p)
+    save(fm_s, first_m)
+    for copy in outs:
+        copy.wait()
+
+
+def lane_steps(width, step=512):
+    return [slice(n, n + step) for n in range(0, width, step)]
+
+
+def part_grad(left, rows, lanes):
+    return jnp.dot(left, rows[:, lanes], preferred_element_type=F32).astype(BF16)
+
+
+def rest_kernel(
+    d_pre_hbm, hidden_hbm, in_hbm_ref, grad_hbm_ref,
+    plain_p, plain_m, held_p, held_m, own_out,
+    d_pre_ref, hidden_ref, in_rows, grad_rows, pp_s, pm_s, hp_s, hm_s, own_s, sems, in_sems,
+):
+    pairs = (
+        (d_pre_hbm, d_pre_ref), (in_hbm_ref, in_rows), (hidden_hbm, hidden_ref), (grad_hbm_ref, grad_rows),
+    )
+    loads = [pltpu.make_async_copy(src, dst, in_sems.at[i]) for i, (src, dst) in enumerate(pairs)]
+    for load in loads:
+        load.start()
+    for load in loads:
+        load.wait()
+    part = plain_p.shape[0]
+    half = part // 2
     outs = []
 
-    def send(i, src, dst):
-        outs.append(pltpu.make_async_copy(src, dst, out_sems.at[i]))
+    def send(src, dst):
+        outs.append(pltpu.make_async_copy(src, dst, sems.at[len(outs)]))
         outs[-1].start()
 
-    width = in_rows.shape[1]
-    step = 512
-    for top in (3 * part, 2 * part, part, 0):
-        for w, (left, rows) in enumerate(((d_pre, in_rows), (hidden, grad_rows))):
+    for piece in (1, 2, 0):
+        for w, (left, rows) in enumerate(((d_pre_ref, in_rows), (hidden_ref, grad_rows))):
             one, two = slice(w * half, w * half + half), slice(w * part, w * part + part)
-            for n in range(width // step):
-                lanes = slice(n * step, n * step + step)
-                total = jnp.dot(
-                    left[top : top + part], rows[:, lanes], preferred_element_type=F32
-                ).astype(BF16)
-                if top == 0:
+            mine = left[piece * part : piece * part + part, :]
+            for lanes in lane_steps(rows.shape[1]):
+                total = part_grad(mine, rows, lanes)
+                if piece == 0:
                     own_s[two, lanes] = total
-                elif top == part:
-                    hp_s[one, lanes] = total[:half]
-                    pp_s[one, lanes] = total[half:]
-                elif top == 2 * part:
-                    pm_s[one, lanes] = total[:half]
-                    hm_s[one, lanes] = total[half:]
                 else:
-                    fp_s[one, lanes] = total[:half]
-                    fm_s[one, lanes] = total[half:]
-        if top == 0:
-            send(6, own_s, own_out)
-        elif top == part:
-            send(4, hp_s, held_p)
-            send(2, pp_s, plain_p)
-        elif top == 2 * part:
-            send(3, pm_s, plain_m)
-            send(5, hm_s, held_m)
+                    low, high = ((hp_s, pp_s), (pm_s, hm_s))[piece - 1]
+                    low[one, lanes] = total[:half]
+                    high[one, lanes] = total[half:]
+        if piece == 0:
+            send(own_s, own_out)
+        elif piece == 1:
+            send(pp_s, plain_p)
+            send(hp_s, held_p)
         else:
-            send(0, fp_s, first_p)
-            send(1, fm_s, first_m)
+            send(pm_s, plain_m)
+            send(hm_s, held_m)
     for copy in outs:
         copy.wait()
 
@@ -207,12 +245,15 @@
     finish(ret_ref, ret_hbm, sems)
 
 
-def combine_kernel(recv_ref, chosen_ref, out_ref, rows):
+def combine_kernel(recv_ref, chosen_hbm, out_ref, rows, chosen_ref, sem):
+    load = pltpu.make_async_copy(chosen_hbm, chosen_ref, sem)
+    load.start()
     order = row_permutation(final_source)
     for blk in range(recv_ref.shape[0] // BLOCK):
         moved = pick(order, recv_ref[blk * BLOCK : blk * BLOCK + BLOCK, :])
         for f in range(4):
             rows[blk * 64 : blk * 64 + 64, f * 128 : f * 128 + 128] = moved[f * 64 : f * 64 + 64, :]
+    load.wait()
     total = lax.dot_general(
         chosen_ref[...], rows[...], CONTRACT_FIRST, preferred_element_type=F32
     )
@@ -287,18 +328,20 @@
     send, chosen = pl.pallas_call(
         dispatch_kernel,
         in_specs=[hbm] * 4,
-        out_specs=(hbm, vmem),
-        out_shape=(in_hbm((send_rows, BLOCK)), on_chip((slot_rows, token_count))),
+        out_specs=(hbm, hbm),
+        out_shape=(in_hbm((send_rows, BLOCK)), in_hbm((slot_rows, token_count))),
         scratch_shapes=[
             pltpu.VMEM((route_count, token_count), I32),
             pltpu.VMEM((route_count, token_count), F32),
             pltpu.VMEM((token_count, part), BF16),
             pltpu.VMEM((token_count, part), BF16),
             pltpu.VMEM((send_rows, BLOCK), BF16),
+            pltpu.VMEM((slot_rows, token_count), BF16),
             pltpu.VMEM((slot_rows, part), BF16),
             pltpu.VMEM((slot_rows, part), BF16),
             pltpu.SemaphoreType.DMA((CHUNKS,)),
             pltpu.SemaphoreType.DMA((4,)),
+            pltpu.SemaphoreType.DMA(()),
         ],
         compiler_params=PARAMS,
         name="dispatch",
@@ -312,17 +355,19 @@
 
     piece = (hidden_part, width)
     whole = (2 * hidden_part, width)
-    d_pre, up_full, own, first_p, first_m, plain_p, plain_m, held_p, held_m = pl.pallas_call(
+    rows_shape, hidden_shape = (row_count, width), (hidden, row_count)
+    d_pre, up_full, hidden_t, d_pre_t, in_rows, grad_rows, first_p, first_m = pl.pallas_call(
         expert_kernel,
         in_specs=[vmem] + [hbm] * 8,
-        out_specs=(vmem,) * 2 + (hbm,) * 7,
-        out_shape=(on_chip((hidden, row_count)), on_chip((hidden, width)), in_hbm(whole))
-        + (in_hbm(piece),) * 6,
-        scratch_shapes=[pltpu.VMEM((hidden, width), BF16)]
-        + [pltpu.VMEM((row_count, width), BF16)] * 2
-        + [pltpu.VMEM(whole, BF16)]
-        + [pltpu.VMEM(piece, BF16)] * 6
-        + [pltpu.SemaphoreType.DMA((8,)), pltpu.SemaphoreType.DMA((7,))],
+        out_specs=(vmem,) * 2 + (hbm,) * 6,
+        out_shape=(on_chip(hidden_shape), on_chip((hidden, width)))
+        + (in_hbm(hidden_shape),) * 2
+        + (in_hbm(rows_shape),) * 2
+        + (in_hbm(piece),) * 2,
+        scratch_shapes=[pltpu.VMEM((hidden, width), BF16), pltpu.VMEM(hidden_shape, BF16)]
+        + [pltpu.VMEM(rows_shape, BF16)] * 2
+        + [pltpu.VMEM(piece, BF16)] * 2
+        + [pltpu.SemaphoreType.DMA((8,)), pltpu.SemaphoreType.DMA((6,))],
         compiler_params=PARAMS,
         name="expert",
     )(keep(recv), *weights)
@@ -337,6 +382,22 @@
         name="rows_back",
     )(keep(d_pre), keep(up_full))
     returned = swap(ret)
+    plain_p, plain_m, held_p, held_m, own = pl.pallas_call(
+        rest_kernel,
+        in_specs=[hbm] * 4,
+        out_specs=(hbm,) * 5,
+        out_shape=(in_hbm(piece),) * 4 + (in_hbm(whole),),
+        scratch_shapes=[pltpu.VMEM(hidden_shape, BF16)] * 2
+        + [pltpu.VMEM(rows_shape, BF16)] * 2
+        + [pltpu.VMEM(piece, BF16)] * 4
+        + [
+            pltpu.VMEM(whole, BF16),
+            pltpu.SemaphoreType.DMA((5,)),
+            pltpu.SemaphoreType.DMA((4,)),
+        ],
+        compiler_params=PARAMS,
+        name="rest",
+    )(*[leave(value) for value in (d_pre_t, hidden_t, in_rows, grad_rows)])
     plain_p, plain_m = shift(plain_p, 1), shift(plain_m, -1)
     last_p = shift((held_p.astype(F32) + got_p.astype(F32)).astype(BF16), 1)
     last_m = shift((held_m.astype(F32) + got_m.astype(F32)).astype(BF16), -1)
@@ -351,10 +412,15 @@
     in_grad = pl.pallas_call(
         combine_kernel,
         out_shape=shape((token_count, part)),
-        scratch_shapes=[pltpu.VMEM((slot_rows, part), BF16)],
+        in_specs=[vmem, hbm],
+        scratch_shapes=[
+            pltpu.VMEM((slot_rows, part), BF16),
+            pltpu.VMEM((slot_rows, token_count), BF16),
+            pltpu.SemaphoreType.DMA(()),
+        ],
         compiler_params=PARAMS,
         name="combine",
-    )(keep(returned), keep(chosen))
+    )(keep(returned), leave(chosen))
     return (in_grad, grad_up[None], grad_down[None])
 
 

time: 221 us -> 221 us (level)
  waiting for transfers between devices: 121 us -> 116 us
  Pallas kernels: 17.7 us -> 22.2 us
    pallas_call x2 -> x3, Pallas kernels: 4.89 us -> 10.4 us  [the longest x1 4.64 us: local(): pl.pallas_call(rest_kernel, in_specs=[hbm] * 4, out_specs=(hbm,) * 5, out...]
    all_to_all x2, waiting for transfers between devices: 17.5 us -> 12.9 us  [swap(): lax.all_to_all(values.reshape(peers, 8, lanes), ('expert', 'dp'), split_a...]
  transfers between devices with their start and end apart: 14 -> 14, of which waited for: 10 -> 10; matrix products, arithmetic and copies ran while one was open for 1% -> 1% of each run, Pallas kernels for 2% -> 4%
where the time goes in v5:
time: 221 us; the launch traced here: 220 us
  waiting for transfers between devices  116 us (52%)
  starting transfers between devices  78.6 us (36%)
  Pallas kernels  22.2 us (10%)
    ppermute x12, waiting for transfers between devices, shift(): return lax.ppermute(value, 'dp', pairs)  103 us
    ppermute x12, starting transfers between devices, shift(): return lax.ppermute(value, 'dp', pairs)  43.1 us
    all_to_all x2, starting transfers between devices, swap(): lax.all_to_all(values.reshape(peers, 8, lanes), ('expert', 'dp'), split_a...  35.5 us
    all_to_all x2, waiting for transfers between devices, swap(): lax.all_to_all(values.reshape(peers, 8, lanes), ('expert', 'dp'), split_a...  12.9 us
    pallas_call x1, Pallas kernels, local(): pl.pallas_call(expert_kernel, in_specs=[vmem] + [hbm] * 8, out_specs=(vme...  7.79 us
    pallas_call x1, Pallas kernels, local(): pl.pallas_call(rest_kernel, in_specs=[hbm] * 4, out_specs=(hbm,) * 5, out...  4.64 us
  transfers between devices with their start and end apart: 14, of which 10 were waited for; matrix products, arithmetic and copies ran while one was open for 1% of the time, Pallas kernels for 4%

profile of v5, /device:TPU:1, one launch (start us, length us, event | category | flops | bytes accessed | tf_op | source)
XLA Modules:
  0.0 220.5 jit_solution(15755135269575414169)
XLA Ops:
  0.6 3.4 %dispatch.1 = (bf16[4096,256]{1,0:T(8,128)(2,1)}, bf16[1024,128]{1,0:T(8,128)(2,1)}) custom-call(s32[4,128]{1,0:T(4,128)} %bitcast.22, f32[4,128]{1,0:T(4,128)} %bitcast.23, bf16[128,512]{1,0:T(8,128)(2,1)} %in_hbm_ref.1, bf16[128,512]{1,0:T(8,128)(2,1)} %out_hbm_ref.1), custom_call_target="tpu_custom_call" | custom-call | tf_op jit(solution)/shard_map/dispatch/pallas_call | solution.py:328
  4.0 0.0 copy-start.1
  4.0 24.3 %all-to-all-start = ((bf16[512,8,256]{2,1,0:T(8,128)(2,1)}), bf16[512,8,256]{2,1,0:T(8,128)(2,1)S(1)}, u32[]{:S(2)}, u32[]{:S(2)}) async-start(bf16[512,8,256]{2,1,0:T(8,128)(2,1)} %bitcast.13), calls=%async_computation | async-start | bytes 4194304 | tf_op jit(solution)/shard_map/all_to_all | solution.py:320
  28.4 0.0 copy-done.1
  28.4 4.8 %collective-permute-start.2 = (bf16[192,2048]{1,0:T(8,128)(2,1)S(1)}, bf16[192,2048]{1,0:T(8,128)(2,1)S(1)}, u32[]{:S(2)}, u32[]{:S(2)}) collective-permute-start(bf16[192,2048]{1,0:T(8,128)(2,1)S(1)} %bitcast.15), channel_id=1, source_target_pairs={{0,2},{1,3},{2,0},{3,1},{4,6},{5,7},{6,4},{7,5},{8,10},{9,11},{10,... | collective-permute-start | bytes 2359304 | tf_op jit(solution)/shard_map/ppermute | solution.py:316
  33.2 2.2 collective-permute-start.1
  35.4 4.3 %collective-permute-start = (bf16[192,2048]{1,0:T(8,128)(2,1)S(1)}, bf16[192,2048]{1,0:T(8,128)(2,1)S(1)}, u32[]{:S(2)}, u32[]{:S(2)}) collective-permute-start(bf16[192,2048]{1,0:T(8,128)(2,1)S(1)} %bitcast.17), channel_id=1, source_target_pairs={{0,3},{1,0},{2,1},{3,2},{4,7},{5,4},{6,5},{7,6},{8,11},{9,8},{10,9... | collective-permute-start | bytes 2359304 | tf_op jit(solution)/shard_map/ppermute | solution.py:316
  39.7 1.9 collective-permute-start.5
  41.6 2.5 %collective-permute-start.4 = (bf16[192,2048]{1,0:T(8,128)(2,1)}, bf16[192,2048]{1,0:T(8,128)(2,1)S(1)}, u32[]{:S(2)}, u32[]{:S(2)}) collective-permute-start(bf16[192,2048]{1,0:T(8,128)(2,1)} %bitcast.19), channel_id=1, source_target_pairs={{0,1},{1,2},{2,3},{3,0},{4,5},{5,6},{6,7},{7,4},{8,9},{9,10},{10,1... | collective-permute-start | bytes 2359304 | tf_op jit(solution)/shard_map/ppermute | solution.py:316
  44.1 9.7 %collective-permute-done.2.u3 = bf16[192,2048]{1,0:T(8,128)(2,1)S(1)} collective-permute-done((bf16[192,2048]{1,0:T(8,128)(2,1)S(1)}, bf16[192,2048]{1,0:T(8,128)(2,1)S(1)}, u32[]{:S(2)}, u32[]{:S(2)}) %collective-permute-start.2) | collective-permute-done | bytes 786464 | tf_op jit(solution)/shard_map/ppermute | solution.py:316
  53.8 0.0 copy-start.2
  53.8 7.6 %collective-permute-start.3 = (bf16[192,2048]{1,0:T(8,128)(2,1)}, bf16[192,2048]{1,0:T(8,128)(2,1)}, u32[]{:S(2)}, u32[]{:S(2)}) collective-permute-start(bf16[192,2048]{1,0:T(8,128)(2,1)} %bitcast.20), channel_id=1, source_target_pairs={{0,3},{1,0},{2,1},{3,2},{4,7},{5,4},{6,5},{7,6},{8,11},{9,8},{10,9... | collective-permute-start | bytes 2359304 | tf_op jit(solution)/shard_map/ppermute | solution.py:316
  61.5 21.6 %collective-permute-done.1.u2 = bf16[192,2048]{1,0:T(8,128)(2,1)S(1)} collective-permute-done((bf16[192,2048]{1,0:T(8,128)(2,1)S(1)}, bf16[192,2048]{1,0:T(8,128)(2,1)S(1)}, u32[]{:S(2)}, u32[]{:S(2)}) %collective-permute-start.1) | collective-permute-done | bytes 786464 | tf_op jit(solution)/shard_map/ppermute | solution.py:316
  83.1 0.0 copy-start.3
  83.1 0.0 collective-permute-done.u1
  83.1 0.0 copy-start.4
  83.1 15.2 %collective-permute-done.5.d3 = bf16[192,2048]{1,0:T(8,128)(2,1)S(1)} collective-permute-done((bf16[192,2048]{1,0:T(8,128)(2,1)}, bf16[192,2048]{1,0:T(8,128)(2,1)S(1)}, u32[]{:S(2)}, u32[]{:S(2)}) %collective-permute-start.5) | collective-permute-done | bytes 786464 | tf_op jit(solution)/shard_map/ppermute | solution.py:316
  98.3 0.0 copy-start.5
  98.3 23.6 %collective-permute-done.4.d2 = bf16[192,2048]{1,0:T(8,128)(2,1)S(1)} collective-permute-done((bf16[192,2048]{1,0:T(8,128)(2,1)}, bf16[192,2048]{1,0:T(8,128)(2,1)S(1)}, u32[]{:S(2)}, u32[]{:S(2)}) %collective-permute-start.4) | collective-permute-done | bytes 786464 | tf_op jit(solution)/shard_map/ppermute | solution.py:316
  121.9 0.0 copy-done.2
  121.9 0.0 copy-done.3
  121.9 0.0 copy-done.4
  121.9 0.0 copy-done.5
  122.0 0.0 copy-start.6
  122.0 0.9 copy-done.6
  122.8 0.0 collective-permute-done.3.d1
  122.8 8.8 %all-to-all-done = bf16[512,8,256]{2,1,0:T(8,128)(2,1)S(1)} async-done(((bf16[512,8,256]{2,1,0:T(8,128)(2,1)}), bf16[512,8,256]{2,1,0:T(8,128)(2,1)S(1)}, u32[]{:S(2)}, u32[]{:S(2)}) %all-to-all-start) | async-done | bytes 2097184 | tf_op jit(solution)/shard_map/all_to_all | solution.py:320
  131.6 7.8 %expert.1 = (bf16[768,256]{1,0:T(8,128)(2,1)S(1)}, bf16[768,2048]{1,0:T(8,128)(2,1)S(1)}, bf16[768,256]{1,0:T(8,128)(2,1)}, bf16[768,256]{1,0:T(8,128)(2,1)}, bf...) custom-call(bf16[4096,256]{1,0:T(8,128)(2,1)S(1)} %bitcast.10, ...), custom_call_target="tpu_custom_call" | custom-call | tf_op jit(solution)/shard_map/expert/pallas_call | solution.py:359
  139.4 1.9 collective-permute-start.6
  141.4 4.6 %collective-permute-start.8 = (bf16[192,2048]{1,0:T(8,128)(2,1)}, bf16[192,2048]{1,0:T(8,128)(2,1)S(1)}, u32[]{:S(2)}, u32[]{:S(2)}) collective-permute-start(bf16[192,2048]{1,0:T(8,128)(2,1)} %get-tuple-element.32), channel_id=1, source_target_pairs={{0,3},{1,0},{2,1},{3,2},{4,7},{5,4},{6,5},{7,6},{8,11},{9,8},{10,9... | collective-permute-start | bytes 2359304 | tf_op jit(solution)/shard_map/ppermute | solution.py:316
  145.9 2.4 %rows_back.1 = bf16[4096,128]{1,0:T(8,128)(2,1)} custom-call(bf16[768,256]{1,0:T(8,128)(2,1)S(1)} %get-tuple-element.21.d_pre_ref, bf16[768,2048]{1,0:T(8,128)(2,1)S(1)} %get-tuple-element.22.up_ref), custom_call_target="tpu_custom_call" | custom-call | tf_op jit(solution)/shard_map/rows_back/pallas_call | solution.py:376
  148.3 11.2 %all-to-all-start.1 = ((bf16[512,8,128]{2,1,0:T(8,128)(2,1)}), bf16[512,8,128]{2,1,0:T(8,128)(2,1)S(1)}, u32[]{:S(2)}, u32[]{:S(2)}) async-start(bf16[512,8,128]{2,1,0:T(8,128)(2,1)} %bitcast.12), calls=%async_computation.1 | async-start | bytes 2097152 | tf_op jit(solution)/shard_map/all_to_all | solution.py:320
  159.5 4.6 %rest.1 = (bf16[192,2048]{1,0:T(8,128)(2,1)}, bf16[192,2048]{1,0:T(8,128)(2,1)}, bf16[192,2048]{1,0:T(8,128)(2,1)}, bf16[192,2048]{1,0:T(8,128)(2,1)}, bf16[384,2048]{1,0:T(8,128)(2,1)}) custom-call(bf16[768,256]{1,0:T(8,128)(2,1)} %get-tuple-element.24.d_pre_hbm, bf16[768,256]{1,0:T(8,128)(2,1)} %get-tuple-element.25.hidden_hbm, ...), custom_call_target="tpu_custom_call" | custom-call | tf_op jit(solution)/shard_map/rest/pallas_call | solution.py:385
  164.1 0.0 copy-start.7
  164.2 3.4 %collective-permute-start.10 = (bf16[192,2048]{1,0:T(8,128)(2,1)}, bf16[192,2048]{1,0:T(8,128)(2,1)S(1)}, u32[]{:S(2)}, u32[]{:S(2)}) collective-permute-start(bf16[192,2048]{1,0:T(8,128)(2,1)} %get-tuple-element.33), channel_id=1, source_target_pairs={{0,1},{1,2},{2,3},{3,0},{4,5},{5,6},{6,7},{7,4},{8,9},{9,10},{10,1... | collective-permute-start | bytes 2359304 | tf_op jit(solution)/shard_map/ppermute | solution.py:316
  167.6 3.2 %collective-permute-start.11 = (bf16[192,2048]{1,0:T(8,128)(2,1)}, bf16[192,2048]{1,0:T(8,128)(2,1)S(1)}, u32[]{:S(2)}, u32[]{:S(2)}) collective-permute-start(bf16[192,2048]{1,0:T(8,128)(2,1)} %get-tuple-element.34), channel_id=1, source_target_pairs={{0,3},{1,0},{2,1},{3,2},{4,7},{5,4},{6,5},{7,6},{8,11},{9,8},{10,9... | collective-permute-start | bytes 2359304 | tf_op jit(solution)/shard_map/ppermute | solution.py:316
  170.8 0.0 collective-permute-done.6
  170.8 1.4 add_convert_fusion.1
  172.2 0.0 copy-start
  172.2 2.2 %collective-permute-start.7 = (bf16[192,2048]{1,0:T(8,128)(2,1)S(1)}, bf16[192,2048]{1,0:T(8,128)(2,1)S(1)}, u32[]{:S(2)}, u32[]{:S(2)}) collective-permute-start(bf16[192,2048]{1,0:T(8,128)(2,1)S(1)} %add_convert_fusion.1), channel_id=1, source_target_pairs={{0,1},{1,2},{2,3},{3,0},{4,5},{5,6},{6,7},{7,4},{8,9},{9,10},{10,1... | collective-permute-start | bytes 2359304 | tf_op jit(solution)/shard_map/ppermute | solution.py:316
  174.4 0.0 collective-permute-done.8
  174.4 0.0 copy-done.7
  174.5 0.3 add_convert_fusion
  174.7 4.4 %collective-permute-start.9 = (bf16[192,2048]{1,0:T(8,128)(2,1)S(1)}, bf16[192,2048]{1,0:T(8,128)(2,1)S(1)}, u32[]{:S(2)}, u32[]{:S(2)}) collective-permute-start(bf16[192,2048]{1,0:T(8,128)(2,1)S(1)} %add_convert_fusion), channel_id=1, source_target_pairs={{0,3},{1,0},{2,1},{3,2},{4,7},{5,4},{6,5},{7,6},{8,11},{9,8},{10,9... | collective-permute-start | bytes 2359304 | tf_op jit(solution)/shard_map/ppermute | solution.py:316
  179.1 8.1 %collective-permute-done.10.plain_p = bf16[192,2048]{1,0:T(8,128)(2,1)S(1)} collective-permute-done((bf16[192,2048]{1,0:T(8,128)(2,1)}, bf16[192,2048]{1,0:T(8,128)(2,1)S(1)}, u32[]{:S(2)}, u32[]{:S(2)}) %collective-permute-start.10) | collective-permute-done | bytes 786464 | tf_op jit(solution)/shard_map/ppermute | solution.py:316
  187.3 4.0 %collective-permute-done.11.plain_m = bf16[192,2048]{1,0:T(8,128)(2,1)S(1)} collective-permute-done((bf16[192,2048]{1,0:T(8,128)(2,1)}, bf16[192,2048]{1,0:T(8,128)(2,1)S(1)}, u32[]{:S(2)}, u32[]{:S(2)}) %collective-permute-start.11) | collective-permute-done | bytes 786464 | tf_op jit(solution)/shard_map/ppermute | solution.py:316
  191.3 17.7 %collective-permute-done.7.last_p = bf16[192,2048]{1,0:T(8,128)(2,1)S(1)} collective-permute-done((bf16[192,2048]{1,0:T(8,128)(2,1)S(1)}, bf16[192,2048]{1,0:T(8,128)(2,1)S(1)}, u32[]{:S(2)}, u32[]{:S(2)}) %collective-permute-start.7) | collective-permute-done | bytes 786464 | tf_op jit(solution)/shard_map/ppermute | solution.py:316
  209.0 3.2 %collective-permute-done.9.last_m = bf16[192,2048]{1,0:T(8,128)(2,1)S(1)} collective-permute-done((bf16[192,2048]{1,0:T(8,128)(2,1)S(1)}, bf16[192,2048]{1,0:T(8,128)(2,1)S(1)}, u32[]{:S(2)}, u32[]{:S(2)}) %collective-permute-start.9) | collective-permute-done | bytes 786464 | tf_op jit(solution)/shard_map/ppermute | solution.py:316
  212.1 0.0 copy-done
  212.1 1.6 grads.1
  213.8 4.1 %all-to-all-done.1 = bf16[512,8,128]{2,1,0:T(8,128)(2,1)S(1)} async-done(((bf16[512,8,128]{2,1,0:T(8,128)(2,1)}), bf16[512,8,128]{2,1,0:T(8,128)(2,1)S(1)}, u32[]{:S(2)}, u32[]{:S(2)}) %all-to-all-start.1) | async-done | bytes 1048608 | tf_op jit(solution)/shard_map/all_to_all | solution.py:320
  217.9 2.4 %combine.1 = bf16[128,512]{1,0:T(8,128)(2,1)} custom-call(bf16[4096,128]{1,0:T(8,128)(2,1)S(1)} %bitcast.11, bf16[1024,128]{1,0:T(8,128)(2,1)} %get-tuple-element.23.chosen_hbm), custom_call_target="tpu_custom_call" | custom-call | tf_op jit(solution)/shard_map/combine/pallas_call | solution.py:412
Async XLA Ops:
  4.0 24.3 %copy-start.1 = (bf16[1,192,2048]{2,1,0:T(8,128)(2,1)S(1)}, bf16[1,192,2048]{2,1,0:T(8,128)(2,1)}, u32[]{:S(2)}) copy-start(bf16[1,192,2048]{2,1,0:T(8,128)(2,1)} %param.10) | copy-start | bytes 2359300
  4.0 127.6 %all-to-all-start = ((bf16[512,8,256]{2,1,0:T(8,128)(2,1)}), bf16[512,8,256]{2,1,0:T(8,128)(2,1)S(1)}, u32[]{:S(2)}, u32[]{:S(2)}) async-start(bf16[512,8,256]{2,1,0:T(8,128)(2,1)} %bitcast.13), calls=%async_computation | async-start | bytes 4194304 | tf_op jit(solution)/shard_map/all_to_all | solution.py:320
  28.4 25.5 %collective-permute-start.2 = (bf16[192,2048]{1,0:T(8,128)(2,1)S(1)}, bf16[192,2048]{1,0:T(8,128)(2,1)S(1)}, u32[]{:S(2)}, u32[]{:S(2)}) collective-permute-start(bf16[192,2048]{1,0:T(8,128)(2,1)S(1)} %bitcast.15), channel_id=1, source_target_pairs={{0,2},{1,3},{2,0},{3,1},{4,6},{5,7},{6,4},{7,5},{8,10},{9,11},{10,... | collective-permute-start | bytes 2359304 | tf_op jit(solution)/shard_map/ppermute | solution.py:316
  33.2 49.9 %collective-permute-start.1 = (bf16[192,2048]{1,0:T(8,128)(2,1)S(1)}, bf16[192,2048]{1,0:T(8,128)(2,1)S(1)}, u32[]{:S(2)}, u32[]{:S(2)}) collective-permute-start(bf16[192,2048]{1,0:T(8,128)(2,1)S(1)} %bitcast.16), channel_id=1, source_target_pairs={{0,1},{1,2},{2,3},{3,0},{4,5},{5,6},{6,7},{7,4},{8,9},{9,10},{10,1... | collective-permute-start | bytes 2359304 | tf_op jit(solution)/shard_map/ppermute | solution.py:316
  35.4 47.7 %collective-permute-start = (bf16[192,2048]{1,0:T(8,128)(2,1)S(1)}, bf16[192,2048]{1,0:T(8,128)(2,1)S(1)}, u32[]{:S(2)}, u32[]{:S(2)}) collective-permute-start(bf16[192,2048]{1,0:T(8,128)(2,1)S(1)} %bitcast.17), channel_id=1, source_target_pairs={{0,3},{1,0},{2,1},{3,2},{4,7},{5,4},{6,5},{7,6},{8,11},{9,8},{10,9... | collective-permute-start | bytes 2359304 | tf_op jit(solution)/shard_map/ppermute | solution.py:316
  39.7 58.6 %collective-permute-start.5 = (bf16[192,2048]{1,0:T(8,128)(2,1)}, bf16[192,2048]{1,0:T(8,128)(2,1)S(1)}, u32[]{:S(2)}, u32[]{:S(2)}) collective-permute-start(bf16[192,2048]{1,0:T(8,128)(2,1)} %bitcast.18), channel_id=1, source_target_pairs={{0,2},{1,3},{2,0},{3,1},{4,6},{5,7},{6,4},{7,5},{8,10},{9,11},{10,... | collective-permute-start | bytes 2359304 | tf_op jit(solution)/shard_map/ppermute | solution.py:316
  41.6 80.3 %collective-permute-start.4 = (bf16[192,2048]{1,0:T(8,128)(2,1)}, bf16[192,2048]{1,0:T(8,128)(2,1)S(1)}, u32[]{:S(2)}, u32[]{:S(2)}) collective-permute-start(bf16[192,2048]{1,0:T(8,128)(2,1)} %bitcast.19), channel_id=1, source_target_pairs={{0,1},{1,2},{2,3},{3,0},{4,5},{5,6},{6,7},{7,4},{8,9},{9,10},{10,1... | collective-permute-start | bytes 2359304 | tf_op jit(solution)/shard_map/ppermute | solution.py:316
  53.8 68.1 %copy-start.2 = (bf16[192,2048]{1,0:T(8,128)(2,1)}, bf16[192,2048]{1,0:T(8,128)(2,1)S(1)}, u32[]{:S(2)}) copy-start(bf16[192,2048]{1,0:T(8,128)(2,1)S(1)} %collective-permute-done.2.u3) | copy-start | bytes 2359300
  53.8 69.0 %collective-permute-start.3 = (bf16[192,2048]{1,0:T(8,128)(2,1)}, bf16[192,2048]{1,0:T(8,128)(2,1)}, u32[]{:S(2)}, u32[]{:S(2)}) collective-permute-start(bf16[192,2048]{1,0:T(8,128)(2,1)} %bitcast.20), channel_id=1, source_target_pairs={{0,3},{1,0},{2,1},{3,2},{4,7},{5,4},{6,5},{7,6},{8,11},{9,8},{10,9... | collective-permute-start | bytes 2359304 | tf_op jit(solution)/shard_map/ppermute | solution.py:316
  83.1 38.8 %copy-start.3 = (bf16[192,2048]{1,0:T(8,128)(2,1)}, bf16[192,2048]{1,0:T(8,128)(2,1)S(1)}, u32[]{:S(2)}) copy-start(bf16[192,2048]{1,0:T(8,128)(2,1)S(1)} %collective-permute-done.1.u2) | copy-start | bytes 2359300
  83.1 38.8 %copy-start.4 = (bf16[192,2048]{1,0:T(8,128)(2,1)}, bf16[192,2048]{1,0:T(8,128)(2,1)S(1)}, u32[]{:S(2)}) copy-start(bf16[192,2048]{1,0:T(8,128)(2,1)S(1)} %collective-permute-done.u1) | copy-start | bytes 2359300
  98.3 23.6 %copy-start.5 = (bf16[192,2048]{1,0:T(8,128)(2,1)}, bf16[192,2048]{1,0:T(8,128)(2,1)S(1)}, u32[]{:S(2)}) copy-start(bf16[192,2048]{1,0:T(8,128)(2,1)S(1)} %collective-permute-done.5.d3) | copy-start | bytes 2359300
  122.0 0.9 copy-start.6
  139.4 31.4 %collective-permute-start.6 = (bf16[192,2048]{1,0:T(8,128)(2,1)}, bf16[192,2048]{1,0:T(8,128)(2,1)S(1)}, u32[]{:S(2)}, u32[]{:S(2)}) collective-permute-start(bf16[192,2048]{1,0:T(8,128)(2,1)} %get-tuple-element.30), channel_id=1, source_target_pairs={{0,1},{1,2},{2,3},{3,0},{4,5},{5,6},{6,7},{7,4},{8,9},{9,10},{10,1... | collective-permute-start | bytes 2359304 | tf_op jit(solution)/shard_map/ppermute | solution.py:316
  141.4 33.1 %collective-permute-start.8 = (bf16[192,2048]{1,0:T(8,128)(2,1)}, bf16[192,2048]{1,0:T(8,128)(2,1)S(1)}, u32[]{:S(2)}, u32[]{:S(2)}) collective-permute-start(bf16[192,2048]{1,0:T(8,128)(2,1)} %get-tuple-element.32), channel_id=1, source_target_pairs={{0,3},{1,0},{2,1},{3,2},{4,7},{5,4},{6,5},{7,6},{8,11},{9,8},{10,9... | collective-permute-start | bytes 2359304 | tf_op jit(solution)/shard_map/ppermute | solution.py:316
  148.3 69.6 %all-to-all-start.1 = ((bf16[512,8,128]{2,1,0:T(8,128)(2,1)}), bf16[512,8,128]{2,1,0:T(8,128)(2,1)S(1)}, u32[]{:S(2)}, u32[]{:S(2)}) async-start(bf16[512,8,128]{2,1,0:T(8,128)(2,1)} %bitcast.12), calls=%async_computation.1 | async-start | bytes 2097152 | tf_op jit(solution)/shard_map/all_to_all | solution.py:320
  164.1 10.3 %copy-start.7 = (bf16[192,2048]{1,0:T(8,128)(2,1)S(1)}, bf16[192,2048]{1,0:T(8,128)(2,1)}, u32[]{:S(2)}) copy-start(bf16[192,2048]{1,0:T(8,128)(2,1)} %get-tuple-element.31) | copy-start | bytes 2359300
  164.2 23.1 %collective-permute-start.10 = (bf16[192,2048]{1,0:T(8,128)(2,1)}, bf16[192,2048]{1,0:T(8,128)(2,1)S(1)}, u32[]{:S(2)}, u32[]{:S(2)}) collective-permute-start(bf16[192,2048]{1,0:T(8,128)(2,1)} %get-tuple-element.33), channel_id=1, source_target_pairs={{0,1},{1,2},{2,3},{3,0},{4,5},{5,6},{6,7},{7,4},{8,9},{9,10},{10,1... | collective-permute-start | bytes 2359304 | tf_op jit(solution)/shard_map/ppermute | solution.py:316
  167.6 23.7 %collective-permute-start.11 = (bf16[192,2048]{1,0:T(8,128)(2,1)}, bf16[192,2048]{1,0:T(8,128)(2,1)S(1)}, u32[]{:S(2)}, u32[]{:S(2)}) collective-permute-start(bf16[192,2048]{1,0:T(8,128)(2,1)} %get-tuple-element.34), channel_id=1, source_target_pairs={{0,3},{1,0},{2,1},{3,2},{4,7},{5,4},{6,5},{7,6},{8,11},{9,8},{10,9... | collective-permute-start | bytes 2359304 | tf_op jit(solution)/shard_map/ppermute | solution.py:316
  172.2 39.9 %copy-start = (bf16[384,2048]{1,0:T(8,128)(2,1)S(1)}, bf16[384,2048]{1,0:T(8,128)(2,1)}, u32[]{:S(2)}) copy-start(bf16[384,2048]{1,0:T(8,128)(2,1)} %get-tuple-element.28.own) | copy-start | bytes 4718596
  172.2 36.8 %collective-permute-start.7 = (bf16[192,2048]{1,0:T(8,128)(2,1)S(1)}, bf16[192,2048]{1,0:T(8,128)(2,1)S(1)}, u32[]{:S(2)}, u32[]{:S(2)}) collective-permute-start(bf16[192,2048]{1,0:T(8,128)(2,1)S(1)} %add_convert_fusion.1), channel_id=1, source_target_pairs={{0,1},{1,2},{2,3},{3,0},{4,5},{5,6},{6,7},{7,4},{8,9},{9,10},{10,1... | collective-permute-start | bytes 2359304 | tf_op jit(solution)/shard_map/ppermute | solution.py:316
  174.7 37.4 %collective-permute-start.9 = (bf16[192,2048]{1,0:T(8,128)(2,1)S(1)}, bf16[192,2048]{1,0:T(8,128)(2,1)S(1)}, u32[]{:S(2)}, u32[]{:S(2)}) collective-permute-start(bf16[192,2048]{1,0:T(8,128)(2,1)S(1)} %add_convert_fusion), channel_id=1, source_target_pairs={{0,3},{1,0},{2,1},{3,2},{4,7},{5,4},{6,5},{7,6},{8,11},{9,8},{10,9... | collective-permute-start | bytes 2359304 | tf_op jit(solution)/shard_map/ppermute | solution.py:316

commit v6 on v4

--- a/solution.py
+++ b/solution.py
@@ -122,8 +122,9 @@
 
 def expert_kernel(
     recv_ref, u0, u1, u2, u3, d0, d1, d2, d3,
-    d_pre_ref, up, own_out, first_p, first_m, plain_p, plain_m, held_p, held_m,
-    down, in_rows, grad_rows, own_s, fp_s, fm_s, pp_s, pm_s, hp_s, hm_s, sems, out_sems,
+    ret_hbm, own_out, first_p, first_m, plain_p, plain_m, held_p, held_m,
+    up, down, in_rows, grad_rows, ret_ref, own_s, fp_s, fm_s, pp_s, pm_s, hp_s, hm_s,
+    sems, out_sems, ret_sems,
 ):
     part = u0.shape[0]
     half = part // 2
@@ -151,7 +152,6 @@
     sigma = jax.nn.sigmoid(pre)
     hidden = (pre * sigma).astype(BF16)
     d_pre = (back * sigma * (1.0 + pre * (1.0 - sigma))).astype(BF16)
-    d_pre_ref[...] = d_pre
 
     outs = []
 
@@ -161,7 +161,7 @@
 
     width = in_rows.shape[1]
     step = 512
-    for top in (3 * part, 2 * part, part, 0):
+    for top in (0, part, 2 * part, 3 * part):
         for w, (left, rows) in enumerate(((d_pre, in_rows), (hidden, grad_rows))):
             one, two = slice(w * half, w * half + half), slice(w * part, w * part + part)
             for n in range(width // step):
@@ -191,20 +191,16 @@
         else:
             send(0, fp_s, first_p)
             send(1, fm_s, first_m)
-    for copy in outs:
-        copy.wait()
-
-
-def return_kernel(d_pre_ref, up_ref, ret_hbm, ret_ref, sems):
-    rows_back = lax.dot_general(
-        d_pre_ref[...], up_ref[...], CONTRACT_FIRST, preferred_element_type=F32
-    ).astype(BF16)
+    rows_back = lax.dot_general(d_pre, up[...], CONTRACT_FIRST, preferred_element_type=F32)
+    rows_back = rows_back.astype(BF16)
     to_rows = row_permutation(rows_source)
     for blk in range(ret_ref.shape[0] // BLOCK):
         parts = [rows_back[blk * 16 : blk * 16 + 16, g * 128 : g * 128 + 128] for g in range(16)]
         ret_ref[blk * BLOCK : blk * BLOCK + BLOCK, :] = pick(to_rows, jnp.concatenate(parts, axis=0))
-        drain(ret_ref, ret_hbm, sems, blk)
-    finish(ret_ref, ret_hbm, sems)
+        drain(ret_ref, ret_hbm, ret_sems, blk)
+    finish(ret_ref, ret_hbm, ret_sems)
+    for copy in outs:
+        copy.wait()
 
 
 def combine_kernel(recv_ref, chosen_ref, out_ref, rows):
@@ -312,30 +308,21 @@
 
     piece = (hidden_part, width)
     whole = (2 * hidden_part, width)
-    d_pre, up_full, own, first_p, first_m, plain_p, plain_m, held_p, held_m = pl.pallas_call(
+    ret, own, first_p, first_m, plain_p, plain_m, held_p, held_m = pl.pallas_call(
         expert_kernel,
         in_specs=[vmem] + [hbm] * 8,
-        out_specs=(vmem,) * 2 + (hbm,) * 7,
-        out_shape=(on_chip((hidden, row_count)), on_chip((hidden, width)), in_hbm(whole))
-        + (in_hbm(piece),) * 6,
-        scratch_shapes=[pltpu.VMEM((hidden, width), BF16)]
+        out_specs=(hbm,) * 8,
+        out_shape=(in_hbm((send_rows, 128)), in_hbm(whole)) + (in_hbm(piece),) * 6,
+        scratch_shapes=[pltpu.VMEM((hidden, width), BF16)] * 2
         + [pltpu.VMEM((row_count, width), BF16)] * 2
-        + [pltpu.VMEM(whole, BF16)]
+        + [pltpu.VMEM((send_rows, 128), BF16), pltpu.VMEM(whole, BF16)]
         + [pltpu.VMEM(piece, BF16)] * 6
-        + [pltpu.SemaphoreType.DMA((8,)), pltpu.SemaphoreType.DMA((7,))],
+        + [pltpu.SemaphoreType.DMA((n,)) for n in (8, 7, CHUNKS)],
         compiler_params=PARAMS,
         name="expert",
     )(keep(recv), *weights)
 
     got_p, got_m = shift(first_p, 1), shift(first_m, -1)
-    ret = pl.pallas_call(
-        return_kernel,
-        out_specs=hbm,
-        out_shape=in_hbm((send_rows, 128)),
-        scratch_shapes=[pltpu.VMEM((send_rows, 128), BF16), pltpu.SemaphoreType.DMA((CHUNKS,))],
-        compiler_params=PARAMS,
-        name="rows_back",
-    )(keep(d_pre), keep(up_full))
     returned = swap(ret)
     plain_p, plain_m = shift(plain_p, 1), shift(plain_m, -1)
     last_p = shift((held_p.astype(F32) + got_p.astype(F32)).astype(BF16), 1)

time: 221 us -> 221 us (level)
    pallas_call x2 -> x1, Pallas kernels: 11.2 us -> 10.9 us  [local(): pl.pallas_call(expert_kernel, in_specs=[vmem] + [hbm] * 8, out_specs=(hbm...]
  transfers between devices with their start and end apart: 14 -> 14, of which waited for: 10 -> 10; matrix products, arithmetic and copies ran while one was open for 1% -> 1% of each run, Pallas kernels for 2% -> 1%
where the time goes in v6:
time: 221 us; the launch traced here: 220 us
  waiting for transfers between devices  121 us (55%)
  starting transfers between devices  78.7 us (36%)
  Pallas kernels  17.4 us (8%)
    ppermute x12, waiting for transfers between devices, shift(): return lax.ppermute(value, 'dp', pairs)  103 us
    ppermute x12, starting transfers between devices, shift(): return lax.ppermute(value, 'dp', pairs)  43.2 us
    all_to_all x2, starting transfers between devices, swap(): lax.all_to_all(values.reshape(peers, 8, lanes), ('expert', 'dp'), split_a...  35.5 us
    all_to_all x2, waiting for transfers between devices, swap(): lax.all_to_all(values.reshape(peers, 8, lanes), ('expert', 'dp'), split_a...  17.5 us
    pallas_call x1, Pallas kernels, local(): pl.pallas_call(expert_kernel, in_specs=[vmem] + [hbm] * 8, out_specs=(hbm...  10.9 us
  transfers between devices with their start and end apart: 14, of which 10 were waited for; matrix products, arithmetic and copies ran while one was open for 1% of the time, Pallas kernels for 1%

profile of v6, /device:TPU:1, one launch (start us, length us, event | category | flops | bytes accessed | tf_op | source)
XLA Modules:
  0.0 220.3 jit_solution(16885263669223998410)
XLA Ops:
  0.6 3.4 %dispatch.1 = (bf16[4096,256]{1,0:T(8,128)(2,1)}, bf16[1024,128]{1,0:T(8,128)(2,1)S(1)}) custom-call(s32[4,128]{1,0:T(4,128)} %bitcast.22, f32[4,128]{1,0:T(4,128)} %bitcast.23, bf16[128,512]{1,0:T(8,128)(2,1)} %in_hbm_ref.1, bf16[128,512]{1,0:T(8,128)(2,1)} %out_hbm_ref.1), custom_call_target="tpu_custom_call" | custom-call | tf_op jit(solution)/shard_map/dispatch/pallas_call | solution.py:283
  4.0 0.0 copy-start.1
  4.0 24.3 %all-to-all-start = ((bf16[512,8,256]{2,1,0:T(8,128)(2,1)}), bf16[512,8,256]{2,1,0:T(8,128)(2,1)S(1)}, u32[]{:S(2)}, u32[]{:S(2)}) async-start(bf16[512,8,256]{2,1,0:T(8,128)(2,1)} %bitcast.12), calls=%async_computation | async-start | bytes 4194304 | tf_op jit(solution)/shard_map/all_to_all | solution.py:275
  28.3 0.0 copy-done.1
  28.3 4.8 %collective-permute-start.2 = (bf16[192,2048]{1,0:T(8,128)(2,1)S(1)}, bf16[192,2048]{1,0:T(8,128)(2,1)S(1)}, u32[]{:S(2)}, u32[]{:S(2)}) collective-permute-start(bf16[192,2048]{1,0:T(8,128)(2,1)S(1)} %bitcast.15), channel_id=1, source_target_pairs={{0,2},{1,3},{2,0},{3,1},{4,6},{5,7},{6,4},{7,5},{8,10},{9,11},{10,... | collective-permute-start | bytes 2359304 | tf_op jit(solution)/shard_map/ppermute | solution.py:271
  33.1 2.2 collective-permute-start.1
  35.3 4.3 %collective-permute-start = (bf16[192,2048]{1,0:T(8,128)(2,1)S(1)}, bf16[192,2048]{1,0:T(8,128)(2,1)S(1)}, u32[]{:S(2)}, u32[]{:S(2)}) collective-permute-start(bf16[192,2048]{1,0:T(8,128)(2,1)S(1)} %bitcast.17), channel_id=1, source_target_pairs={{0,3},{1,0},{2,1},{3,2},{4,7},{5,4},{6,5},{7,6},{8,11},{9,8},{10,9... | collective-permute-start | bytes 2359304 | tf_op jit(solution)/shard_map/ppermute | solution.py:271
  39.6 1.9 collective-permute-start.5
  41.6 2.5 %collective-permute-start.4 = (bf16[192,2048]{1,0:T(8,128)(2,1)}, bf16[192,2048]{1,0:T(8,128)(2,1)S(1)}, u32[]{:S(2)}, u32[]{:S(2)}) collective-permute-start(bf16[192,2048]{1,0:T(8,128)(2,1)} %bitcast.19), channel_id=1, source_target_pairs={{0,1},{1,2},{2,3},{3,0},{4,5},{5,6},{6,7},{7,4},{8,9},{9,10},{10,1... | collective-permute-start | bytes 2359304 | tf_op jit(solution)/shard_map/ppermute | solution.py:271
  44.1 9.7 %collective-permute-done.2.u3 = bf16[192,2048]{1,0:T(8,128)(2,1)S(1)} collective-permute-done((bf16[192,2048]{1,0:T(8,128)(2,1)S(1)}, bf16[192,2048]{1,0:T(8,128)(2,1)S(1)}, u32[]{:S(2)}, u32[]{:S(2)}) %collective-permute-start.2) | collective-permute-done | bytes 786464 | tf_op jit(solution)/shard_map/ppermute | solution.py:271
  53.8 0.0 copy-start.2
  53.8 7.6 %collective-permute-start.3 = (bf16[192,2048]{1,0:T(8,128)(2,1)}, bf16[192,2048]{1,0:T(8,128)(2,1)}, u32[]{:S(2)}, u32[]{:S(2)}) collective-permute-start(bf16[192,2048]{1,0:T(8,128)(2,1)} %bitcast.20), channel_id=1, source_target_pairs={{0,3},{1,0},{2,1},{3,2},{4,7},{5,4},{6,5},{7,6},{8,11},{9,8},{10,9... | collective-permute-start | bytes 2359304 | tf_op jit(solution)/shard_map/ppermute | solution.py:271
  61.4 21.6 %collective-permute-done.1.u2 = bf16[192,2048]{1,0:T(8,128)(2,1)S(1)} collective-permute-done((bf16[192,2048]{1,0:T(8,128)(2,1)S(1)}, bf16[192,2048]{1,0:T(8,128)(2,1)S(1)}, u32[]{:S(2)}, u32[]{:S(2)}) %collective-permute-start.1) | collective-permute-done | bytes 786464 | tf_op jit(solution)/shard_map/ppermute | solution.py:271
  83.1 0.0 copy-start.3
  83.1 0.0 collective-permute-done.u1
  83.1 0.0 copy-start.4
  83.1 15.2 %collective-permute-done.5.d3 = bf16[192,2048]{1,0:T(8,128)(2,1)S(1)} collective-permute-done((bf16[192,2048]{1,0:T(8,128)(2,1)}, bf16[192,2048]{1,0:T(8,128)(2,1)S(1)}, u32[]{:S(2)}, u32[]{:S(2)}) %collective-permute-start.5) | collective-permute-done | bytes 786464 | tf_op jit(solution)/shard_map/ppermute | solution.py:271
  98.3 0.0 copy-start.5
  98.3 23.6 %collective-permute-done.4.d2 = bf16[192,2048]{1,0:T(8,128)(2,1)S(1)} collective-permute-done((bf16[192,2048]{1,0:T(8,128)(2,1)}, bf16[192,2048]{1,0:T(8,128)(2,1)S(1)}, u32[]{:S(2)}, u32[]{:S(2)}) %collective-permute-start.4) | collective-permute-done | bytes 786464 | tf_op jit(solution)/shard_map/ppermute | solution.py:271
  121.9 0.0 copy-done.2
  121.9 0.0 copy-done.3
  121.9 0.0 copy-done.4
  121.9 0.0 copy-done.5
  121.9 0.0 copy-start.6
  121.9 0.9 copy-done.6
  122.9 0.0 collective-permute-done.3.d1
  122.9 8.7 %all-to-all-done = bf16[512,8,256]{2,1,0:T(8,128)(2,1)S(1)} async-done(((bf16[512,8,256]{2,1,0:T(8,128)(2,1)}), bf16[512,8,256]{2,1,0:T(8,128)(2,1)S(1)}, u32[]{:S(2)}, u32[]{:S(2)}) %all-to-all-start) | async-done | bytes 2097184 | tf_op jit(solution)/shard_map/all_to_all | solution.py:275
  131.6 10.9 %expert.1 = (bf16[4096,128]{1,0:T(8,128)(2,1)}, bf16[384,2048]{1,0:T(8,128)(2,1)}, bf16[192,2048]{1,0:T(8,128)(2,1)}, bf16[192,2048]{1,0:T(8,128)(2,1)}, bf16[19...) custom-call(bf16[4096,256]{1,0:T(8,128)(2,1)S(1)} %bitcast.10, ...), custom_call_target="tpu_custom_call" | custom-call | tf_op jit(solution)/shard_map/expert/pallas_call | solution.py:311
  142.5 0.0 copy-start.8
  142.5 2.1 collective-permute-start.6
  144.6 4.6 %collective-permute-start.8 = (bf16[192,2048]{1,0:T(8,128)(2,1)}, bf16[192,2048]{1,0:T(8,128)(2,1)S(1)}, u32[]{:S(2)}, u32[]{:S(2)}) collective-permute-start(bf16[192,2048]{1,0:T(8,128)(2,1)} %get-tuple-element.22), channel_id=1, source_target_pairs={{0,3},{1,0},{2,1},{3,2},{4,7},{5,4},{6,5},{7,6},{8,11},{9,8},{10,9... | collective-permute-start | bytes 2359304 | tf_op jit(solution)/shard_map/ppermute | solution.py:271
  149.2 11.2 %all-to-all-start.1 = ((bf16[512,8,128]{2,1,0:T(8,128)(2,1)}), bf16[512,8,128]{2,1,0:T(8,128)(2,1)S(1)}, u32[]{:S(2)}, u32[]{:S(2)}) async-start(bf16[512,8,128]{2,1,0:T(8,128)(2,1)} %bitcast.13), calls=%async_computation.1 | async-start | bytes 2097152 | tf_op jit(solution)/shard_map/all_to_all | solution.py:275
  160.4 0.0 copy-start.7
  160.4 3.4 %collective-permute-start.10 = (bf16[192,2048]{1,0:T(8,128)(2,1)}, bf16[192,2048]{1,0:T(8,128)(2,1)S(1)}, u32[]{:S(2)}, u32[]{:S(2)}) collective-permute-start(bf16[192,2048]{1,0:T(8,128)(2,1)} %get-tuple-element.23), channel_id=1, source_target_pairs={{0,1},{1,2},{2,3},{3,0},{4,5},{5,6},{6,7},{7,4},{8,9},{9,10},{10,1... | collective-permute-start | bytes 2359304 | tf_op jit(solution)/shard_map/ppermute | solution.py:271
  163.8 3.2 %collective-permute-start.11 = (bf16[192,2048]{1,0:T(8,128)(2,1)}, bf16[192,2048]{1,0:T(8,128)(2,1)S(1)}, u32[]{:S(2)}, u32[]{:S(2)}) collective-permute-start(bf16[192,2048]{1,0:T(8,128)(2,1)} %get-tuple-element.24), channel_id=1, source_target_pairs={{0,3},{1,0},{2,1},{3,2},{4,7},{5,4},{6,5},{7,6},{8,11},{9,8},{10,9... | collective-permute-start | bytes 2359304 | tf_op jit(solution)/shard_map/ppermute | solution.py:271
  167.0 0.0 collective-permute-done.6
  167.0 0.0 copy-done.8
  167.0 1.4 add_convert_fusion.1
  168.4 0.0 copy-start
  168.5 2.2 %collective-permute-start.7 = (bf16[192,2048]{1,0:T(8,128)(2,1)S(1)}, bf16[192,2048]{1,0:T(8,128)(2,1)S(1)}, u32[]{:S(2)}, u32[]{:S(2)}) collective-permute-start(bf16[192,2048]{1,0:T(8,128)(2,1)S(1)} %add_convert_fusion.1), channel_id=1, source_target_pairs={{0,1},{1,2},{2,3},{3,0},{4,5},{5,6},{6,7},{7,4},{8,9},{9,10},{10,1... | collective-permute-start | bytes 2359304 | tf_op jit(solution)/shard_map/ppermute | solution.py:271
  170.7 0.0 collective-permute-done.8
  170.7 0.0 copy-done.7
  170.7 0.3 add_convert_fusion
  171.0 4.4 %collective-permute-start.9 = (bf16[192,2048]{1,0:T(8,128)(2,1)S(1)}, bf16[192,2048]{1,0:T(8,128)(2,1)S(1)}, u32[]{:S(2)}, u32[]{:S(2)}) collective-permute-start(bf16[192,2048]{1,0:T(8,128)(2,1)S(1)} %add_convert_fusion), channel_id=1, source_target_pairs={{0,3},{1,0},{2,1},{3,2},{4,7},{5,4},{6,5},{7,6},{8,11},{9,8},{10,9... | collective-permute-start | bytes 2359304 | tf_op jit(solution)/shard_map/ppermute | solution.py:271
  175.4 8.1 %collective-permute-done.10.plain_p = bf16[192,2048]{1,0:T(8,128)(2,1)S(1)} collective-permute-done((bf16[192,2048]{1,0:T(8,128)(2,1)}, bf16[192,2048]{1,0:T(8,128)(2,1)S(1)}, u32[]{:S(2)}, u32[]{:S(2)}) %collective-permute-start.10) | collective-permute-done | bytes 786464 | tf_op jit(solution)/shard_map/ppermute | solution.py:271
  183.5 3.3 %collective-permute-done.11.plain_m = bf16[192,2048]{1,0:T(8,128)(2,1)S(1)} collective-permute-done((bf16[192,2048]{1,0:T(8,128)(2,1)}, bf16[192,2048]{1,0:T(8,128)(2,1)S(1)}, u32[]{:S(2)}, u32[]{:S(2)}) %collective-permute-start.11) | collective-permute-done | bytes 786464 | tf_op jit(solution)/shard_map/ppermute | solution.py:271
  186.9 18.5 %collective-permute-done.7.last_p = bf16[192,2048]{1,0:T(8,128)(2,1)S(1)} collective-permute-done((bf16[192,2048]{1,0:T(8,128)(2,1)S(1)}, bf16[192,2048]{1,0:T(8,128)(2,1)S(1)}, u32[]{:S(2)}, u32[]{:S(2)}) %collective-permute-start.7) | collective-permute-done | bytes 786464 | tf_op jit(solution)/shard_map/ppermute | solution.py:271
  205.4 3.0 %collective-permute-done.9.last_m = bf16[192,2048]{1,0:T(8,128)(2,1)S(1)} collective-permute-done((bf16[192,2048]{1,0:T(8,128)(2,1)S(1)}, bf16[192,2048]{1,0:T(8,128)(2,1)S(1)}, u32[]{:S(2)}, u32[]{:S(2)}) %collective-permute-start.9) | collective-permute-done | bytes 786464 | tf_op jit(solution)/shard_map/ppermute | solution.py:271
  208.4 0.0 copy-done
  208.4 1.6 grads.1
  210.0 8.8 %all-to-all-done.1 = bf16[512,8,128]{2,1,0:T(8,128)(2,1)S(1)} async-done(((bf16[512,8,128]{2,1,0:T(8,128)(2,1)}), bf16[512,8,128]{2,1,0:T(8,128)(2,1)S(1)}, u32[]{:S(2)}, u32[]{:S(2)}) %all-to-all-start.1) | async-done | bytes 1048608 | tf_op jit(solution)/shard_map/all_to_all | solution.py:275
  218.8 1.5 combine.1
Async XLA Ops:
  4.0 24.3 %copy-start.1 = (bf16[1,192,2048]{2,1,0:T(8,128)(2,1)S(1)}, bf16[1,192,2048]{2,1,0:T(8,128)(2,1)}, u32[]{:S(2)}) copy-start(bf16[1,192,2048]{2,1,0:T(8,128)(2,1)} %param.10) | copy-start | bytes 2359300
  4.0 127.6 %all-to-all-start = ((bf16[512,8,256]{2,1,0:T(8,128)(2,1)}), bf16[512,8,256]{2,1,0:T(8,128)(2,1)S(1)}, u32[]{:S(2)}, u32[]{:S(2)}) async-start(bf16[512,8,256]{2,1,0:T(8,128)(2,1)} %bitcast.12), calls=%async_computation | async-start | bytes 4194304 | tf_op jit(solution)/shard_map/all_to_all | solution.py:275
  28.3 25.5 %collective-permute-start.2 = (bf16[192,2048]{1,0:T(8,128)(2,1)S(1)}, bf16[192,2048]{1,0:T(8,128)(2,1)S(1)}, u32[]{:S(2)}, u32[]{:S(2)}) collective-permute-start(bf16[192,2048]{1,0:T(8,128)(2,1)S(1)} %bitcast.15), channel_id=1, source_target_pairs={{0,2},{1,3},{2,0},{3,1},{4,6},{5,7},{6,4},{7,5},{8,10},{9,11},{10,... | collective-permute-start | bytes 2359304 | tf_op jit(solution)/shard_map/ppermute | solution.py:271
  33.1 49.9 %collective-permute-start.1 = (bf16[192,2048]{1,0:T(8,128)(2,1)S(1)}, bf16[192,2048]{1,0:T(8,128)(2,1)S(1)}, u32[]{:S(2)}, u32[]{:S(2)}) collective-permute-start(bf16[192,2048]{1,0:T(8,128)(2,1)S(1)} %bitcast.16), channel_id=1, source_target_pairs={{0,1},{1,2},{2,3},{3,0},{4,5},{5,6},{6,7},{7,4},{8,9},{9,10},{10,1... | collective-permute-start | bytes 2359304 | tf_op jit(solution)/shard_map/ppermute | solution.py:271
  35.3 47.7 %collective-permute-start = (bf16[192,2048]{1,0:T(8,128)(2,1)S(1)}, bf16[192,2048]{1,0:T(8,128)(2,1)S(1)}, u32[]{:S(2)}, u32[]{:S(2)}) collective-permute-start(bf16[192,2048]{1,0:T(8,128)(2,1)S(1)} %bitcast.17), channel_id=1, source_target_pairs={{0,3},{1,0},{2,1},{3,2},{4,7},{5,4},{6,5},{7,6},{8,11},{9,8},{10,9... | collective-permute-start | bytes 2359304 | tf_op jit(solution)/shard_map/ppermute | solution.py:271
  39.6 58.6 %collective-permute-start.5 = (bf16[192,2048]{1,0:T(8,128)(2,1)}, bf16[192,2048]{1,0:T(8,128)(2,1)S(1)}, u32[]{:S(2)}, u32[]{:S(2)}) collective-permute-start(bf16[192,2048]{1,0:T(8,128)(2,1)} %bitcast.18), channel_id=1, source_target_pairs={{0,2},{1,3},{2,0},{3,1},{4,6},{5,7},{6,4},{7,5},{8,10},{9,11},{10,... | collective-permute-start | bytes 2359304 | tf_op jit(solution)/shard_map/ppermute | solution.py:271
  41.6 80.3 %collective-permute-start.4 = (bf16[192,2048]{1,0:T(8,128)(2,1)}, bf16[192,2048]{1,0:T(8,128)(2,1)S(1)}, u32[]{:S(2)}, u32[]{:S(2)}) collective-permute-start(bf16[192,2048]{1,0:T(8,128)(2,1)} %bitcast.19), channel_id=1, source_target_pairs={{0,1},{1,2},{2,3},{3,0},{4,5},{5,6},{6,7},{7,4},{8,9},{9,10},{10,1... | collective-permute-start | bytes 2359304 | tf_op jit(solution)/shard_map/ppermute | solution.py:271
  53.8 68.1 %copy-start.2 = (bf16[192,2048]{1,0:T(8,128)(2,1)}, bf16[192,2048]{1,0:T(8,128)(2,1)S(1)}, u32[]{:S(2)}) copy-start(bf16[192,2048]{1,0:T(8,128)(2,1)S(1)} %collective-permute-done.2.u3) | copy-start | bytes 2359300
  53.8 69.1 %collective-permute-start.3 = (bf16[192,2048]{1,0:T(8,128)(2,1)}, bf16[192,2048]{1,0:T(8,128)(2,1)}, u32[]{:S(2)}, u32[]{:S(2)}) collective-permute-start(bf16[192,2048]{1,0:T(8,128)(2,1)} %bitcast.20), channel_id=1, source_target_pairs={{0,3},{1,0},{2,1},{3,2},{4,7},{5,4},{6,5},{7,6},{8,11},{9,8},{10,9... | collective-permute-start | bytes 2359304 | tf_op jit(solution)/shard_map/ppermute | solution.py:271
  83.1 38.8 %copy-start.3 = (bf16[192,2048]{1,0:T(8,128)(2,1)}, bf16[192,2048]{1,0:T(8,128)(2,1)S(1)}, u32[]{:S(2)}) copy-start(bf16[192,2048]{1,0:T(8,128)(2,1)S(1)} %collective-permute-done.1.u2) | copy-start | bytes 2359300
  83.1 38.8 %copy-start.4 = (bf16[192,2048]{1,0:T(8,128)(2,1)}, bf16[192,2048]{1,0:T(8,128)(2,1)S(1)}, u32[]{:S(2)}) copy-start(bf16[192,2048]{1,0:T(8,128)(2,1)S(1)} %collective-permute-done.u1) | copy-start | bytes 2359300
  98.3 23.6 %copy-start.5 = (bf16[192,2048]{1,0:T(8,128)(2,1)}, bf16[192,2048]{1,0:T(8,128)(2,1)S(1)}, u32[]{:S(2)}) copy-start(bf16[192,2048]{1,0:T(8,128)(2,1)S(1)} %collective-permute-done.5.d3) | copy-start | bytes 2359300
  121.9 0.9 copy-start.6
  142.5 24.5 %copy-start.8 = (bf16[192,2048]{1,0:T(8,128)(2,1)S(1)}, bf16[192,2048]{1,0:T(8,128)(2,1)}, u32[]{:S(2)}) copy-start(bf16[192,2048]{1,0:T(8,128)(2,1)} %get-tuple-element.19) | copy-start | bytes 2359300
  142.5 24.5 %collective-permute-start.6 = (bf16[192,2048]{1,0:T(8,128)(2,1)}, bf16[192,2048]{1,0:T(8,128)(2,1)}, u32[]{:S(2)}, u32[]{:S(2)}) collective-permute-start(bf16[192,2048]{1,0:T(8,128)(2,1)} %get-tuple-element.20), channel_id=1, source_target_pairs={{0,1},{1,2},{2,3},{3,0},{4,5},{5,6},{6,7},{7,4},{8,9},{9,10},{10,1... | collective-permute-start | bytes 2359304 | tf_op jit(solution)/shard_map/ppermute | solution.py:271
  144.6 26.1 %collective-permute-start.8 = (bf16[192,2048]{1,0:T(8,128)(2,1)}, bf16[192,2048]{1,0:T(8,128)(2,1)S(1)}, u32[]{:S(2)}, u32[]{:S(2)}) collective-permute-start(bf16[192,2048]{1,0:T(8,128)(2,1)} %get-tuple-element.22), channel_id=1, source_target_pairs={{0,3},{1,0},{2,1},{3,2},{4,7},{5,4},{6,5},{7,6},{8,11},{9,8},{10,9... | collective-permute-start | bytes 2359304 | tf_op jit(solution)/shard_map/ppermute | solution.py:271
  149.2 69.6 %all-to-all-start.1 = ((bf16[512,8,128]{2,1,0:T(8,128)(2,1)}), bf16[512,8,128]{2,1,0:T(8,128)(2,1)S(1)}, u32[]{:S(2)}, u32[]{:S(2)}) async-start(bf16[512,8,128]{2,1,0:T(8,128)(2,1)} %bitcast.13), calls=%async_computation.1 | async-start | bytes 2097152 | tf_op jit(solution)/shard_map/all_to_all | solution.py:275
  160.4 10.3 %copy-start.7 = (bf16[192,2048]{1,0:T(8,128)(2,1)S(1)}, bf16[192,2048]{1,0:T(8,128)(2,1)}, u32[]{:S(2)}) copy-start(bf16[192,2048]{1,0:T(8,128)(2,1)} %get-tuple-element.21) | copy-start | bytes 2359300
  160.4 23.2 %collective-permute-start.10 = (bf16[192,2048]{1,0:T(8,128)(2,1)}, bf16[192,2048]{1,0:T(8,128)(2,1)S(1)}, u32[]{:S(2)}, u32[]{:S(2)}) collective-permute-start(bf16[192,2048]{1,0:T(8,128)(2,1)} %get-tuple-element.23), channel_id=1, source_target_pairs={{0,1},{1,2},{2,3},{3,0},{4,5},{5,6},{6,7},{7,4},{8,9},{9,10},{10,1... | collective-permute-start | bytes 2359304 | tf_op jit(solution)/shard_map/ppermute | solution.py:271
  163.8 23.0 %collective-permute-start.11 = (bf16[192,2048]{1,0:T(8,128)(2,1)}, bf16[192,2048]{1,0:T(8,128)(2,1)S(1)}, u32[]{:S(2)}, u32[]{:S(2)}) collective-permute-start(bf16[192,2048]{1,0:T(8,128)(2,1)} %get-tuple-element.24), channel_id=1, source_target_pairs={{0,3},{1,0},{2,1},{3,2},{4,7},{5,4},{6,5},{7,6},{8,11},{9,8},{10,9... | collective-permute-start | bytes 2359304 | tf_op jit(solution)/shard_map/ppermute | solution.py:271
  168.4 39.9 %copy-start = (bf16[384,2048]{1,0:T(8,128)(2,1)S(1)}, bf16[384,2048]{1,0:T(8,128)(2,1)}, u32[]{:S(2)}) copy-start(bf16[384,2048]{1,0:T(8,128)(2,1)} %get-tuple-element.18.own) | copy-start | bytes 4718596
  168.5 37.0 %collective-permute-start.7 = (bf16[192,2048]{1,0:T(8,128)(2,1)S(1)}, bf16[192,2048]{1,0:T(8,128)(2,1)S(1)}, u32[]{:S(2)}, u32[]{:S(2)}) collective-permute-start(bf16[192,2048]{1,0:T(8,128)(2,1)S(1)} %add_convert_fusion.1), channel_id=1, source_target_pairs={{0,1},{1,2},{2,3},{3,0},{4,5},{5,6},{6,7},{7,4},{8,9},{9,10},{10,1... | collective-permute-start | bytes 2359304 | tf_op jit(solution)/shard_map/ppermute | solution.py:271
  171.0 37.4 %collective-permute-start.9 = (bf16[192,2048]{1,0:T(8,128)(2,1)S(1)}, bf16[192,2048]{1,0:T(8,128)(2,1)S(1)}, u32[]{:S(2)}, u32[]{:S(2)}) collective-permute-start(bf16[192,2048]{1,0:T(8,128)(2,1)S(1)} %add_convert_fusion), channel_id=1, source_target_pairs={{0,3},{1,0},{2,1},{3,2},{4,7},{5,4},{6,5},{7,6},{8,11},{9,8},{10,9... | collective-permute-start | bytes 2359304 | tf_op jit(solution)/shard_map/ppermute | solution.py:271

commit v7 on v6

--- a/solution.py
+++ b/solution.py
@@ -127,7 +127,7 @@
     sems, out_sems, ret_sems,
 ):
     part = u0.shape[0]
-    half = part // 2
+    cut = first_p.shape[0] // 2
     copies = []
     for i, (ref, full) in enumerate(
         [(r, up) for r in (u0, u1, u2, u3)] + [(r, down) for r in (d0, d1, d2, d3)]
@@ -163,7 +163,9 @@
     step = 512
     for top in (0, part, 2 * part, 3 * part):
         for w, (left, rows) in enumerate(((d_pre, in_rows), (hidden, grad_rows))):
-            one, two = slice(w * half, w * half + half), slice(w * part, w * part + part)
+            low = slice(w * cut, w * cut + cut)
+            high = slice(w * (part - cut), w * (part - cut) + part - cut)
+            two = slice(w * part, w * part + part)
             for n in range(width // step):
                 lanes = slice(n * step, n * step + step)
                 total = jnp.dot(
@@ -172,14 +174,14 @@
                 if top == 0:
                     own_s[two, lanes] = total
                 elif top == part:
-                    hp_s[one, lanes] = total[:half]
-                    pp_s[one, lanes] = total[half:]
+                    hp_s[low, lanes] = total[:cut]
+                    pp_s[high, lanes] = total[cut:]
                 elif top == 2 * part:
-                    pm_s[one, lanes] = total[:half]
-                    hm_s[one, lanes] = total[half:]
+                    pm_s[low, lanes] = total[:cut]
+                    hm_s[high, lanes] = total[cut:]
                 else:
-                    fp_s[one, lanes] = total[:half]
-                    fm_s[one, lanes] = total[half:]
+                    fp_s[low, lanes] = total[:cut]
+                    fm_s[high, lanes] = total[cut:]
         if top == 0:
             send(6, own_s, own_out)
         elif top == part:
@@ -216,16 +218,21 @@
 
 
 def grads_kernel(own, last_p, last_m, plain_p, plain_m, up_out, down_out):
-    half = last_p.shape[0] // 2
+    part = up_out.shape[0]
+    cut = last_p.shape[0] // 2
     for w, out in enumerate((up_out, down_out)):
-        one = slice(w * half, w * half + half)
-        low = slice(2 * w * half, 2 * w * half + half)
-        high = slice(2 * w * half + half, 2 * w * half + 2 * half)
-        out[:half, :] = (
-            own[low, :].astype(F32) + last_p[one, :].astype(F32) + plain_m[one, :].astype(F32)
+        top = w * part
+        low = slice(w * cut, w * cut + cut)
+        high = slice(w * (part - cut), w * (part - cut) + part - cut)
+        out[:cut, :] = (
+            own[top : top + cut, :].astype(F32)
+            + last_p[low, :].astype(F32)
+            + plain_m[low, :].astype(F32)
         ).astype(BF16)
-        out[half:, :] = (
-            own[high, :].astype(F32) + plain_p[one, :].astype(F32) + last_m[one, :].astype(F32)
+        out[cut:, :] = (
+            own[top + cut : top + part, :].astype(F32)
+            + plain_p[high, :].astype(F32)
+            + last_m[high, :].astype(F32)
         ).astype(BF16)
 
 
@@ -264,7 +271,7 @@
     peers = expert_count * dp_count
     hidden_part = up_weight.shape[1]
     hidden = hidden_part * dp_count
-    half = hidden_part // 2
+    cut = hidden_part * 3 // 4
 
     def shift(value, by):
         pairs = [(i, (i + by) % dp_count) for i in range(dp_count)]
@@ -307,16 +314,18 @@
     weights = [leave(value) for value in ups + downs]
 
     piece = (hidden_part, width)
+    lows, highs = (2 * cut, width), (2 * (hidden_part - cut), width)
+    pieces = (lows, highs, highs, lows, lows, highs)
     whole = (2 * hidden_part, width)
     ret, own, first_p, first_m, plain_p, plain_m, held_p, held_m = pl.pallas_call(
         expert_kernel,
         in_specs=[vmem] + [hbm] * 8,
         out_specs=(hbm,) * 8,
-        out_shape=(in_hbm((send_rows, 128)), in_hbm(whole)) + (in_hbm(piece),) * 6,
+        out_shape=(in_hbm((send_rows, 128)), in_hbm(whole)) + tuple(in_hbm(dims) for dims in pieces),
         scratch_shapes=[pltpu.VMEM((hidden, width), BF16)] * 2
         + [pltpu.VMEM((row_count, width), BF16)] * 2
         + [pltpu.VMEM((send_rows, 128), BF16), pltpu.VMEM(whole, BF16)]
-        + [pltpu.VMEM(piece, BF16)] * 6
+        + [pltpu.VMEM(dims, BF16) for dims in pieces]
         + [pltpu.SemaphoreType.DMA((n,)) for n in (8, 7, CHUNKS)],
         compiler_params=PARAMS,
         name="expert",

time: 221 us -> 228 us (1.032)
  waiting for transfers between devices: 121 us -> 128 us
    ppermute x12, waiting for transfers between devices: 103 us -> 120 us  [shift(): return lax.ppermute(value, 'dp', pairs)]
    all_to_all x2, waiting for transfers between devices: 17.5 us -> 8.74 us  [swap(): lax.all_to_all(values.reshape(peers, 8, lanes), ('expert', 'dp'), split_a...]
    ppermute x12, starting transfers between devices: 43.2 us -> 40.8 us  [shift(): return lax.ppermute(value, 'dp', pairs)]
  transfers between devices with their start and end apart: 14 -> 14, of which waited for: 10 -> 7; matrix products, arithmetic and copies ran while one was open for 1% -> 1% of each run, Pallas kernels for 1% -> 1%
where the time goes in v7:
time: 228 us; the launch traced here: 227 us
  waiting for transfers between devices  128 us (56%)
  starting transfers between devices  77.8 us (34%)
  Pallas kernels  17.4 us (8%)
    ppermute x12, waiting for transfers between devices, shift(): return lax.ppermute(value, 'dp', pairs)  120 us
    ppermute x12, starting transfers between devices, shift(): return lax.ppermute(value, 'dp', pairs)  40.8 us
    all_to_all x2, starting transfers between devices, swap(): lax.all_to_all(values.reshape(peers, 8, lanes), ('expert', 'dp'), split_a...  37 us
    pallas_call x1, Pallas kernels, local(): pl.pallas_call(expert_kernel, in_specs=[vmem] + [hbm] * 8, out_specs=(hbm...  10.9 us
    all_to_all x2, waiting for transfers between devices, swap(): lax.all_to_all(values.reshape(peers, 8, lanes), ('expert', 'dp'), split_a...  8.74 us
  transfers between devices with their start and end apart: 14, of which 7 were waited for; matrix products, arithmetic and copies ran while one was open for 1% of the time, Pallas kernels for 1%

profile of v7, /device:TPU:1, one launch (start us, length us, event | category | flops | bytes accessed | tf_op | source)
XLA Modules:
  0.0 227.3 jit_solution(3967397380741239562)
XLA Ops:
  0.6 3.4 %dispatch.1 = (bf16[4096,256]{1,0:T(8,128)(2,1)}, bf16[1024,128]{1,0:T(8,128)(2,1)S(1)}) custom-call(s32[4,128]{1,0:T(4,128)} %bitcast.22, f32[4,128]{1,0:T(4,128)} %bitcast.23, bf16[128,512]{1,0:T(8,128)(2,1)} %in_hbm_ref.1, bf16[128,512]{1,0:T(8,128)(2,1)} %out_hbm_ref.1), custom_call_target="tpu_custom_call" | custom-call | tf_op jit(solution)/shard_map/dispatch/pallas_call | solution.py:290
  4.0 0.0 copy-start.2
  4.0 24.3 %all-to-all-start = ((bf16[512,8,256]{2,1,0:T(8,128)(2,1)}), bf16[512,8,256]{2,1,0:T(8,128)(2,1)S(1)}, u32[]{:S(2)}, u32[]{:S(2)}) async-start(bf16[512,8,256]{2,1,0:T(8,128)(2,1)} %bitcast.12), calls=%async_computation | async-start | bytes 4194304 | tf_op jit(solution)/shard_map/all_to_all | solution.py:282
  28.3 0.0 copy-done.2
  28.3 4.8 %collective-permute-start.2 = (bf16[192,2048]{1,0:T(8,128)(2,1)S(1)}, bf16[192,2048]{1,0:T(8,128)(2,1)S(1)}, u32[]{:S(2)}, u32[]{:S(2)}) collective-permute-start(bf16[192,2048]{1,0:T(8,128)(2,1)S(1)} %bitcast.15), channel_id=1, source_target_pairs={{0,2},{1,3},{2,0},{3,1},{4,6},{5,7},{6,4},{7,5},{8,10},{9,11},{10,... | collective-permute-start | bytes 2359304 | tf_op jit(solution)/shard_map/ppermute | solution.py:278
  33.1 2.2 collective-permute-start.1
  35.3 4.3 %collective-permute-start = (bf16[192,2048]{1,0:T(8,128)(2,1)S(1)}, bf16[192,2048]{1,0:T(8,128)(2,1)S(1)}, u32[]{:S(2)}, u32[]{:S(2)}) collective-permute-start(bf16[192,2048]{1,0:T(8,128)(2,1)S(1)} %bitcast.17), channel_id=1, source_target_pairs={{0,3},{1,0},{2,1},{3,2},{4,7},{5,4},{6,5},{7,6},{8,11},{9,8},{10,9... | collective-permute-start | bytes 2359304 | tf_op jit(solution)/shard_map/ppermute | solution.py:278
  39.7 1.9 collective-permute-start.5
  41.6 2.5 %collective-permute-start.4 = (bf16[192,2048]{1,0:T(8,128)(2,1)}, bf16[192,2048]{1,0:T(8,128)(2,1)S(1)}, u32[]{:S(2)}, u32[]{:S(2)}) collective-permute-start(bf16[192,2048]{1,0:T(8,128)(2,1)} %bitcast.19), channel_id=1, source_target_pairs={{0,1},{1,2},{2,3},{3,0},{4,5},{5,6},{6,7},{7,4},{8,9},{9,10},{10,1... | collective-permute-start | bytes 2359304 | tf_op jit(solution)/shard_map/ppermute | solution.py:278
  44.1 9.7 %collective-permute-done.2.u3 = bf16[192,2048]{1,0:T(8,128)(2,1)S(1)} collective-permute-done((bf16[192,2048]{1,0:T(8,128)(2,1)S(1)}, bf16[192,2048]{1,0:T(8,128)(2,1)S(1)}, u32[]{:S(2)}, u32[]{:S(2)}) %collective-permute-start.2) | collective-permute-done | bytes 786464 | tf_op jit(solution)/shard_map/ppermute | solution.py:278
  53.8 0.0 copy-start.3
  53.8 7.6 %collective-permute-start.3 = (bf16[192,2048]{1,0:T(8,128)(2,1)}, bf16[192,2048]{1,0:T(8,128)(2,1)}, u32[]{:S(2)}, u32[]{:S(2)}) collective-permute-start(bf16[192,2048]{1,0:T(8,128)(2,1)} %bitcast.20), channel_id=1, source_target_pairs={{0,3},{1,0},{2,1},{3,2},{4,7},{5,4},{6,5},{7,6},{8,11},{9,8},{10,9... | collective-permute-start | bytes 2359304 | tf_op jit(solution)/shard_map/ppermute | solution.py:278
  61.4 21.6 %collective-permute-done.1.u2 = bf16[192,2048]{1,0:T(8,128)(2,1)S(1)} collective-permute-done((bf16[192,2048]{1,0:T(8,128)(2,1)S(1)}, bf16[192,2048]{1,0:T(8,128)(2,1)S(1)}, u32[]{:S(2)}, u32[]{:S(2)}) %collective-permute-start.1) | collective-permute-done | bytes 786464 | tf_op jit(solution)/shard_map/ppermute | solution.py:278
  83.1 0.0 copy-start.4
  83.1 0.0 collective-permute-done.u1
  83.1 0.0 copy-start.5
  83.1 15.2 %collective-permute-done.5.d3 = bf16[192,2048]{1,0:T(8,128)(2,1)S(1)} collective-permute-done((bf16[192,2048]{1,0:T(8,128)(2,1)}, bf16[192,2048]{1,0:T(8,128)(2,1)S(1)}, u32[]{:S(2)}, u32[]{:S(2)}) %collective-permute-start.5) | collective-permute-done | bytes 786464 | tf_op jit(solution)/shard_map/ppermute | solution.py:278
  98.3 0.0 copy-start.6
  98.3 23.6 %collective-permute-done.4.d2 = bf16[192,2048]{1,0:T(8,128)(2,1)S(1)} collective-permute-done((bf16[192,2048]{1,0:T(8,128)(2,1)}, bf16[192,2048]{1,0:T(8,128)(2,1)S(1)}, u32[]{:S(2)}, u32[]{:S(2)}) %collective-permute-start.4) | collective-permute-done | bytes 786464 | tf_op jit(solution)/shard_map/ppermute | solution.py:278
  121.9 0.0 copy-done.3
  121.9 0.0 copy-done.4
  121.9 0.0 copy-done.5
  121.9 0.0 copy-done.6
  121.9 0.0 copy-start.7
  121.9 0.9 copy-done.7
  122.9 0.0 collective-permute-done.3.d1
  122.9 8.7 %all-to-all-done = bf16[512,8,256]{2,1,0:T(8,128)(2,1)S(1)} async-done(((bf16[512,8,256]{2,1,0:T(8,128)(2,1)}), bf16[512,8,256]{2,1,0:T(8,128)(2,1)S(1)}, u32[]{:S(2)}, u32[]{:S(2)}) %all-to-all-start) | async-done | bytes 2097184 | tf_op jit(solution)/shard_map/all_to_all | solution.py:282
  131.6 10.9 %expert.1 = (bf16[4096,128]{1,0:T(8,128)(2,1)}, bf16[384,2048]{1,0:T(8,128)(2,1)}, bf16[288,2048]{1,0:T(8,128)(2,1)}, bf16[96,2048]{1,0:T(8,128)(2,1)}, bf16[96,...) custom-call(bf16[4096,256]{1,0:T(8,128)(2,1)S(1)} %bitcast.10, ...), custom_call_target="tpu_custom_call" | custom-call | tf_op jit(solution)/shard_map/expert/pallas_call | solution.py:320
  142.5 0.0 copy-start.10
  142.5 0.0 copy-start.1
  142.5 2.1 collective-permute-start.6
  144.6 12.7 %all-to-all-start.1 = ((bf16[512,8,128]{2,1,0:T(8,128)(2,1)}), bf16[512,8,128]{2,1,0:T(8,128)(2,1)S(1)}, u32[]{:S(2)}, u32[]{:S(2)}) async-start(bf16[512,8,128]{2,1,0:T(8,128)(2,1)} %bitcast.13), calls=%async_computation.1 | async-start | bytes 2097152 | tf_op jit(solution)/shard_map/all_to_all | solution.py:282
  157.3 0.0 copy-done.10
  157.3 4.5 %collective-permute-start.8 = (bf16[96,2048]{1,0:T(8,128)(2,1)S(1)}, bf16[96,2048]{1,0:T(8,128)(2,1)S(1)}, u32[]{:S(2)}, u32[]{:S(2)}) collective-permute-start(bf16[96,2048]{1,0:T(8,128)(2,1)S(1)} %copy-done.10), channel_id=1, source_target_pairs={{0,3},{1,0},{2,1},{3,2},{4,7},{5,4},{6,5},{7,6},{8,11},{9,8},{10,9... | collective-permute-start | bytes 1179656 | tf_op jit(solution)/shard_map/ppermute | solution.py:278
  161.8 2.5 %collective-permute-start.11 = (bf16[288,2048]{1,0:T(8,128)(2,1)}, bf16[288,2048]{1,0:T(8,128)(2,1)S(1)}, u32[]{:S(2)}, u32[]{:S(2)}) collective-permute-start(bf16[288,2048]{1,0:T(8,128)(2,1)} %get-tuple-element.24), channel_id=1, source_target_pairs={{0,3},{1,0},{2,1},{3,2},{4,7},{5,4},{6,5},{7,6},{8,11},{9,8},{10,9... | collective-permute-start | bytes 3538952 | tf_op jit(solution)/shard_map/ppermute | solution.py:278
  164.3 13.6 %collective-permute-done.6 = bf16[288,2048]{1,0:T(8,128)(2,1)} collective-permute-done((bf16[288,2048]{1,0:T(8,128)(2,1)}, bf16[288,2048]{1,0:T(8,128)(2,1)}, u32[]{:S(2)}, u32[]{:S(2)}) %collective-permute-start.6) | collective-permute-done | bytes 1179680 | tf_op jit(solution)/shard_map/ppermute | solution.py:278
  177.9 0.0 copy-done.1
  177.9 0.0 copy-start.9
  177.9 0.0 copy-start.8
  177.9 0.0 copy-start
  177.9 1.9 add_convert_fusion
  179.8 1.9 collective-permute-start.7
  181.7 0.0 copy-done.9
  181.7 1.9 collective-permute-start.10
  183.6 0.0 collective-permute-done.8
  183.7 0.0 copy-done.8
  183.7 0.1 add_convert_fusion.1
  183.8 4.6 %collective-permute-start.9 = (bf16[96,2048]{1,0:T(8,128)(2,1)S(1)}, bf16[96,2048]{1,0:T(8,128)(2,1)S(1)}, u32[]{:S(2)}, u32[]{:S(2)}) collective-permute-start(bf16[96,2048]{1,0:T(8,128)(2,1)S(1)} %add_convert_fusion.1), channel_id=1, source_target_pairs={{0,3},{1,0},{2,1},{3,2},{4,7},{5,4},{6,5},{7,6},{8,11},{9,8},{10,9... | collective-permute-start | bytes 1179656 | tf_op jit(solution)/shard_map/ppermute | solution.py:278
  188.3 35.8 %collective-permute-done.10.plain_p = bf16[96,2048]{1,0:T(8,128)(2,1)S(1)} collective-permute-done((bf16[96,2048]{1,0:T(8,128)(2,1)S(1)}, bf16[96,2048]{1,0:T(8,128)(2,1)S(1)}, u32[]{:S(2)}, u32[]{:S(2)}) %collective-permute-start.10) | collective-permute-done | bytes 393248 | tf_op jit(solution)/shard_map/ppermute | solution.py:278
  224.1 0.0 collective-permute-done.9.last_m
  224.2 0.0 collective-permute-done.11.plain_m
  224.2 0.0 collective-permute-done.7.last_p
  224.2 0.0 copy-done
  224.2 1.6 grads.1
  225.8 0.0 all-to-all-done.1
  225.8 1.5 combine.1
Async XLA Ops:
  4.0 24.3 %copy-start.2 = (bf16[1,192,2048]{2,1,0:T(8,128)(2,1)S(1)}, bf16[1,192,2048]{2,1,0:T(8,128)(2,1)}, u32[]{:S(2)}) copy-start(bf16[1,192,2048]{2,1,0:T(8,128)(2,1)} %param.10) | copy-start | bytes 2359300
  4.0 127.6 %all-to-all-start = ((bf16[512,8,256]{2,1,0:T(8,128)(2,1)}), bf16[512,8,256]{2,1,0:T(8,128)(2,1)S(1)}, u32[]{:S(2)}, u32[]{:S(2)}) async-start(bf16[512,8,256]{2,1,0:T(8,128)(2,1)} %bitcast.12), calls=%async_computation | async-start | bytes 4194304 | tf_op jit(solution)/shard_map/all_to_all | solution.py:282
  28.3 25.5 %collective-permute-start.2 = (bf16[192,2048]{1,0:T(8,128)(2,1)S(1)}, bf16[192,2048]{1,0:T(8,128)(2,1)S(1)}, u32[]{:S(2)}, u32[]{:S(2)}) collective-permute-start(bf16[192,2048]{1,0:T(8,128)(2,1)S(1)} %bitcast.15), channel_id=1, source_target_pairs={{0,2},{1,3},{2,0},{3,1},{4,6},{5,7},{6,4},{7,5},{8,10},{9,11},{10,... | collective-permute-start | bytes 2359304 | tf_op jit(solution)/shard_map/ppermute | solution.py:278
  33.1 49.9 %collective-permute-start.1 = (bf16[192,2048]{1,0:T(8,128)(2,1)S(1)}, bf16[192,2048]{1,0:T(8,128)(2,1)S(1)}, u32[]{:S(2)}, u32[]{:S(2)}) collective-permute-start(bf16[192,2048]{1,0:T(8,128)(2,1)S(1)} %bitcast.16), channel_id=1, source_target_pairs={{0,1},{1,2},{2,3},{3,0},{4,5},{5,6},{6,7},{7,4},{8,9},{9,10},{10,1... | collective-permute-start | bytes 2359304 | tf_op jit(solution)/shard_map/ppermute | solution.py:278
  35.3 47.7 %collective-permute-start = (bf16[192,2048]{1,0:T(8,128)(2,1)S(1)}, bf16[192,2048]{1,0:T(8,128)(2,1)S(1)}, u32[]{:S(2)}, u32[]{:S(2)}) collective-permute-start(bf16[192,2048]{1,0:T(8,128)(2,1)S(1)} %bitcast.17), channel_id=1, source_target_pairs={{0,3},{1,0},{2,1},{3,2},{4,7},{5,4},{6,5},{7,6},{8,11},{9,8},{10,9... | collective-permute-start | bytes 2359304 | tf_op jit(solution)/shard_map/ppermute | solution.py:278
  39.7 58.6 %collective-permute-start.5 = (bf16[192,2048]{1,0:T(8,128)(2,1)}, bf16[192,2048]{1,0:T(8,128)(2,1)S(1)}, u32[]{:S(2)}, u32[]{:S(2)}) collective-permute-start(bf16[192,2048]{1,0:T(8,128)(2,1)} %bitcast.18), channel_id=1, source_target_pairs={{0,2},{1,3},{2,0},{3,1},{4,6},{5,7},{6,4},{7,5},{8,10},{9,11},{10,... | collective-permute-start | bytes 2359304 | tf_op jit(solution)/shard_map/ppermute | solution.py:278
  41.6 80.3 %collective-permute-start.4 = (bf16[192,2048]{1,0:T(8,128)(2,1)}, bf16[192,2048]{1,0:T(8,128)(2,1)S(1)}, u32[]{:S(2)}, u32[]{:S(2)}) collective-permute-start(bf16[192,2048]{1,0:T(8,128)(2,1)} %bitcast.19), channel_id=1, source_target_pairs={{0,1},{1,2},{2,3},{3,0},{4,5},{5,6},{6,7},{7,4},{8,9},{9,10},{10,1... | collective-permute-start | bytes 2359304 | tf_op jit(solution)/shard_map/ppermute | solution.py:278
  53.8 68.1 %copy-start.3 = (bf16[192,2048]{1,0:T(8,128)(2,1)}, bf16[192,2048]{1,0:T(8,128)(2,1)S(1)}, u32[]{:S(2)}) copy-start(bf16[192,2048]{1,0:T(8,128)(2,1)S(1)} %collective-permute-done.2.u3) | copy-start | bytes 2359300
  53.8 69.1 %collective-permute-start.3 = (bf16[192,2048]{1,0:T(8,128)(2,1)}, bf16[192,2048]{1,0:T(8,128)(2,1)}, u32[]{:S(2)}, u32[]{:S(2)}) collective-permute-start(bf16[192,2048]{1,0:T(8,128)(2,1)} %bitcast.20), channel_id=1, source_target_pairs={{0,3},{1,0},{2,1},{3,2},{4,7},{5,4},{6,5},{7,6},{8,11},{9,8},{10,9... | collective-permute-start | bytes 2359304 | tf_op jit(solution)/shard_map/ppermute | solution.py:278
  83.1 38.8 %copy-start.4 = (bf16[192,2048]{1,0:T(8,128)(2,1)}, bf16[192,2048]{1,0:T(8,128)(2,1)S(1)}, u32[]{:S(2)}) copy-start(bf16[192,2048]{1,0:T(8,128)(2,1)S(1)} %collective-permute-done.1.u2) | copy-start | bytes 2359300
  83.1 38.8 %copy-start.5 = (bf16[192,2048]{1,0:T(8,128)(2,1)}, bf16[192,2048]{1,0:T(8,128)(2,1)S(1)}, u32[]{:S(2)}) copy-start(bf16[192,2048]{1,0:T(8,128)(2,1)S(1)} %collective-permute-done.u1) | copy-start | bytes 2359300
  98.3 23.6 %copy-start.6 = (bf16[192,2048]{1,0:T(8,128)(2,1)}, bf16[192,2048]{1,0:T(8,128)(2,1)S(1)}, u32[]{:S(2)}) copy-start(bf16[192,2048]{1,0:T(8,128)(2,1)S(1)} %collective-permute-done.5.d3) | copy-start | bytes 2359300
  121.9 0.9 copy-start.7
  142.5 14.8 %copy-start.10 = (bf16[96,2048]{1,0:T(8,128)(2,1)S(1)}, bf16[96,2048]{1,0:T(8,128)(2,1)}, u32[]{:S(2)}) copy-start(bf16[96,2048]{1,0:T(8,128)(2,1)} %get-tuple-element.22) | copy-start | bytes 1179652
  142.5 35.4 %copy-start.1 = (bf16[288,2048]{1,0:T(8,128)(2,1)S(1)}, bf16[288,2048]{1,0:T(8,128)(2,1)}, u32[]{:S(2)}) copy-start(bf16[288,2048]{1,0:T(8,128)(2,1)} %get-tuple-element.19) | copy-start | bytes 3538948
  142.5 35.4 %collective-permute-start.6 = (bf16[288,2048]{1,0:T(8,128)(2,1)}, bf16[288,2048]{1,0:T(8,128)(2,1)}, u32[]{:S(2)}, u32[]{:S(2)}) collective-permute-start(bf16[288,2048]{1,0:T(8,128)(2,1)} %get-tuple-element.20), channel_id=1, source_target_pairs={{0,1},{1,2},{2,3},{3,0},{4,5},{5,6},{6,7},{7,4},{8,9},{9,10},{10,1... | collective-permute-start | bytes 3538952 | tf_op jit(solution)/shard_map/ppermute | solution.py:278
  144.6 81.2 %all-to-all-start.1 = ((bf16[512,8,128]{2,1,0:T(8,128)(2,1)}), bf16[512,8,128]{2,1,0:T(8,128)(2,1)S(1)}, u32[]{:S(2)}, u32[]{:S(2)}) async-start(bf16[512,8,128]{2,1,0:T(8,128)(2,1)} %bitcast.13), calls=%async_computation.1 | async-start | bytes 2097152 | tf_op jit(solution)/shard_map/all_to_all | solution.py:282
  157.3 26.3 %collective-permute-start.8 = (bf16[96,2048]{1,0:T(8,128)(2,1)S(1)}, bf16[96,2048]{1,0:T(8,128)(2,1)S(1)}, u32[]{:S(2)}, u32[]{:S(2)}) collective-permute-start(bf16[96,2048]{1,0:T(8,128)(2,1)S(1)} %copy-done.10), channel_id=1, source_target_pairs={{0,3},{1,0},{2,1},{3,2},{4,7},{5,4},{6,5},{7,6},{8,11},{9,8},{10,9... | collective-permute-start | bytes 1179656 | tf_op jit(solution)/shard_map/ppermute | solution.py:278
  161.8 62.3 %collective-permute-start.11 = (bf16[288,2048]{1,0:T(8,128)(2,1)}, bf16[288,2048]{1,0:T(8,128)(2,1)S(1)}, u32[]{:S(2)}, u32[]{:S(2)}) collective-permute-start(bf16[288,2048]{1,0:T(8,128)(2,1)} %get-tuple-element.24), channel_id=1, source_target_pairs={{0,3},{1,0},{2,1},{3,2},{4,7},{5,4},{6,5},{7,6},{8,11},{9,8},{10,9... | collective-permute-start | bytes 3538952 | tf_op jit(solution)/shard_map/ppermute | solution.py:278
  177.9 3.8 %copy-start.9 = (bf16[96,2048]{1,0:T(8,128)(2,1)S(1)}, bf16[96,2048]{1,0:T(8,128)(2,1)}, u32[]{:S(2)}) copy-start(bf16[96,2048]{1,0:T(8,128)(2,1)} %get-tuple-element.23) | copy-start | bytes 1179652
  177.9 5.8 %copy-start.8 = (bf16[96,2048]{1,0:T(8,128)(2,1)S(1)}, bf16[96,2048]{1,0:T(8,128)(2,1)}, u32[]{:S(2)}) copy-start(bf16[96,2048]{1,0:T(8,128)(2,1)} %get-tuple-element.21) | copy-start | bytes 1179652
  177.9 46.3 %copy-start = (bf16[384,2048]{1,0:T(8,128)(2,1)S(1)}, bf16[384,2048]{1,0:T(8,128)(2,1)}, u32[]{:S(2)}) copy-start(bf16[384,2048]{1,0:T(8,128)(2,1)} %get-tuple-element.18.own) | copy-start | bytes 4718596
  179.8 44.4 %collective-permute-start.7 = (bf16[288,2048]{1,0:T(8,128)(2,1)S(1)}, bf16[288,2048]{1,0:T(8,128)(2,1)S(1)}, u32[]{:S(2)}, u32[]{:S(2)}) collective-permute-start(bf16[288,2048]{1,0:T(8,128)(2,1)S(1)} %add_convert_fusion), channel_id=1, source_target_pairs={{0,1},{1,2},{2,3},{3,0},{4,5},{5,6},{6,7},{7,4},{8,9},{9,10},{10,1... | collective-permute-start | bytes 3538952 | tf_op jit(solution)/shard_map/ppermute | solution.py:278
  181.7 42.4 %collective-permute-start.10 = (bf16[96,2048]{1,0:T(8,128)(2,1)S(1)}, bf16[96,2048]{1,0:T(8,128)(2,1)S(1)}, u32[]{:S(2)}, u32[]{:S(2)}) collective-permute-start(bf16[96,2048]{1,0:T(8,128)(2,1)S(1)} %copy-done.9), channel_id=1, source_target_pairs={{0,1},{1,2},{2,3},{3,0},{4,5},{5,6},{6,7},{7,4},{8,9},{9,10},{10,1... | collective-permute-start | bytes 1179656 | tf_op jit(solution)/shard_map/ppermute | solution.py:278
  183.8 40.4 %collective-permute-start.9 = (bf16[96,2048]{1,0:T(8,128)(2,1)S(1)}, bf16[96,2048]{1,0:T(8,128)(2,1)S(1)}, u32[]{:S(2)}, u32[]{:S(2)}) collective-permute-start(bf16[96,2048]{1,0:T(8,128)(2,1)S(1)} %add_convert_fusion.1), channel_id=1, source_target_pairs={{0,3},{1,0},{2,1},{3,2},{4,7},{5,4},{6,5},{7,6},{8,11},{9,8},{10,9... | collective-permute-start | bytes 1179656 | tf_op jit(solution)/shard_map/ppermute | solution.py:278

commit v8 on v7

--- a/solution.py
+++ b/solution.py
@@ -271,7 +271,7 @@
     peers = expert_count * dp_count
     hidden_part = up_weight.shape[1]
     hidden = hidden_part * dp_count
-    cut = hidden_part * 3 // 4
+    cut = hidden_part * 5 // 6
 
     def shift(value, by):
         pairs = [(i, (i + by) % dp_count) for i in range(dp_count)]
@@ -309,8 +309,8 @@
     recv = swap(send)
 
     up_own, down_own = up_weight[0], down_weight[0]
-    ups = [up_own] + [shift(up_own, by) for by in (-1, 1, 2)]
-    downs = [down_own] + [shift(down_own, by) for by in (-1, 1, 2)]
+    ups = [up_own] + [shift(up_own, by) for by in (1, -1, 2)]
+    downs = [down_own] + [shift(down_own, by) for by in (1, -1, 2)]
     weights = [leave(value) for value in ups + downs]
 
     piece = (hidden_part, width)
@@ -331,11 +331,11 @@
         name="expert",
     )(keep(recv), *weights)
 
-    got_p, got_m = shift(first_p, 1), shift(first_m, -1)
+    got_p, got_m = shift(first_p, -1), shift(first_m, 1)
     returned = swap(ret)
-    plain_p, plain_m = shift(plain_p, 1), shift(plain_m, -1)
-    last_p = shift((held_p.astype(F32) + got_p.astype(F32)).astype(BF16), 1)
-    last_m = shift((held_m.astype(F32) + got_m.astype(F32)).astype(BF16), -1)
+    plain_p, plain_m = shift(plain_p, -1), shift(plain_m, 1)
+    last_p = shift((held_p.astype(F32) + got_p.astype(F32)).astype(BF16), -1)
+    last_m = shift((held_m.astype(F32) + got_m.astype(F32)).astype(BF16), 1)
     grad_up, grad_down = pl.pallas_call(
         grads_kernel,
         out_shape=(shape(piece), shape(piece)),

time: 228 us -> 229 us (level)
  transfers between devices with their start and end apart: 14 -> 14, of which waited for: 7 -> 9; matrix products, arithmetic and copies ran while one was open for 1% -> 1% of each run, Pallas kernels for 1% -> 1%
where the time goes in v8:
time: 229 us; the launch traced here: 228 us
  waiting for transfers between devices  129 us (56%)
  starting transfers between devices  77.9 us (34%)
  Pallas kernels  17.4 us (8%)
    ppermute x12, waiting for transfers between devices, shift(): return lax.ppermute(value, 'dp', pairs)  121 us
    ppermute x12, starting transfers between devices, shift(): return lax.ppermute(value, 'dp', pairs)  41.3 us
    all_to_all x2, starting transfers between devices, swap(): lax.all_to_all(values.reshape(peers, 8, lanes), ('expert', 'dp'), split_a...  36.6 us
    pallas_call x1, Pallas kernels, local(): pl.pallas_call(expert_kernel, in_specs=[vmem] + [hbm] * 8, out_specs=(hbm...  10.9 us
    all_to_all x2, waiting for transfers between devices, swap(): lax.all_to_all(values.reshape(peers, 8, lanes), ('expert', 'dp'), split_a...  8.32 us
  transfers between devices with their start and end apart: 14, of which 9 were waited for; matrix products, arithmetic and copies ran while one was open for 1% of the time, Pallas kernels for 1%

profile of v8, /device:TPU:1, one launch (start us, length us, event | category | flops | bytes accessed | tf_op | source)
XLA Modules:
  0.0 228.0 jit_solution(8601756198940965741)
XLA Ops:
  0.6 3.4 %dispatch.1 = (bf16[4096,256]{1,0:T(8,128)(2,1)}, bf16[1024,128]{1,0:T(8,128)(2,1)S(1)}) custom-call(s32[4,128]{1,0:T(4,128)} %bitcast.22, f32[4,128]{1,0:T(4,128)} %bitcast.23, bf16[128,512]{1,0:T(8,128)(2,1)} %in_hbm_ref.1, bf16[128,512]{1,0:T(8,128)(2,1)} %out_hbm_ref.1), custom_call_target="tpu_custom_call" | custom-call | tf_op jit(solution)/shard_map/dispatch/pallas_call | solution.py:290
  4.0 0.0 copy-start.2
  4.0 24.3 %all-to-all-start = ((bf16[512,8,256]{2,1,0:T(8,128)(2,1)}), bf16[512,8,256]{2,1,0:T(8,128)(2,1)S(1)}, u32[]{:S(2)}, u32[]{:S(2)}) async-start(bf16[512,8,256]{2,1,0:T(8,128)(2,1)} %bitcast.12), calls=%async_computation | async-start | bytes 4194304 | tf_op jit(solution)/shard_map/all_to_all | solution.py:282
  28.3 0.0 copy-done.2
  28.3 4.8 %collective-permute-start.2 = (bf16[192,2048]{1,0:T(8,128)(2,1)S(1)}, bf16[192,2048]{1,0:T(8,128)(2,1)S(1)}, u32[]{:S(2)}, u32[]{:S(2)}) collective-permute-start(bf16[192,2048]{1,0:T(8,128)(2,1)S(1)} %bitcast.15), channel_id=1, source_target_pairs={{0,2},{1,3},{2,0},{3,1},{4,6},{5,7},{6,4},{7,5},{8,10},{9,11},{10,... | collective-permute-start | bytes 2359304 | tf_op jit(solution)/shard_map/ppermute | solution.py:278
  33.1 2.8 %collective-permute-start.1 = (bf16[192,2048]{1,0:T(8,128)(2,1)S(1)}, bf16[192,2048]{1,0:T(8,128)(2,1)S(1)}, u32[]{:S(2)}, u32[]{:S(2)}) collective-permute-start(bf16[192,2048]{1,0:T(8,128)(2,1)S(1)} %bitcast.16), channel_id=1, source_target_pairs={{0,3},{1,0},{2,1},{3,2},{4,7},{5,4},{6,5},{7,6},{8,11},{9,8},{10,9... | collective-permute-start | bytes 2359304 | tf_op jit(solution)/shard_map/ppermute | solution.py:278
  36.0 2.5 %collective-permute-start = (bf16[192,2048]{1,0:T(8,128)(2,1)S(1)}, bf16[192,2048]{1,0:T(8,128)(2,1)S(1)}, u32[]{:S(2)}, u32[]{:S(2)}) collective-permute-start(bf16[192,2048]{1,0:T(8,128)(2,1)S(1)} %bitcast.17), channel_id=1, source_target_pairs={{0,1},{1,2},{2,3},{3,0},{4,5},{5,6},{6,7},{7,4},{8,9},{9,10},{10,1... | collective-permute-start | bytes 2359304 | tf_op jit(solution)/shard_map/ppermute | solution.py:278
  38.4 2.5 %collective-permute-start.5 = (bf16[192,2048]{1,0:T(8,128)(2,1)}, bf16[192,2048]{1,0:T(8,128)(2,1)S(1)}, u32[]{:S(2)}, u32[]{:S(2)}) collective-permute-start(bf16[192,2048]{1,0:T(8,128)(2,1)} %bitcast.18), channel_id=1, source_target_pairs={{0,2},{1,3},{2,0},{3,1},{4,6},{5,7},{6,4},{7,5},{8,10},{9,11},{10,... | collective-permute-start | bytes 2359304 | tf_op jit(solution)/shard_map/ppermute | solution.py:278
  41.0 4.0 %collective-permute-start.4 = (bf16[192,2048]{1,0:T(8,128)(2,1)}, bf16[192,2048]{1,0:T(8,128)(2,1)S(1)}, u32[]{:S(2)}, u32[]{:S(2)}) collective-permute-start(bf16[192,2048]{1,0:T(8,128)(2,1)} %bitcast.19), channel_id=1, source_target_pairs={{0,3},{1,0},{2,1},{3,2},{4,7},{5,4},{6,5},{7,6},{8,11},{9,8},{10,9... | collective-permute-start | bytes 2359304 | tf_op jit(solution)/shard_map/ppermute | solution.py:278
  45.0 8.9 %collective-permute-done.2.u3 = bf16[192,2048]{1,0:T(8,128)(2,1)S(1)} collective-permute-done((bf16[192,2048]{1,0:T(8,128)(2,1)S(1)}, bf16[192,2048]{1,0:T(8,128)(2,1)S(1)}, u32[]{:S(2)}, u32[]{:S(2)}) %collective-permute-start.2) | collective-permute-done | bytes 786464 | tf_op jit(solution)/shard_map/ppermute | solution.py:278
  53.9 0.0 copy-start.3
  53.9 5.7 %collective-permute-start.3 = (bf16[192,2048]{1,0:T(8,128)(2,1)}, bf16[192,2048]{1,0:T(8,128)(2,1)}, u32[]{:S(2)}, u32[]{:S(2)}) collective-permute-start(bf16[192,2048]{1,0:T(8,128)(2,1)} %bitcast.20), channel_id=1, source_target_pairs={{0,1},{1,2},{2,3},{3,0},{4,5},{5,6},{6,7},{7,4},{8,9},{9,10},{10,1... | collective-permute-start | bytes 2359304 | tf_op jit(solution)/shard_map/ppermute | solution.py:278
  59.5 19.2 %collective-permute-done.1.u2 = bf16[192,2048]{1,0:T(8,128)(2,1)S(1)} collective-permute-done((bf16[192,2048]{1,0:T(8,128)(2,1)S(1)}, bf16[192,2048]{1,0:T(8,128)(2,1)S(1)}, u32[]{:S(2)}, u32[]{:S(2)}) %collective-permute-start.1) | collective-permute-done | bytes 786464 | tf_op jit(solution)/shard_map/ppermute | solution.py:278
  78.7 0.0 copy-start.4
  78.7 4.9 %collective-permute-done.u1 = bf16[192,2048]{1,0:T(8,128)(2,1)S(1)} collective-permute-done((bf16[192,2048]{1,0:T(8,128)(2,1)S(1)}, bf16[192,2048]{1,0:T(8,128)(2,1)S(1)}, u32[]{:S(2)}, u32[]{:S(2)}) %collective-permute-start) | collective-permute-done | bytes 786464 | tf_op jit(solution)/shard_map/ppermute | solution.py:278
  83.6 0.0 copy-start.5
  83.6 14.8 %collective-permute-done.5.d3 = bf16[192,2048]{1,0:T(8,128)(2,1)S(1)} collective-permute-done((bf16[192,2048]{1,0:T(8,128)(2,1)}, bf16[192,2048]{1,0:T(8,128)(2,1)S(1)}, u32[]{:S(2)}, u32[]{:S(2)}) %collective-permute-start.5) | collective-permute-done | bytes 786464 | tf_op jit(solution)/shard_map/ppermute | solution.py:278
  98.4 0.0 copy-start.6
  98.4 24.0 %collective-permute-done.4.d2 = bf16[192,2048]{1,0:T(8,128)(2,1)S(1)} collective-permute-done((bf16[192,2048]{1,0:T(8,128)(2,1)}, bf16[192,2048]{1,0:T(8,128)(2,1)S(1)}, u32[]{:S(2)}, u32[]{:S(2)}) %collective-permute-start.4) | collective-permute-done | bytes 786464 | tf_op jit(solution)/shard_map/ppermute | solution.py:278
  122.4 0.0 copy-done.3
  122.4 0.0 copy-done.4
  122.4 0.0 copy-done.5
  122.4 0.0 copy-done.6
  122.4 0.0 copy-start.7
  122.4 0.9 copy-done.7
  123.3 0.0 collective-permute-done.3.d1
  123.3 8.3 %all-to-all-done = bf16[512,8,256]{2,1,0:T(8,128)(2,1)S(1)} async-done(((bf16[512,8,256]{2,1,0:T(8,128)(2,1)}), bf16[512,8,256]{2,1,0:T(8,128)(2,1)S(1)}, u32[]{:S(2)}, u32[]{:S(2)}) %all-to-all-start) | async-done | bytes 2097184 | tf_op jit(solution)/shard_map/all_to_all | solution.py:282
  131.6 10.9 %expert.1 = (bf16[4096,128]{1,0:T(8,128)(2,1)}, bf16[384,2048]{1,0:T(8,128)(2,1)}, bf16[320,2048]{1,0:T(8,128)(2,1)}, bf16[64,2048]{1,0:T(8,128)(2,1)}, bf16[64,...) custom-call(bf16[4096,256]{1,0:T(8,128)(2,1)S(1)} %bitcast.10, ...), custom_call_target="tpu_custom_call" | custom-call | tf_op jit(solution)/shard_map/expert/pallas_call | solution.py:320
  142.5 0.0 copy-start.1
  142.5 2.3 %collective-permute-start.6 = (bf16[320,2048]{1,0:T(8,128)(2,1)}, bf16[320,2048]{1,0:T(8,128)(2,1)}, u32[]{:S(2)}, u32[]{:S(2)}) collective-permute-start(bf16[320,2048]{1,0:T(8,128)(2,1)} %get-tuple-element.20), channel_id=1, source_target_pairs={{0,3},{1,0},{2,1},{3,2},{4,7},{5,4},{6,5},{7,6},{8,11},{9,8},{10,9... | collective-permute-start | bytes 3932168 | tf_op jit(solution)/shard_map/ppermute | solution.py:278
  144.8 12.3 %all-to-all-start.1 = ((bf16[512,8,128]{2,1,0:T(8,128)(2,1)}), bf16[512,8,128]{2,1,0:T(8,128)(2,1)S(1)}, u32[]{:S(2)}, u32[]{:S(2)}) async-start(bf16[512,8,128]{2,1,0:T(8,128)(2,1)} %bitcast.13), calls=%async_computation.1 | async-start | bytes 2097152 | tf_op jit(solution)/shard_map/all_to_all | solution.py:282
  157.2 3.3 %collective-permute-start.11 = (bf16[320,2048]{1,0:T(8,128)(2,1)}, bf16[320,2048]{1,0:T(8,128)(2,1)S(1)}, u32[]{:S(2)}, u32[]{:S(2)}) collective-permute-start(bf16[320,2048]{1,0:T(8,128)(2,1)} %get-tuple-element.24), channel_id=1, source_target_pairs={{0,1},{1,2},{2,3},{3,0},{4,5},{5,6},{6,7},{7,4},{8,9},{9,10},{10,1... | collective-permute-start | bytes 3932168 | tf_op jit(solution)/shard_map/ppermute | solution.py:278
  160.5 19.5 %collective-permute-done.6 = bf16[320,2048]{1,0:T(8,128)(2,1)} collective-permute-done((bf16[320,2048]{1,0:T(8,128)(2,1)}, bf16[320,2048]{1,0:T(8,128)(2,1)}, u32[]{:S(2)}, u32[]{:S(2)}) %collective-permute-start.6) | collective-permute-done | bytes 1310752 | tf_op jit(solution)/shard_map/ppermute | solution.py:278
  180.0 0.0 copy-done.1
  180.0 0.0 copy-start.10
  180.0 0.0 copy-start.9
  180.0 0.0 copy-start.8
  180.0 0.0 copy-start
  180.0 1.9 add_convert_fusion
  181.9 1.9 collective-permute-start.7
  183.8 0.0 copy-done.10
  183.9 3.4 %collective-permute-start.8 = (bf16[64,2048]{1,0:T(8,128)(2,1)S(1)}, bf16[64,2048]{1,0:T(8,128)(2,1)S(1)}, u32[]{:S(2)}, u32[]{:S(2)}) collective-permute-start(bf16[64,2048]{1,0:T(8,128)(2,1)S(1)} %copy-done.10), channel_id=1, source_target_pairs={{0,1},{1,2},{2,3},{3,0},{4,5},{5,6},{6,7},{7,4},{8,9},{9,10},{10,1... | collective-permute-start | bytes 786440 | tf_op jit(solution)/shard_map/ppermute | solution.py:278
  187.2 0.0 copy-done.9
  187.2 3.1 %collective-permute-start.10 = (bf16[64,2048]{1,0:T(8,128)(2,1)S(1)}, bf16[64,2048]{1,0:T(8,128)(2,1)S(1)}, u32[]{:S(2)}, u32[]{:S(2)}) collective-permute-start(bf16[64,2048]{1,0:T(8,128)(2,1)S(1)} %copy-done.9), channel_id=1, source_target_pairs={{0,3},{1,0},{2,1},{3,2},{4,7},{5,4},{6,5},{7,6},{8,11},{9,8},{10,9... | collective-permute-start | bytes 786440 | tf_op jit(solution)/shard_map/ppermute | solution.py:278
  190.4 11.7 %collective-permute-done.8 = bf16[64,2048]{1,0:T(8,128)(2,1)S(1)} collective-permute-done((bf16[64,2048]{1,0:T(8,128)(2,1)S(1)}, bf16[64,2048]{1,0:T(8,128)(2,1)S(1)}, u32[]{:S(2)}, u32[]{:S(2)}) %collective-permute-start.8) | collective-permute-done | bytes 262176 | tf_op jit(solution)/shard_map/ppermute | solution.py:278
  202.1 0.0 copy-done.8
  202.1 0.1 add_convert_fusion.1
  202.1 5.0 %collective-permute-start.9 = (bf16[64,2048]{1,0:T(8,128)(2,1)S(1)}, bf16[64,2048]{1,0:T(8,128)(2,1)S(1)}, u32[]{:S(2)}, u32[]{:S(2)}) collective-permute-start(bf16[64,2048]{1,0:T(8,128)(2,1)S(1)} %add_convert_fusion.1), channel_id=1, source_target_pairs={{0,1},{1,2},{2,3},{3,0},{4,5},{5,6},{6,7},{7,4},{8,9},{9,10},{10,1... | collective-permute-start | bytes 786440 | tf_op jit(solution)/shard_map/ppermute | solution.py:278
  207.2 17.7 %collective-permute-done.10.plain_p = bf16[64,2048]{1,0:T(8,128)(2,1)S(1)} collective-permute-done((bf16[64,2048]{1,0:T(8,128)(2,1)S(1)}, bf16[64,2048]{1,0:T(8,128)(2,1)S(1)}, u32[]{:S(2)}, u32[]{:S(2)}) %collective-permute-start.10) | collective-permute-done | bytes 262176 | tf_op jit(solution)/shard_map/ppermute | solution.py:278
  224.8 0.0 collective-permute-done.9.last_m
  224.8 0.0 collective-permute-done.11.plain_m
  224.8 0.0 collective-permute-done.7.last_p
  224.8 0.0 copy-done
  224.8 1.6 grads.1
  226.5 0.0 all-to-all-done.1
  226.5 1.5 combine.1
Async XLA Ops:
  4.0 24.3 %copy-start.2 = (bf16[1,192,2048]{2,1,0:T(8,128)(2,1)S(1)}, bf16[1,192,2048]{2,1,0:T(8,128)(2,1)}, u32[]{:S(2)}) copy-start(bf16[1,192,2048]{2,1,0:T(8,128)(2,1)} %param.10) | copy-start | bytes 2359300
  4.0 127.6 %all-to-all-start = ((bf16[512,8,256]{2,1,0:T(8,128)(2,1)}), bf16[512,8,256]{2,1,0:T(8,128)(2,1)S(1)}, u32[]{:S(2)}, u32[]{:S(2)}) async-start(bf16[512,8,256]{2,1,0:T(8,128)(2,1)} %bitcast.12), calls=%async_computation | async-start | bytes 4194304 | tf_op jit(solution)/shard_map/all_to_all | solution.py:282
  28.3 25.5 %collective-permute-start.2 = (bf16[192,2048]{1,0:T(8,128)(2,1)S(1)}, bf16[192,2048]{1,0:T(8,128)(2,1)S(1)}, u32[]{:S(2)}, u32[]{:S(2)}) collective-permute-start(bf16[192,2048]{1,0:T(8,128)(2,1)S(1)} %bitcast.15), channel_id=1, source_target_pairs={{0,2},{1,3},{2,0},{3,1},{4,6},{5,7},{6,4},{7,5},{8,10},{9,11},{10,... | collective-permute-start | bytes 2359304 | tf_op jit(solution)/shard_map/ppermute | solution.py:278
  33.1 45.6 %collective-permute-start.1 = (bf16[192,2048]{1,0:T(8,128)(2,1)S(1)}, bf16[192,2048]{1,0:T(8,128)(2,1)S(1)}, u32[]{:S(2)}, u32[]{:S(2)}) collective-permute-start(bf16[192,2048]{1,0:T(8,128)(2,1)S(1)} %bitcast.16), channel_id=1, source_target_pairs={{0,3},{1,0},{2,1},{3,2},{4,7},{5,4},{6,5},{7,6},{8,11},{9,8},{10,9... | collective-permute-start | bytes 2359304 | tf_op jit(solution)/shard_map/ppermute | solution.py:278
  36.0 47.6 %collective-permute-start = (bf16[192,2048]{1,0:T(8,128)(2,1)S(1)}, bf16[192,2048]{1,0:T(8,128)(2,1)S(1)}, u32[]{:S(2)}, u32[]{:S(2)}) collective-permute-start(bf16[192,2048]{1,0:T(8,128)(2,1)S(1)} %bitcast.17), channel_id=1, source_target_pairs={{0,1},{1,2},{2,3},{3,0},{4,5},{5,6},{6,7},{7,4},{8,9},{9,10},{10,1... | collective-permute-start | bytes 2359304 | tf_op jit(solution)/shard_map/ppermute | solution.py:278
  38.4 59.9 %collective-permute-start.5 = (bf16[192,2048]{1,0:T(8,128)(2,1)}, bf16[192,2048]{1,0:T(8,128)(2,1)S(1)}, u32[]{:S(2)}, u32[]{:S(2)}) collective-permute-start(bf16[192,2048]{1,0:T(8,128)(2,1)} %bitcast.18), channel_id=1, source_target_pairs={{0,2},{1,3},{2,0},{3,1},{4,6},{5,7},{6,4},{7,5},{8,10},{9,11},{10,... | collective-permute-start | bytes 2359304 | tf_op jit(solution)/shard_map/ppermute | solution.py:278
  41.0 81.4 %collective-permute-start.4 = (bf16[192,2048]{1,0:T(8,128)(2,1)}, bf16[192,2048]{1,0:T(8,128)(2,1)S(1)}, u32[]{:S(2)}, u32[]{:S(2)}) collective-permute-start(bf16[192,2048]{1,0:T(8,128)(2,1)} %bitcast.19), channel_id=1, source_target_pairs={{0,3},{1,0},{2,1},{3,2},{4,7},{5,4},{6,5},{7,6},{8,11},{9,8},{10,9... | collective-permute-start | bytes 2359304 | tf_op jit(solution)/shard_map/ppermute | solution.py:278
  53.9 68.5 %copy-start.3 = (bf16[192,2048]{1,0:T(8,128)(2,1)}, bf16[192,2048]{1,0:T(8,128)(2,1)S(1)}, u32[]{:S(2)}) copy-start(bf16[192,2048]{1,0:T(8,128)(2,1)S(1)} %collective-permute-done.2.u3) | copy-start | bytes 2359300
  53.9 69.4 %collective-permute-start.3 = (bf16[192,2048]{1,0:T(8,128)(2,1)}, bf16[192,2048]{1,0:T(8,128)(2,1)}, u32[]{:S(2)}, u32[]{:S(2)}) collective-permute-start(bf16[192,2048]{1,0:T(8,128)(2,1)} %bitcast.20), channel_id=1, source_target_pairs={{0,1},{1,2},{2,3},{3,0},{4,5},{5,6},{6,7},{7,4},{8,9},{9,10},{10,1... | collective-permute-start | bytes 2359304 | tf_op jit(solution)/shard_map/ppermute | solution.py:278
  78.7 43.7 %copy-start.4 = (bf16[192,2048]{1,0:T(8,128)(2,1)}, bf16[192,2048]{1,0:T(8,128)(2,1)S(1)}, u32[]{:S(2)}) copy-start(bf16[192,2048]{1,0:T(8,128)(2,1)S(1)} %collective-permute-done.1.u2) | copy-start | bytes 2359300
  83.6 38.8 %copy-start.5 = (bf16[192,2048]{1,0:T(8,128)(2,1)}, bf16[192,2048]{1,0:T(8,128)(2,1)S(1)}, u32[]{:S(2)}) copy-start(bf16[192,2048]{1,0:T(8,128)(2,1)S(1)} %collective-permute-done.u1) | copy-start | bytes 2359300
  98.4 24.0 %copy-start.6 = (bf16[192,2048]{1,0:T(8,128)(2,1)}, bf16[192,2048]{1,0:T(8,128)(2,1)S(1)}, u32[]{:S(2)}) copy-start(bf16[192,2048]{1,0:T(8,128)(2,1)S(1)} %collective-permute-done.5.d3) | copy-start | bytes 2359300
  122.4 0.9 copy-start.7
  142.5 37.5 %copy-start.1 = (bf16[320,2048]{1,0:T(8,128)(2,1)S(1)}, bf16[320,2048]{1,0:T(8,128)(2,1)}, u32[]{:S(2)}) copy-start(bf16[320,2048]{1,0:T(8,128)(2,1)} %get-tuple-element.19) | copy-start | bytes 3932164
  142.5 37.5 %collective-permute-start.6 = (bf16[320,2048]{1,0:T(8,128)(2,1)}, bf16[320,2048]{1,0:T(8,128)(2,1)}, u32[]{:S(2)}, u32[]{:S(2)}) collective-permute-start(bf16[320,2048]{1,0:T(8,128)(2,1)} %get-tuple-element.20), channel_id=1, source_target_pairs={{0,3},{1,0},{2,1},{3,2},{4,7},{5,4},{6,5},{7,6},{8,11},{9,8},{10,9... | collective-permute-start | bytes 3932168 | tf_op jit(solution)/shard_map/ppermute | solution.py:278
  144.8 81.6 %all-to-all-start.1 = ((bf16[512,8,128]{2,1,0:T(8,128)(2,1)}), bf16[512,8,128]{2,1,0:T(8,128)(2,1)S(1)}, u32[]{:S(2)}, u32[]{:S(2)}) async-start(bf16[512,8,128]{2,1,0:T(8,128)(2,1)} %bitcast.13), calls=%async_computation.1 | async-start | bytes 2097152 | tf_op jit(solution)/shard_map/all_to_all | solution.py:282
  157.2 67.7 %collective-permute-start.11 = (bf16[320,2048]{1,0:T(8,128)(2,1)}, bf16[320,2048]{1,0:T(8,128)(2,1)S(1)}, u32[]{:S(2)}, u32[]{:S(2)}) collective-permute-start(bf16[320,2048]{1,0:T(8,128)(2,1)} %get-tuple-element.24), channel_id=1, source_target_pairs={{0,1},{1,2},{2,3},{3,0},{4,5},{5,6},{6,7},{7,4},{8,9},{9,10},{10,1... | collective-permute-start | bytes 3932168 | tf_op jit(solution)/shard_map/ppermute | solution.py:278
  180.0 3.9 %copy-start.10 = (bf16[64,2048]{1,0:T(8,128)(2,1)S(1)}, bf16[64,2048]{1,0:T(8,128)(2,1)}, u32[]{:S(2)}) copy-start(bf16[64,2048]{1,0:T(8,128)(2,1)} %get-tuple-element.22) | copy-start | bytes 786436
  180.0 7.3 %copy-start.9 = (bf16[64,2048]{1,0:T(8,128)(2,1)S(1)}, bf16[64,2048]{1,0:T(8,128)(2,1)}, u32[]{:S(2)}) copy-start(bf16[64,2048]{1,0:T(8,128)(2,1)} %get-tuple-element.23) | copy-start | bytes 786436
  180.0 22.1 %copy-start.8 = (bf16[64,2048]{1,0:T(8,128)(2,1)S(1)}, bf16[64,2048]{1,0:T(8,128)(2,1)}, u32[]{:S(2)}) copy-start(bf16[64,2048]{1,0:T(8,128)(2,1)} %get-tuple-element.21) | copy-start | bytes 786436
  180.0 44.8 %copy-start = (bf16[384,2048]{1,0:T(8,128)(2,1)S(1)}, bf16[384,2048]{1,0:T(8,128)(2,1)}, u32[]{:S(2)}) copy-start(bf16[384,2048]{1,0:T(8,128)(2,1)} %get-tuple-element.18.own) | copy-start | bytes 4718596
  181.9 42.9 %collective-permute-start.7 = (bf16[320,2048]{1,0:T(8,128)(2,1)S(1)}, bf16[320,2048]{1,0:T(8,128)(2,1)S(1)}, u32[]{:S(2)}, u32[]{:S(2)}) collective-permute-start(bf16[320,2048]{1,0:T(8,128)(2,1)S(1)} %add_convert_fusion), channel_id=1, source_target_pairs={{0,3},{1,0},{2,1},{3,2},{4,7},{5,4},{6,5},{7,6},{8,11},{9,8},{10,9... | collective-permute-start | bytes 3932168 | tf_op jit(solution)/shard_map/ppermute | solution.py:278
  183.9 18.2 %collective-permute-start.8 = (bf16[64,2048]{1,0:T(8,128)(2,1)S(1)}, bf16[64,2048]{1,0:T(8,128)(2,1)S(1)}, u32[]{:S(2)}, u32[]{:S(2)}) collective-permute-start(bf16[64,2048]{1,0:T(8,128)(2,1)S(1)} %copy-done.10), channel_id=1, source_target_pairs={{0,1},{1,2},{2,3},{3,0},{4,5},{5,6},{6,7},{7,4},{8,9},{9,10},{10,1... | collective-permute-start | bytes 786440 | tf_op jit(solution)/shard_map/ppermute | solution.py:278
  187.2 37.6 %collective-permute-start.10 = (bf16[64,2048]{1,0:T(8,128)(2,1)S(1)}, bf16[64,2048]{1,0:T(8,128)(2,1)S(1)}, u32[]{:S(2)}, u32[]{:S(2)}) collective-permute-start(bf16[64,2048]{1,0:T(8,128)(2,1)S(1)} %copy-done.9), channel_id=1, source_target_pairs={{0,3},{1,0},{2,1},{3,2},{4,7},{5,4},{6,5},{7,6},{8,11},{9,8},{10,9... | collective-permute-start | bytes 786440 | tf_op jit(solution)/shard_map/ppermute | solution.py:278
  202.1 22.7 %collective-permute-start.9 = (bf16[64,2048]{1,0:T(8,128)(2,1)S(1)}, bf16[64,2048]{1,0:T(8,128)(2,1)S(1)}, u32[]{:S(2)}, u32[]{:S(2)}) collective-permute-start(bf16[64,2048]{1,0:T(8,128)(2,1)S(1)} %add_convert_fusion.1), channel_id=1, source_target_pairs={{0,1},{1,2},{2,3},{3,0},{4,5},{5,6},{6,7},{7,4},{8,9},{9,10},{10,1... | collective-permute-start | bytes 786440 | tf_op jit(solution)/shard_map/ppermute | solution.py:278
